TPU v7x, 32 devices: a whole 2x2x4 slice. The times are simulated.
32 devices in a mesh: beams: 2 (over x), trials: 16 (over z, y, core).
Axes of the slice: x: 2, y: 2, z: 4, core: 2. Of those that a mesh axis runs over, the one named last changes fastest.
Arguments:
- spectra: bfloat16 [4096, 8192], P(('beams', 'trials')), parts along dimension 0, may hold values from -12 to 12
- delays: int32 [64, 16], P('trials'), may hold values from 0 to 56
- spans: int32 [16], replicated, may hold values from 1 to 8, as said below
- widths: int32 [8], replicated, may hold values from 1 to 128
Outputs:
- boxcar_out: float32 [128, 8, 1024], P(('beams', 'trials')), parts along dimension 0
There are 2 independent parts, one for each index of `beams`. A program takes and returns all parts, laid end to end along the dimension named above; an argument that names none is the same for every part. Nothing has to cross between parts.
Inputs may be any that keep to these rules, and one draw needn't show every extreme that they name: Ranges come in pairs: spans[2 i] + spans[2 i + 1] = 9 for every i; some range has exactly 8 live blocks.
All inputs are finite; a program needn't handle non-finite values.
Results may differ from a plain program's by a relative error of at most 0.0003.
Values sent between devices are 32-bit elements; how exact they have to be, the bound alone decides.
No kernel may reach another device: no remote copies, remote signals or barrier semaphores. Data moves between devices by JAX's collectives and lax.ppermute only.
A program may use at most 64 MiB of HBM per device.

v0:
```python
import jax
import jax.numpy as jnp
from jax import lax
from jax.sharding import PartitionSpec as P

CH_SUB = 128
SAMPLE_COUNT = 8192
SUBT = 2
SHIFT = 8
SPAN = 8
KMAX = 8
NB = 64
OUT = 1024


def boxcars(trial, widths):
    total_len = trial.shape[1]
    prefix = jnp.cumsum(trial, axis=1)
    padded_series = jnp.concatenate([jnp.zeros_like(prefix), prefix], axis=1)

    def one_width(width):
        start = total_len - width
        lagged = lax.dynamic_slice_in_dim(padded_series, start, total_len, 1)
        return (prefix - lagged) / jnp.sqrt(width.astype(jnp.float32))

    return jax.vmap(one_width, out_axes=1)(widths)


def finish(trial, live, widths):
    trial = jnp.where(jnp.arange(trial.shape[1])[None, :] < live, trial, jnp.float32(0.0))
    return boxcars(trial, widths)


def subband_series(spectra, channel_mean, channels):
    chan = jnp.arange(CH_SUB)
    level = jnp.arange(SUBT)
    delay_in = level[:, None] * SHIFT * chan[None, :] // CH_SUB
    select = (delay_in[:, None, :] == jnp.arange(KMAX)[None, :, None]).reshape(SUBT * KMAX, CH_SUB)
    counts = jnp.sum(select.astype(jnp.float32), axis=1)
    grouped = jnp.dot(select.astype(jnp.bfloat16), spectra, preferred_element_type=jnp.float32)
    grouped = grouped - counts[:, None] * channel_mean[None, :]
    grouped = jnp.pad(grouped.reshape(SUBT, KMAX, SAMPLE_COUNT), ((0, 0), (0, 0), (0, KMAX)))
    time_series = grouped[:, 0, 0:SAMPLE_COUNT]
    for lag in range(1, KMAX):
        time_series = time_series + grouped[:, lag, lag : lag + SAMPLE_COUNT]
    return time_series / jnp.sqrt(jnp.float32(channels))


def on_device(spectra, delays, spans, widths):
    group = lax.axis_size("trials")
    mine = lax.axis_index("trials")
    channels = CH_SUB * group
    ones_row = jnp.ones((1, CH_SUB), jnp.bfloat16)
    local_sums = jnp.dot(ones_row, spectra, preferred_element_type=jnp.float32)[0]
    channel_mean = lax.psum(local_sums, "trials") / channels
    time_series = subband_series(spectra, channel_mean, channels)
    offsets = jnp.arange(SPAN)
    live = lax.dynamic_index_in_dim(spans, mine, 0, keepdims=False) * 128
    tr_dev = delays.shape[0]
    own_delays = lax.all_to_all(delays, "trials", split_axis=1, concat_axis=0, tiled=True)[:, 0]
    series_blocks = time_series.reshape(SUBT, NB, 128)
    trial_sub = jnp.arange(tr_dev * group) % SUBT
    window = series_blocks[trial_sub[:, None], own_delays[:, None] + offsets[None, :]]
    window = window.reshape(group, tr_dev, OUT)
    return finish(
        jnp.sum(lax.all_to_all(window, "trials", split_axis=0, concat_axis=0, tiled=True), axis=0),
        live,
        widths,
    )


def solution(mesh):
    in_specs = (P(("beams", "trials"), None), P("trials", None), P(), P())
    out_specs = P(("beams", "trials"), None, None)
    return jax.shard_map(
        on_device, mesh=mesh, in_specs=in_specs, out_specs=out_specs, check_vma=False
    )
```

profile of v0, /device:TPU:0, one launch (start us, length us, event | category | flops | bytes accessed | tf_op | source)
XLA Modules:
  0.0 105.8 jit_solution(5896541626378385895)
XLA Ops:
  0.0 1.5 %copy.11 = s32[4,16,1]{0,2,1:T(1,128)} copy(s32[4,16,1]{1,0,2:T(4,128)} %bitcast.41) | data formatting | bytes 512 | tf_op jit(solution)/shard_map/all_to_all | solution.py:60
  1.5 7.4 %all-to-all-start = ((s32[4,16,1]{0,2,1:T(1,128)}), s32[4,16,1]{0,2,1:T(1,128)S(1)}, u32[]{:S(2)}, u32[]{:S(2)}) async-start(s32[4,16,1]{0,2,1:T(1,128)} %copy.11), calls=%async_computation | async-start | bytes 16384 | tf_op jit(solution)/shard_map/all_to_all | solution.py:60
  8.9 0.4 fusion.17
  9.3 61.9 %psum.7 = f32[8192]{0:T(1024)S(1)} all-reduce(f32[8192]{0:T(1024)S(1)} %bitcast.38), channel_id=1, replica_groups=mesh['beams'=2,'trials'=16] {'trials'}, use_global_device_ids=true, to_apply=%region_1.2 | all-reduce | flops 8192 | bytes 65536 | tf_op jit(solution)/shard_map/psum | solution.py:55
  71.2 0.1 and_select_fusion.1
  71.3 0.1 convert_reduce_fusion
  71.4 0.1 mul.60
  71.5 0.1 eq.32
  71.6 0.4 fusion
  72.0 1.0 fusion.8
  73.1 0.1 add.123
  73.2 0.1 fusion.11
  73.3 0.1 reshape.197
  73.4 3.7 %gather_fusion = f32[512,128]{1,0:T(8,128)S(1)} fusion(f32[2,64,128]{2,1,0:T(8,128)S(1)} %bitcast.35, s32[512]{0:T(512)S(1)} %reshape.197), kind=kCustom, calls=%fused_computation | custom fusion | bytes 528384 | tf_op jit(solution)/shard_map/gather | solution.py:63
  77.0 0.8 reshape.171
  77.8 3.5 %all-to-all-start.1 = ((f32[16,4,1024]{2,1,0:T(4,128)}), f32[16,4,1024]{2,1,0:T(4,128)S(1)}, u32[]{:S(2)}, u32[]{:S(2)}) async-start(f32[16,4,1024]{2,1,0:T(4,128)} %reshape.171), calls=%async_computation.1 | async-start | bytes 524288 | tf_op jit(solution)/shard_map/all_to_all | solution.py:66
  81.4 0.6 dynamic_slice.4
  82.7 8.7 %all-to-all-done.1 = f32[16,4,1024]{2,1,0:T(4,128)S(1)} async-done(((f32[16,4,1024]{2,1,0:T(4,128)}), f32[16,4,1024]{2,1,0:T(4,128)S(1)}, u32[]{:S(2)}, u32[]{:S(2)}) %all-to-all-start.1) | async-done | bytes 262176 | tf_op jit(solution)/shard_map/all_to_all | solution.py:66
  91.4 1.1 %reduce-window.6 = f32[4,8,128]{2,1,0:T(8,128)S(1)} reduce-window(f32[4,8,128]{2,1,0:T(8,128)S(1)} %bitcast_select_fusion, f32[]{:T(128)} %constant.65.clone.1), window={size=1x1x128 pad=0_0x0_0x127_0}, to_apply=%region_3.4 | reduce-window | flops 520192 | bytes 32772 | tf_op jit(solution)/shard_map/reduce-window
  92.6 0.2 slice_reduce_fusion
  92.7 0.2 reduce-window.9
  92.9 0.1 add_bitcast_fusion
  93.0 12.1 %while.1 = (s32[]{:T(128)}, f32[4,2048]{1,0:T(4,128)S(1)}, s32[8,2]{0,1:T(2,128)S(1)}, f32[8,4,1024]{2,0,1:T(8,128)S(1)}, s32[]{:T(128)}, /*index=5*/s32[]{:T(128)}) while((s32[]{:T(128)}, f32[4,2048]{1,0:T(4,128)S(1)}, s32[8,2]{0,1:T(2,128)S(1)}, f32[8,4,1024]{2,0,1:T(8,128)S(1)}, s32[]{:T(128)}, /*index=5*/s32[]{:T(128)}) %tuple.16), condition=%wide.while_cond, body=%wide.while_body.sunk | while | flops 2 | bytes 98417 | solution.py:23
  93.1 0.5 slice.108
  93.6 0.7 dynamic-slice_bitcast_fusion.2
  94.3 0.1 dynamic-update-slice.3
  94.6 0.5 slice.108
  95.1 0.7 dynamic-slice_bitcast_fusion.2
  95.9 0.1 dynamic-update-slice.3
  96.1 0.5 slice.108
  96.6 0.7 dynamic-slice_bitcast_fusion.2
  97.4 0.1 dynamic-update-slice.3
  97.6 0.5 slice.108
  98.1 0.7 dynamic-slice_bitcast_fusion.2
  98.9 0.1 dynamic-update-slice.3
  99.1 0.5 slice.108
  99.6 0.7 dynamic-slice_bitcast_fusion.2
  100.4 0.1 dynamic-update-slice.3
  100.6 0.5 slice.108
  101.1 0.7 dynamic-slice_bitcast_fusion.2
  101.9 0.1 dynamic-update-slice.3
  102.1 0.5 slice.108
  102.6 0.7 dynamic-slice_bitcast_fusion.2
  103.4 0.1 dynamic-update-slice.3
  103.6 0.5 slice.108
  104.2 0.7 dynamic-slice_bitcast_fusion.2
  104.9 0.1 dynamic-update-slice.3
  105.1 0.7 divide_bitcast_fusion
  (37 shorter events, 0.9 us)
Async XLA Ops:
  0.0 8.9 %copy-start = (bf16[128,8192]{1,0:T(8,128)(2,1)S(1)}, bf16[128,8192]{1,0:T(8,128)(2,1)}, u32[]{:S(2)}) copy-start(bf16[128,8192]{1,0:T(8,128)(2,1)} %param.4) | copy-start | bytes 6291460
  1.5 71.5 %all-to-all-start = ((s32[4,16,1]{0,2,1:T(1,128)}), s32[4,16,1]{0,2,1:T(1,128)S(1)}, u32[]{:S(2)}, u32[]{:S(2)}) async-start(s32[4,16,1]{0,2,1:T(1,128)} %copy.11), calls=%async_computation | async-start | bytes 16384 | tf_op jit(solution)/shard_map/all_to_all | solution.py:60
  72.0 9.3 %copy-start.2 = (s32[8]{0:T(128)S(1)}, s32[8]{0:T(128)}, u32[]{:S(2)}) copy-start(s32[8]{0:T(128)} %param.7) | copy-start | bytes 100
  72.0 9.4 %copy-start.1 = (s32[16]{0:T(128)S(1)}, s32[16]{0:T(128)}, u32[]{:S(2)}) copy-start(s32[16]{0:T(128)} %param.6) | copy-start | bytes 196
  77.8 13.5 %all-to-all-start.1 = ((f32[16,4,1024]{2,1,0:T(4,128)}), f32[16,4,1024]{2,1,0:T(4,128)S(1)}, u32[]{:S(2)}, u32[]{:S(2)}) async-start(f32[16,4,1024]{2,1,0:T(4,128)} %reshape.171), calls=%async_computation.1 | async-start | bytes 524288 | tf_op jit(solution)/shard_map/all_to_all | solution.py:66
where the time goes:
time: 106 us
  blocking collectives  61.9 us (58%)
  local copies, waits for them, and re-layouts  18.9 us (18%)
  starting transfers between devices  10.9 us (10%)
  waiting for transfers between devices  8.69 us (8%)
  other arithmetic  3.51 us (3%)
    psum x1, blocking collectives, on_device(): channel_mean = lax.psum(local_sums, 'trials') / channels  61.9 us
    gather x40, local copies, waits for them, and re-layouts  11.8 us
    all_to_all x1, waiting for transfers between devices, on_device(): lax.all_to_all(window, 'trials', split_axis=0, concat_axis=0, tiled=True)  8.69 us
    all_to_all x1, starting transfers between devices, on_device(): lax.all_to_all(delays, 'trials', split_axis=1, concat_axis=0, tiled=True)  7.39 us
    gather x1, local copies, waits for them, and re-layouts, on_device(): series_blocks[trial_sub[:, None], own_delays[:, None] + offsets[None, :]]  3.66 us
    all_to_all x1, starting transfers between devices, on_device(): lax.all_to_all(window, 'trials', split_axis=0, concat_axis=0, tiled=True)  3.53 us
  transfers between devices with their start and end apart: 2, of which 1 were waited for; matrix products, arithmetic and copies ran while one was open for 3% of the time, Pallas kernels for 0%

commit v1 on v0

v1 whole, which is shorter than its diff:
```python
import functools

import jax
import jax.numpy as jnp
from jax import lax
from jax.experimental import pallas as pl
from jax.experimental.pallas import tpu as pltpu
from jax.sharding import PartitionSpec as P

CH_SUB = 128
SUBT = 2
SPAN = 8
KMAX = 8
LANES = 128
PER_LAG = CH_SUB // KMAX
VMEM = pltpu.MemorySpace.VMEM
SMEM = pltpu.MemorySpace.SMEM


def in_vmem(x):
    return pltpu.with_memory_space_constraint(x, VMEM)


def swap(x, bit, group):
    return lax.ppermute(x, "trials", [(i, i ^ bit) for i in range(group)])


def shifted(x, k):
    lane = lax.broadcasted_iota(jnp.int32, x.shape, 1)
    row = lax.broadcasted_iota(jnp.int32, x.shape, 0)
    here = pltpu.roll(x, LANES - k, 1)
    after = pltpu.roll(here, x.shape[0] - 1, 0)
    after = jnp.where(row == x.shape[0] - 1, 0.0, after)
    return jnp.where(lane < LANES - k, here, after)


def raw_kernel(chunks, x_hbm, out, x, sems):
    blocks = out.shape[1]
    width = x.shape[1] // chunks
    copies = []
    for i in range(chunks):
        part = pl.ds(i * width, width)
        copies.append(pltpu.make_async_copy(x_hbm.at[:, part], x.at[:, part], sems.at[i]))
        copies[-1].start()
    row = lax.broadcasted_iota(jnp.int32, (2 * KMAX, CH_SUB), 0)
    chan = lax.broadcasted_iota(jnp.int32, (2 * KMAX, CH_SUB), 1)
    select = ((row >= KMAX) | (chan // PER_LAG == KMAX - 1 - row)).astype(jnp.bfloat16)
    sub = lax.broadcasted_iota(jnp.int32, (KMAX, LANES), 0)
    lane = lax.broadcasted_iota(jnp.int32, (KMAX, LANES), 1)
    stays = lane < LANES - (KMAX - 1 - sub)
    per = width // LANES
    rolled, plain = [], []
    for i in range(chunks):
        copies[i].wait()
        sums = jnp.dot(select, x[:, i * width : (i + 1) * width], preferred_element_type=jnp.float32)
        for b in range(per):
            cut = sums[:KMAX, b * LANES : (b + 1) * LANES]
            rolled.append(pltpu.roll(cut, LANES - (KMAX - 1), 1, stride=1, stride_axis=0))
            plain.append(sums[KMAX:, b * LANES : (b + 1) * LANES])
    rolled.append(jnp.zeros((KMAX, LANES), jnp.float32))
    for b0 in range(0, blocks, 8):
        first = plain[b0]
        for k in range(1, 8):
            first = jnp.where(sub == k, plain[b0 + k], first)
        out[0, b0 : b0 + 8] = first
        level = [jnp.where(stays, rolled[b], rolled[b + 1]) for b in range(b0, b0 + 8)]
        for half in (4, 2, 1):
            low = (sub & half) == 0
            level = [
                jnp.where(low, level[k], level[k + half])
                + pltpu.roll(jnp.where(low, level[k + half], level[k]), half, 0)
                if half == 4
                else jnp.where(low, level[k] + pltpu.roll(level[k], 8 - half, 0), level[k + half] + pltpu.roll(level[k + half], half, 0))
                for k in range(half)
            ]
        out[1, b0 : b0 + 8] = level[0]


def raw_series(spectra):
    samples = spectra.shape[1]
    chunks = 4
    return pl.pallas_call(
        functools.partial(raw_kernel, chunks),
        out_shape=VMEM((SUBT, samples // LANES, LANES), jnp.float32),
        in_specs=[pl.BlockSpec(memory_space=pl.ANY)],
        out_specs=pl.BlockSpec(memory_space=VMEM),
        scratch_shapes=[pltpu.VMEM(spectra.shape, spectra.dtype), pltpu.SemaphoreType.DMA((chunks,))],
    )(spectra)


def window_kernel(masks, owners, channels, *refs):
    known = len(masks)
    raw, rest = refs[:known], refs[known:]
    delays_in, out, mean, delays, sems = rest[:owners], rest[owners], rest[owners + 1], rest[owners + 2], rest[owners + 3]
    copies = [pltpu.make_async_copy(delays_in[e], delays.at[e], sems.at[e]) for e in range(owners)]
    for c in copies:
        c.start()
    total = raw[0][0]
    for a in range(1, known):
        total = total + raw[a][0]
    mean[0] = total * (CH_SUB / channels)
    total = total * (PER_LAG / channels)
    for k in (1, 2, 4):
        total = total + shifted(total, k)
    mean[1] = total
    me = lax.axis_index("trials")
    trials, group = delays.shape[1:]
    for c in copies:
        c.wait()

    def one(e):
        for i in range(trials):
            j = i % SUBT
            acc = None
            for a in range(known):
                cut = raw[a][j, pl.ds(delays[e, i, me ^ masks[a]], SPAN), :]
                acc = cut if acc is None else acc + cut
            less = None
            if group <= 16:
                for s in range(group):
                    cut = mean[j, pl.ds(delays[e, i, s], SPAN), :]
                    less = cut if less is None else less + cut
            else:
                less = lax.fori_loop(
                    0, group, lambda s, v: v + mean[j, pl.ds(delays[e, i, s], SPAN), :], jnp.zeros_like(acc)
                )
            out[e, i] = acc - less

    if owners <= 4:
        for e in range(owners):
            one(e)
    else:
        pl.loop(0, owners)(one)


def window_sums(raw, masks, delays, channels):
    owners = len(delays)
    trials, group = delays[0].shape
    samples = raw[0].shape[1:]
    return pl.pallas_call(
        functools.partial(window_kernel, masks, owners, channels),
        out_shape=VMEM((owners, trials, SPAN, LANES), jnp.float32),
        in_specs=[pl.BlockSpec(memory_space=VMEM)] * len(raw) + [pl.BlockSpec(memory_space=pl.ANY)] * owners,
        out_specs=pl.BlockSpec(memory_space=VMEM),
        scratch_shapes=[
            pltpu.VMEM((SUBT,) + samples, jnp.float32),
            pltpu.SMEM((owners, trials, group), jnp.int32),
            pltpu.SemaphoreType.DMA((owners,)),
        ],
    )(*[in_vmem(r) for r in raw], *delays)


def boxcar_kernel(channels, parts, *refs):
    ins, (spans_in, widths_in, out, spans, widths, sems) = refs[:parts], refs[parts:]
    copies = [
        pltpu.make_async_copy(spans_in, spans, sems.at[0]),
        pltpu.make_async_copy(widths_in, widths, sems.at[1]),
    ]
    for c in copies:
        c.start()
    trial = ins[0][...]
    for p in range(1, parts):
        trial = trial + ins[p][...]
    trials = trial.shape[0]
    flat = trial.reshape(trials * SPAN, LANES)
    block = lax.broadcasted_iota(jnp.int32, flat.shape, 0) % SPAN
    lane = lax.broadcasted_iota(jnp.int32, flat.shape, 1)
    copies[0].wait()
    flat = jnp.where(block < spans[lax.axis_index("trials")], flat, 0.0)
    prefix = flat
    for k in (1, 2, 4, 8, 16, 32, 64):
        prefix = prefix + jnp.where(lane >= k, pltpu.roll(prefix, k, 1), 0.0)
    ends = jnp.broadcast_to(prefix[:, LANES - 1 :], prefix.shape)
    before = jnp.where(block >= 1, pltpu.roll(ends, 1, 0), 0.0)
    for k in (1, 2, 4):
        before = before + jnp.where(block >= k, pltpu.roll(before, k, 0), 0.0)
    prefix = prefix + before
    copies[1].wait()
    for w in range(widths.shape[0]):
        width = widths[w]
        scale = 1.0 / (jnp.sqrt(jnp.full((SPAN, LANES), width, jnp.float32)) * (channels**0.5))
        here = pltpu.roll(prefix, width, 1)
        last = jnp.where(block >= 1, pltpu.roll(here, 1, 0), 0.0)
        lagged = jnp.where(lane >= width, here, last)
        diff = (prefix - lagged).reshape(trials, SPAN, LANES)
        for t in range(trials):
            out[t, :, w, :] = diff[t] * scale


def boxcars(parts, spans, widths, channels):
    trials = parts[0].shape[0]
    nw = widths.shape[0]
    out = pl.pallas_call(
        functools.partial(boxcar_kernel, channels, len(parts)),
        out_shape=jax.ShapeDtypeStruct((trials, SPAN, nw, LANES), jnp.float32),
        in_specs=[pl.BlockSpec(memory_space=VMEM)] * len(parts) + [pl.BlockSpec(memory_space=pl.ANY)] * 2,
        out_specs=pl.BlockSpec(memory_space=VMEM),
        scratch_shapes=[
            pltpu.SMEM(spans.shape, jnp.int32),
            pltpu.SMEM(widths.shape, jnp.int32),
            pltpu.SemaphoreType.DMA((2,)),
        ],
    )(*[in_vmem(p) for p in parts], spans, widths)
    return out.transpose(0, 2, 1, 3).reshape(trials, nw, SPAN * LANES)


def on_device(spectra, delays, spans, widths):
    group = lax.axis_size("trials")
    channels = CH_SUB * group
    gather_bits = [b for b in (2, 4) if b < group]
    sum_bits = [b for b in (1, 8, 16, 32, 64, 128, 256) if b < group]

    raw = [raw_series(spectra)]
    masks = [0]
    for b in gather_bits:
        raw = raw + [swap(r, b, group) for r in raw]
        masks = masks + [m ^ b for m in masks]

    owned = [delays]
    for b in reversed(sum_bits):
        owned = owned + [swap(d, b, group) for d in owned]

    sums = window_sums(raw, masks, owned, channels)
    for n, b in enumerate(sum_bits):
        half = sums.shape[0] // 2
        mine, theirs = sums[:half], swap(sums[half:], b, group)
        if n + 1 < len(sum_bits):
            sums = mine + theirs
    return boxcars([mine[0], theirs[0]], spans, widths, channels)


def solution(mesh):
    in_specs = (P(("beams", "trials"), None), P("trials", None), P(), P())
    out_specs = P(("beams", "trials"), None, None)
    return jax.shard_map(
        on_device, mesh=mesh, in_specs=in_specs, out_specs=out_specs, check_vma=False
    )
```

time: 106 us -> 25.1 us (0.24)
  blocking collectives: 61.9 us -> 0 us
  local copies, waits for them, and re-layouts: 18.9 us -> 0.55 us
  Pallas kernels: 0 us -> 5.29 us
  other arithmetic: 3.51 us -> 0.01 us
  waiting for transfers between devices: 8.69 us -> 6.79 us
  starting transfers between devices: 10.9 us -> 12.2 us
    psum x1 -> x0, blocking collectives: 61.9 us -> none  [on_device(): channel_mean = lax.psum(local_sums, 'trials') / channels]
    gather x41 -> x0, local copies, waits for them, and re-layouts: 15.5 us -> none
    ppermute x0 -> x8, starting transfers between devices: none -> 12.2 us  [swap(): return lax.ppermute(x, 'trials', [(i, i ^ bit) for i in range(group)])]
    all_to_all x2 -> x0, starting transfers between devices: 10.9 us -> none  [the longest x1 7.39 us: on_device(): lax.all_to_all(delays, 'trials', split_axis=1, concat_axis=0, tiled=True)]
    all_to_all x2 -> x0, waiting for transfers between devices: 8.69 us -> none  [the longest x1 8.69 us: on_device(): lax.all_to_all(window, 'trials', split_axis=0, concat_axis=0, tiled=True)]
    ppermute x0 -> x8, waiting for transfers between devices: none -> 6.79 us  [swap(): return lax.ppermute(x, 'trials', [(i, i ^ bit) for i in range(group)])]
    pallas_call x0 -> x3, Pallas kernels: none -> 5.29 us  [the longest x1 2.11 us: raw_series(): pl.pallas_call(functools.partial(raw_kernel, chunks), out_shape=VMEM((SUB...]
    div x3 -> x0, other arithmetic: 1.76 us -> none  [the longest x1 1.01 us: subband_series(): return time_series / jnp.sqrt(jnp.float32(channels))]
  transfers between devices with their start and end apart: 2 -> 8, of which waited for: 1 -> 5; matrix products, arithmetic and copies ran while one was open for 3% -> 0% of each run, Pallas kernels for 0% -> 0%
where the time goes in v1:
time: 25.1 us; the launch traced here: 24.9 us
  starting transfers between devices  12.2 us (49%)
  waiting for transfers between devices  6.79 us (27%)
  Pallas kernels  5.29 us (21%)
  local copies, waits for them, and re-layouts  0.55 us (2%)
    ppermute x8, starting transfers between devices, swap(): return lax.ppermute(x, 'trials', [(i, i ^ bit) for i in range(group)])  12.2 us
    ppermute x8, waiting for transfers between devices, swap(): return lax.ppermute(x, 'trials', [(i, i ^ bit) for i in range(group)])  6.79 us
    pallas_call x1, Pallas kernels, raw_series(): pl.pallas_call(functools.partial(raw_kernel, chunks), out_shape=VMEM((SUB...  2.11 us
    pallas_call x1, Pallas kernels, boxcars(): pl.pallas_call(functools.partial(boxcar_kernel, channels, len(parts)), ou...  2.09 us
    pallas_call x1, Pallas kernels, window_sums(): pl.pallas_call(functools.partial(window_kernel, masks, owners, channels),...  1.09 us
    unnamed x8, local copies, waits for them, and re-layouts  0.54 us
  transfers between devices with their start and end apart: 8, of which 5 were waited for; matrix products, arithmetic and copies ran while one was open for 0% of the time, Pallas kernels for 0%

profile of v1, /device:TPU:0, one launch (start us, length us, event | category | flops | bytes accessed | tf_op | source)
XLA Modules:
  0.0 24.9 jit_solution(4873572737974512829)
XLA Ops:
  0.0 0.0 copy-start
  0.0 2.1 %shard_map.46.refs_0_ = f32[2,64,128]{2,1,0:T(8,128)S(1)} custom-call(bf16[128,8192]{1,0:T(8,128)(2,1)} %x_hbm.1), custom_call_target="tpu_custom_call" | custom-call | tf_op jit(solution)/shard_map/pallas_call | solution.py:82
  2.1 3.0 %collective-permute-start = (f32[2,64,128]{2,1,0:T(8,128)S(1)}, f32[2,64,128]{2,1,0:T(8,128)S(1)}, u32[]{:S(2)}, u32[]{:S(2)}) collective-permute-start(f32[2,64,128]{2,1,0:T(8,128)S(1)} %shard_map.46.refs_0_), channel_id=1, source_target_pairs={{0,2},{1,3},{2,0},{3,1},{4,6},{5,7},{6,4},{7,5},{8,10},{9,11},{10,... | collective-permute-start | bytes 196616 | tf_op jit(solution)/shard_map/ppermute | solution.py:25
  5.2 1.6 %collective-permute-start.1 = (f32[2,64,128]{2,1,0:T(8,128)S(1)}, f32[2,64,128]{2,1,0:T(8,128)S(1)}, u32[]{:S(2)}, u32[]{:S(2)}) collective-permute-start(f32[2,64,128]{2,1,0:T(8,128)S(1)} %shard_map.46.refs_0_), channel_id=1, source_target_pairs={{0,4},{1,5},{2,6},{3,7},{4,0},{5,1},{6,2},{7,3},{8,12},{9,13},{10,... | collective-permute-start | bytes 196616 | tf_op jit(solution)/shard_map/ppermute | solution.py:25
  6.7 0.7 %collective-permute-done.refs_1_ = f32[2,64,128]{2,1,0:T(8,128)S(1)} collective-permute-done((f32[2,64,128]{2,1,0:T(8,128)S(1)}, f32[2,64,128]{2,1,0:T(8,128)S(1)}, u32[]{:S(2)}, u32[]{:S(2)}) %collective-permute-start) | collective-permute-done | bytes 65568 | tf_op jit(solution)/shard_map/ppermute | solution.py:25
  7.4 2.1 %collective-permute-start.2 = (f32[2,64,128]{2,1,0:T(8,128)S(1)}, f32[2,64,128]{2,1,0:T(8,128)S(1)}, u32[]{:S(2)}, u32[]{:S(2)}) collective-permute-start(f32[2,64,128]{2,1,0:T(8,128)S(1)} %collective-permute-done.refs_1_), channel_id=1, source_target_pairs={{0,4},{1,5},{2,6},{3,7},{4,0},{5,1},{6,2},{7,3},{8,12},{9,13},{10,... | collective-permute-start | bytes 196616 | tf_op jit(solution)/shard_map/ppermute | solution.py:25
  9.5 0.0 copy-done
  9.5 2.6 %collective-permute-start.3 = (s32[4,16]{1,0:T(4,128)S(1)}, s32[4,16]{1,0:T(4,128)S(1)}, u32[]{:S(2)}, u32[]{:S(2)}) collective-permute-start(s32[4,16]{1,0:T(4,128)S(1)} %copy-done), channel_id=1, source_target_pairs={{0,8},{1,9},{2,10},{3,11},{4,12},{5,13},{6,14},{7,15},{8,0},{9,1},... | collective-permute-start | bytes 776 | tf_op jit(solution)/shard_map/ppermute | solution.py:25
  12.1 0.0 collective-permute-start.4
  12.1 1.9 %collective-permute-done.3.refs_5_ = s32[4,16]{1,0:T(4,128)S(1)} collective-permute-done((s32[4,16]{1,0:T(4,128)S(1)}, s32[4,16]{1,0:T(4,128)S(1)}, u32[]{:S(2)}, u32[]{:S(2)}) %collective-permute-start.3) | collective-permute-done | bytes 288 | tf_op jit(solution)/shard_map/ppermute | solution.py:25
  14.0 0.0 copy-start.1
  14.0 0.0 collective-permute-start.5
  14.0 0.0 collective-permute-done.4.refs_6_
  14.0 0.0 copy-start.2
  14.0 1.1 %collective-permute-done.5.refs_7_ = s32[4,16]{1,0:T(4,128)S(1)} collective-permute-done((s32[4,16]{1,0:T(4,128)S(1)}, s32[4,16]{1,0:T(4,128)S(1)}, u32[]{:S(2)}, u32[]{:S(2)}) %collective-permute-start.5) | collective-permute-done | bytes 288 | tf_op jit(solution)/shard_map/ppermute | solution.py:25
  15.1 0.0 copy-start.3
  15.1 0.0 collective-permute-done.1.refs_2_
  15.1 0.0 collective-permute-done.2.refs_3_
  15.1 0.0 copy-done.1
  15.1 0.0 copy-done.2
  15.2 0.5 %copy-done.3 = s32[4,16]{1,0:T(4,128)} copy-done((s32[4,16]{1,0:T(4,128)}, s32[4,16]{1,0:T(4,128)S(1)}, u32[]{:S(2)}) %copy-start.3) | copy-done | bytes 280
  15.7 1.1 %shard_map.47 = f32[4,4,8,128]{3,2,1,0:T(8,128)S(1)} custom-call(f32[2,64,128]{2,1,0:T(8,128)S(1)} %shard_map.46.refs_0_, f32[2,64,128]{2,1,0:T(8,128)S(1)} %collective-permute-done.refs_1_, f32[2,64,128]{2,1,0:T(8,128)S(1)} %collective-permute-done.1.refs_2_, f32[2,64,128]{2,1,0:T(8,128)S(1)} %collective-permute-done.2.refs_3_, s32[4,16]{1,0:T(4,128)} %refs_4_.1, ...), custom_call_target="tpu_custom_call" | custom-call | tf_op jit(solution)/shard_map/pallas_call | solution.py:140
  16.8 0.2 collective-permute-start.6
  17.0 1.0 %collective-permute-done.6 = f32[2,4,8,128]{3,2,1,0:T(8,128)S(1)} collective-permute-done((f32[2,4,8,128]{3,2,1,0:T(8,128)S(1)}, f32[2,4,8,128]{3,2,1,0:T(8,128)S(1)}, u32[]{:S(2)}, u32[]{:S(2)}) %collective-permute-start.6) | collective-permute-done | bytes 32800 | tf_op jit(solution)/shard_map/ppermute | solution.py:25
  18.1 2.7 %collective-permute-start.7 = (f32[1,4,8,128]{3,2,1,0:T(8,128)S(1)}, f32[1,4,8,128]{3,2,1,0:T(8,128)S(1)}, u32[]{:S(2)}, u32[]{:S(2)}) collective-permute-start(f32[1,4,8,128]{3,2,1,0:T(8,128)S(1)} %get-tuple-element.5), channel_id=1, source_target_pairs={{0,8},{1,9},{2,10},{3,11},{4,12},{5,13},{6,14},{7,15},{8,0},{9,1},... | collective-permute-start | bytes 49160 | tf_op jit(solution)/shard_map/ppermute | solution.py:25
  20.7 2.0 %collective-permute-done.7 = f32[1,4,8,128]{3,2,1,0:T(8,128)S(1)} collective-permute-done((f32[1,4,8,128]{3,2,1,0:T(8,128)S(1)}, f32[1,4,8,128]{3,2,1,0:T(8,128)S(1)}, u32[]{:S(2)}, u32[]{:S(2)}) %collective-permute-start.7) | collective-permute-done | bytes 16416 | tf_op jit(solution)/shard_map/ppermute | solution.py:25
  22.8 2.1 %shard_map.48 = f32[4,8,8,128]{3,2,1,0:T(8,128)} custom-call(f32[4,8,128]{2,1,0:T(8,128)S(1)} %get-tuple-element.6.refs_0_, f32[4,8,128]{2,1,0:T(8,128)S(1)} %bitcast.6, s32[16]{0:T(128)} %refs_2_.1, s32[8]{0:T(128)} %refs_3_.1), custom_call_target="tpu_custom_call" | custom-call | tf_op jit(solution)/shard_map/pallas_call | solution.py:193
  (3 shorter events, 0.0 us)
Async XLA Ops:
  0.0 9.5 %copy-start = (s32[4,16]{1,0:T(4,128)S(1)}, s32[4,16]{1,0:T(4,128)}, u32[]{:S(2)}) copy-start(s32[4,16]{1,0:T(4,128)} %refs_4_.1) | copy-start | bytes 772
  2.1 5.3 %collective-permute-start = (f32[2,64,128]{2,1,0:T(8,128)S(1)}, f32[2,64,128]{2,1,0:T(8,128)S(1)}, u32[]{:S(2)}, u32[]{:S(2)}) collective-permute-start(f32[2,64,128]{2,1,0:T(8,128)S(1)} %shard_map.46.refs_0_), channel_id=1, source_target_pairs={{0,2},{1,3},{2,0},{3,1},{4,6},{5,7},{6,4},{7,5},{8,10},{9,11},{10,... | collective-permute-start | bytes 196616 | tf_op jit(solution)/shard_map/ppermute | solution.py:25
  5.2 10.0 %collective-permute-start.1 = (f32[2,64,128]{2,1,0:T(8,128)S(1)}, f32[2,64,128]{2,1,0:T(8,128)S(1)}, u32[]{:S(2)}, u32[]{:S(2)}) collective-permute-start(f32[2,64,128]{2,1,0:T(8,128)S(1)} %shard_map.46.refs_0_), channel_id=1, source_target_pairs={{0,4},{1,5},{2,6},{3,7},{4,0},{5,1},{6,2},{7,3},{8,12},{9,13},{10,... | collective-permute-start | bytes 196616 | tf_op jit(solution)/shard_map/ppermute | solution.py:25
  7.4 7.7 %collective-permute-start.2 = (f32[2,64,128]{2,1,0:T(8,128)S(1)}, f32[2,64,128]{2,1,0:T(8,128)S(1)}, u32[]{:S(2)}, u32[]{:S(2)}) collective-permute-start(f32[2,64,128]{2,1,0:T(8,128)S(1)} %collective-permute-done.refs_1_), channel_id=1, source_target_pairs={{0,4},{1,5},{2,6},{3,7},{4,0},{5,1},{6,2},{7,3},{8,12},{9,13},{10,... | collective-permute-start | bytes 196616 | tf_op jit(solution)/shard_map/ppermute | solution.py:25
  9.5 4.5 %collective-permute-start.3 = (s32[4,16]{1,0:T(4,128)S(1)}, s32[4,16]{1,0:T(4,128)S(1)}, u32[]{:S(2)}, u32[]{:S(2)}) collective-permute-start(s32[4,16]{1,0:T(4,128)S(1)} %copy-done), channel_id=1, source_target_pairs={{0,8},{1,9},{2,10},{3,11},{4,12},{5,13},{6,14},{7,15},{8,0},{9,1},... | collective-permute-start | bytes 776 | tf_op jit(solution)/shard_map/ppermute | solution.py:25
  12.1 1.9 %collective-permute-start.4 = (s32[4,16]{1,0:T(4,128)S(1)}, s32[4,16]{1,0:T(4,128)S(1)}, u32[]{:S(2)}, u32[]{:S(2)}) collective-permute-start(s32[4,16]{1,0:T(4,128)S(1)} %copy-done), channel_id=1, source_target_pairs={{0,1},{1,0},{2,3},{3,2},{4,5},{5,4},{6,7},{7,6},{8,9},{9,8},{10,11... | collective-permute-start | bytes 776 | tf_op jit(solution)/shard_map/ppermute | solution.py:25
  14.0 1.2 %copy-start.1 = (s32[4,16]{1,0:T(4,128)}, s32[4,16]{1,0:T(4,128)S(1)}, u32[]{:S(2)}) copy-start(s32[4,16]{1,0:T(4,128)S(1)} %collective-permute-done.3.refs_5_) | copy-start | bytes 772
  14.0 1.2 %collective-permute-start.5 = (s32[4,16]{1,0:T(4,128)S(1)}, s32[4,16]{1,0:T(4,128)S(1)}, u32[]{:S(2)}, u32[]{:S(2)}) collective-permute-start(s32[4,16]{1,0:T(4,128)S(1)} %collective-permute-done.3.refs_5_), channel_id=1, source_target_pairs={{0,1},{1,0},{2,3},{3,2},{4,5},{5,4},{6,7},{7,6},{8,9},{9,8},{10,11... | collective-permute-start | bytes 776 | tf_op jit(solution)/shard_map/ppermute | solution.py:25
  14.0 1.2 %copy-start.2 = (s32[4,16]{1,0:T(4,128)}, s32[4,16]{1,0:T(4,128)S(1)}, u32[]{:S(2)}) copy-start(s32[4,16]{1,0:T(4,128)S(1)} %collective-permute-done.4.refs_6_) | copy-start | bytes 772
  15.1 0.6 %copy-start.3 = (s32[4,16]{1,0:T(4,128)}, s32[4,16]{1,0:T(4,128)S(1)}, u32[]{:S(2)}) copy-start(s32[4,16]{1,0:T(4,128)S(1)} %collective-permute-done.5.refs_7_) | copy-start | bytes 772
  16.8 1.3 %collective-permute-start.6 = (f32[2,4,8,128]{3,2,1,0:T(8,128)S(1)}, f32[2,4,8,128]{3,2,1,0:T(8,128)S(1)}, u32[]{:S(2)}, u32[]{:S(2)}) collective-permute-start(f32[2,4,8,128]{3,2,1,0:T(8,128)S(1)} %slice.17), channel_id=1, source_target_pairs={{0,1},{1,0},{2,3},{3,2},{4,5},{5,4},{6,7},{7,6},{8,9},{9,8},{10,11... | collective-permute-start | bytes 98312 | tf_op jit(solution)/shard_map/ppermute | solution.py:25
  18.1 4.7 %collective-permute-start.7 = (f32[1,4,8,128]{3,2,1,0:T(8,128)S(1)}, f32[1,4,8,128]{3,2,1,0:T(8,128)S(1)}, u32[]{:S(2)}, u32[]{:S(2)}) collective-permute-start(f32[1,4,8,128]{3,2,1,0:T(8,128)S(1)} %get-tuple-element.5), channel_id=1, source_target_pairs={{0,8},{1,9},{2,10},{3,11},{4,12},{5,13},{6,14},{7,15},{8,0},{9,1},... | collective-permute-start | bytes 49160 | tf_op jit(solution)/shard_map/ppermute | solution.py:25

commit v2 on v0

v2 whole, which is shorter than its diff:
```python
import functools

import jax
import jax.numpy as jnp
from jax import lax
from jax.experimental import pallas as pl
from jax.experimental.pallas import tpu as pltpu
from jax.sharding import PartitionSpec as P

CH_SUB = 128
SUBT = 2
SPAN = 8
KMAX = 8
LANES = 128
PER_LAG = CH_SUB // KMAX
VMEM = pltpu.MemorySpace.VMEM
SMEM = pltpu.MemorySpace.SMEM
IN_VMEM = pl.BlockSpec(memory_space=VMEM)
IN_SMEM = pl.BlockSpec(memory_space=SMEM)


def in_vmem(x):
    return pltpu.with_memory_space_constraint(x, VMEM)


def in_smem(x):
    return pltpu.with_memory_space_constraint(x, SMEM)


def cost(flops, read):
    return pl.CostEstimate(flops=flops, bytes_accessed=read, transcendentals=0)


def swap(x, bit, group):
    return lax.ppermute(x, "trials", [(i, i ^ bit) for i in range(group)])


def shifted(x, k):
    lane = lax.broadcasted_iota(jnp.int32, x.shape, 1)
    row = lax.broadcasted_iota(jnp.int32, x.shape, 0)
    here = pltpu.roll(x, LANES - k, 1)
    after = pltpu.roll(here, x.shape[0] - 1, 0)
    after = jnp.where(row == x.shape[0] - 1, 0.0, after)
    return jnp.where(lane < LANES - k, here, after)


def raw_kernel(chunks, x_hbm, delays_hbm, out, rows, x, delays, sems):
    blocks = x.shape[1] // LANES
    width = x.shape[1] // chunks
    copies = []
    for i in range(chunks):
        part = pl.ds(i * width, width)
        copies.append(pltpu.make_async_copy(x_hbm.at[:, part], x.at[:, part], sems.at[i]))
        copies[-1].start()
    copies.append(pltpu.make_async_copy(delays_hbm, delays, sems.at[chunks]))
    copies[-1].start()
    row = lax.broadcasted_iota(jnp.int32, (2 * KMAX, CH_SUB), 0)
    chan = lax.broadcasted_iota(jnp.int32, (2 * KMAX, CH_SUB), 1)
    select = ((row >= KMAX) | (chan // PER_LAG == KMAX - 1 - row)).astype(jnp.bfloat16)
    sub = lax.broadcasted_iota(jnp.int32, (KMAX, LANES), 0)
    lane = lax.broadcasted_iota(jnp.int32, (KMAX, LANES), 1)
    stays = lane < LANES - (KMAX - 1 - sub)
    rows[...] = jnp.zeros_like(rows)
    rolled, plain = [], []

    def finish(b0):
        first = plain[b0]
        for k in range(1, 8):
            first = jnp.where(sub == k, plain[b0 + k], first)
        out[0, b0 : b0 + 8] = first
        level = [jnp.where(stays, rolled[b], rolled[b + 1]) for b in range(b0, b0 + 8)]
        for half in (4, 2, 1):
            low = (sub & half) == 0
            level = [
                jnp.where(low, level[k] + pltpu.roll(level[k], 8 - half, 0), level[k + half] + pltpu.roll(level[k + half], half, 0))
                for k in range(half)
            ]
        out[1, b0 : b0 + 8] = level[0]

    for b0 in range(0, blocks, 8):
        if b0 * LANES % width == 0:
            copies[b0 * LANES // width].wait()
        part = x[:, b0 * LANES : (b0 + 8) * LANES]
        sums = jnp.dot(select, part, preferred_element_type=jnp.float32)
        for b in range(8):
            cut = sums[:KMAX, b * LANES : (b + 1) * LANES]
            rolled.append(pltpu.roll(cut, LANES - (KMAX - 1), 1, stride=1, stride_axis=0))
            plain.append(sums[KMAX:, b * LANES : (b + 1) * LANES])
        if b0:
            finish(b0 - 8)
    rolled.append(jnp.zeros((KMAX, LANES), jnp.float32))
    finish(blocks - 8)
    copies[chunks].wait()
    rows[: delays.shape[0], : delays.shape[1]] = delays[...]


def raw_series(spectra, delays):
    channels, samples = spectra.shape
    chunks = 2
    return pl.pallas_call(
        functools.partial(raw_kernel, chunks),
        out_shape=(VMEM((SUBT, samples // LANES, LANES), jnp.float32), VMEM((8, LANES), jnp.int32)),
        in_specs=[pl.BlockSpec(memory_space=pl.ANY)] * 2,
        out_specs=(IN_VMEM,) * 2,
        scratch_shapes=[
            pltpu.VMEM(spectra.shape, spectra.dtype),
            pltpu.VMEM(delays.shape, delays.dtype),
            pltpu.SemaphoreType.DMA((chunks + 1,)),
        ],
        cost_estimate=cost(4 * KMAX * channels * samples, 2 * channels * samples),
    )(spectra, delays)


def pack_kernel(mine, theirs, both):
    core = lax.axis_index("trials") & 1
    first = core == 0
    both[...] = jnp.zeros_like(both)
    rows, cols = theirs.shape
    both[0, :rows, :cols] = jnp.where(first, mine[:rows, :cols], theirs[...])
    both[1, :rows, :cols] = jnp.where(first, theirs[...], mine[:rows, :cols])


def pack_delays(mine, theirs):
    return pl.pallas_call(
        pack_kernel,
        out_shape=VMEM((2,) + mine.shape, jnp.int32),
        in_specs=[IN_VMEM] * 2,
        out_specs=IN_VMEM,
        cost_estimate=cost(0, 1 << 20),
    )(in_vmem(mine), in_vmem(theirs))


def scalars_kernel(x, out, sem):
    copy = pltpu.make_async_copy(x, out, sem)
    copy.start()
    copy.wait()


def to_scalars(x):
    return pl.pallas_call(
        scalars_kernel,
        out_shape=SMEM(x.shape, x.dtype),
        in_specs=[IN_VMEM],
        out_specs=IN_SMEM,
        scratch_shapes=[pltpu.SemaphoreType.DMA(())],
        cost_estimate=cost(0, 1 << 20),
    )(in_vmem(x))


def tables_kernel(channels, widths, spans, bands, scale, mask):
    lag = lax.broadcasted_iota(jnp.int32, (LANES, LANES), 1) - lax.broadcasted_iota(jnp.int32, (LANES, LANES), 0)
    row = lax.broadcasted_iota(jnp.int32, (SPAN, LANES), 0)
    for n in range(widths.shape[0]):
        width = widths[n]
        cols = pl.ds(n * LANES, LANES)
        bands[:LANES, cols] = ((lag >= 0) & (lag < width)).astype(jnp.bfloat16)
        bands[LANES:, cols] = (lag + LANES < width).astype(jnp.bfloat16)
        scale[n : n + 1] = 1.0 / (jnp.sqrt(jnp.full((1, LANES), width, jnp.float32)) * (channels**0.5))
    mask[...] = (row < spans[lax.axis_index("trials")]).astype(jnp.float32)


def tables(widths, spans, channels):
    nw = widths.shape[0]
    return pl.pallas_call(
        functools.partial(tables_kernel, channels),
        out_shape=(
            VMEM((2 * LANES, nw * LANES), jnp.bfloat16),
            VMEM((nw, LANES), jnp.float32),
            VMEM((SPAN, LANES), jnp.float32),
        ),
        in_specs=[IN_SMEM] * 2,
        out_specs=(IN_VMEM,) * 3,
        cost_estimate=cost(0, 1 << 20),
    )(widths, spans)


def windows(out, e, raw, masks, mean, delays, row, trials, group):
    me = lax.axis_index("trials")
    for i in range(trials):
        j = i % SUBT
        acc = None
        for a, ref in enumerate(raw):
            cut = ref[j, pl.ds(delays[row, i, me ^ masks[a]], SPAN), :]
            acc = cut if acc is None else acc + cut
        less = None
        if group <= 16:
            for s in range(group):
                cut = mean[j, pl.ds(delays[row, i, s], SPAN), :]
                less = cut if less is None else less + cut
        else:
            less = lax.fori_loop(
                0, group, lambda s, v: v + mean[j, pl.ds(delays[row, i, s], SPAN), :], jnp.zeros_like(acc)
            )
        out[e, i] = acc - less


def near_kernel(masks, trials, group, channels, *refs):
    known = len(masks)
    raw, (near, keep, send, mean) = refs[:known], refs[known:]
    total = raw[0][0]
    for a in range(1, known):
        total = total + raw[a][0]
    mean[0] = total * (CH_SUB / channels)
    total = total * (PER_LAG / channels)
    for k in (1, 2, 4):
        total = total + shifted(total, k)
    mean[1] = total
    core = lax.axis_index("trials") & 1
    windows(keep, 0, raw, masks, mean, near, core, trials, group)
    windows(send, 0, raw, masks, mean, near, 1 - core, trials, group)


def near_sums(raw, masks, near, trials, group):
    one = VMEM((1, trials, SPAN, LANES), jnp.float32)
    return pl.pallas_call(
        functools.partial(near_kernel, masks, trials, group, CH_SUB * group),
        out_shape=(one, one, VMEM(raw[0].shape, jnp.float32)),
        in_specs=[IN_VMEM] * len(raw) + [IN_SMEM],
        out_specs=(IN_VMEM,) * 3,
        cost_estimate=cost(0, 1 << 20),
    )(*[in_vmem(r) for r in raw], in_smem(near))


def far_kernel(masks, trials, group, *refs):
    known = len(masks)
    raw, (mean, keep_near, send_near, far_in, keep, send, far, sem) = refs[:known], refs[known:]
    copy = pltpu.make_async_copy(far_in, far, sem)
    copy.start()
    core = lax.axis_index("trials") & 1
    chips = far.shape[0] // 2
    keep[:1] = keep_near[...]
    send[:1] = send_near[...]
    copy.wait()

    def chip(e):
        windows(send, e + 1, raw, masks, mean, far, 2 * e + 1 - core, trials, group)
        windows(keep, e + 1, raw, masks, mean, far, 2 * e + core, trials, group)

    if chips == 1:
        chip(0)
    else:
        pl.loop(0, chips)(chip)


def far_sums(raw, masks, mean, keep, send, far, group):
    trials = keep.shape[1]
    half = VMEM((far.shape[0] // 2 + 1, trials, SPAN, LANES), jnp.float32)
    return pl.pallas_call(
        functools.partial(far_kernel, masks, trials, group),
        out_shape=(half, half),
        in_specs=[IN_VMEM] * (len(raw) + 4),
        out_specs=(IN_VMEM,) * 2,
        scratch_shapes=[pltpu.SMEM(far.shape, jnp.int32), pltpu.SemaphoreType.DMA(())],
        cost_estimate=cost(0, 1 << 20),
    )(*[in_vmem(v) for v in (*raw, mean, keep, send, far)])


def boxcar_kernel(a, b, bands, scale, mask, out, y, sems):
    trials = a.shape[0]
    rows = trials * SPAN
    trial = jnp.where(mask[...][None] > 0.0, a[...] + b[...], 0.0).reshape(rows, LANES)
    block = lax.broadcasted_iota(jnp.int32, trial.shape, 0) % SPAN
    before = jnp.where(block >= 1, pltpu.roll(trial, 1, 0), 0.0)
    rest = jnp.concatenate([trial, before], axis=1)
    pieces = []
    for _ in range(3):
        pieces.append(rest.astype(jnp.bfloat16))
        rest = rest - pieces[-1].astype(jnp.float32)
    sums = jnp.dot(jnp.concatenate(pieces, axis=0), bands[...], preferred_element_type=jnp.float32)
    sums = sums[:rows] + (sums[rows : 2 * rows] + sums[2 * rows :])
    copies = []
    for t in range(trials):
        for n in range(scale.shape[0]):
            y[t, :, n, :] = sums[t * SPAN : (t + 1) * SPAN, n * LANES : (n + 1) * LANES] * scale[n : n + 1]
        copies.append(pltpu.make_async_copy(y.at[t], out.at[t], sems.at[t]))
        copies[-1].start()
    for c in copies:
        c.wait()


def boxcars(a, b, bands, scale, mask):
    trials, nw = a.shape[0], scale.shape[0]
    shape = (trials, SPAN, nw, LANES)
    out = pl.pallas_call(
        boxcar_kernel,
        out_shape=jax.ShapeDtypeStruct(shape, jnp.float32),
        in_specs=[IN_VMEM] * 5,
        out_specs=pl.BlockSpec(memory_space=pl.ANY),
        scratch_shapes=[pltpu.VMEM(shape, jnp.float32), pltpu.SemaphoreType.DMA((trials,))],
        cost_estimate=cost(0, 1 << 20),
    )(*[in_vmem(v) for v in (a, b, bands, scale, mask)])
    return out.transpose(0, 2, 1, 3).reshape(trials, nw, SPAN * LANES)


def on_device(spectra, delays, spans, widths):
    group = lax.axis_size("trials")
    channels = CH_SUB * group
    trials = delays.shape[0]
    masks = (0, 2, 4, 6)
    far_bits = [b for b in (8, 16, 32, 64, 128, 256) if b < group]

    raw, rows = raw_series(spectra, delays)
    raws = [raw] + [swap(raw, m, group) for m in masks[1:]]
    owned = pack_delays(rows, swap(delays, 1, group))
    near = to_scalars(owned)
    for b in far_bits:
        owned = jnp.concatenate([owned, swap(owned, b, group)])[2 if b == far_bits[-1] else 0 :]
    boxes = tables(widths, spans, channels)

    keep, send, mean = near_sums(raws, masks, near, trials, group)
    keep, send = far_sums(raws, masks, mean, keep, send, owned, group)
    theirs = swap(send, 1, group)
    for b in reversed(far_bits):
        sums = keep + theirs
        half = sums.shape[0] // 2
        keep, theirs = sums[:half], swap(sums[half:], b, group)
    return boxcars(keep[0], theirs[0], *boxes)


def solution(mesh):
    in_specs = (P(("beams", "trials"), None), P("trials", None), P(), P())
    out_specs = P(("beams", "trials"), None, None)
    return jax.shard_map(
        on_device, mesh=mesh, in_specs=in_specs, out_specs=out_specs, check_vma=False
    )
```

time: 106 us -> 20.3 us (0.19)
  blocking collectives: 61.9 us -> 0 us
  local copies, waits for them, and re-layouts: 18.9 us -> 0.01 us
  Pallas kernels: 0 us -> 5.61 us
  waiting for transfers between devices: 8.69 us -> 3.79 us
  other arithmetic: 3.51 us -> 0.01 us
    psum x1 -> x0, blocking collectives: 61.9 us -> none  [on_device(): channel_mean = lax.psum(local_sums, 'trials') / channels]
    gather x41 -> x0, local copies, waits for them, and re-layouts: 15.5 us -> none
    all_to_all x2 -> x0, starting transfers between devices: 10.9 us -> none  [the longest x1 7.39 us: on_device(): lax.all_to_all(delays, 'trials', split_axis=1, concat_axis=0, tiled=True)]
    ppermute x0 -> x7, starting transfers between devices: none -> 10.6 us  [swap(): return lax.ppermute(x, 'trials', [(i, i ^ bit) for i in range(group)])]
    all_to_all x2 -> x0, waiting for transfers between devices: 8.69 us -> none  [the longest x1 8.69 us: on_device(): lax.all_to_all(window, 'trials', split_axis=0, concat_axis=0, tiled=True)]
    pallas_call x0 -> x7, Pallas kernels: none -> 5.61 us  [the longest x1 1.92 us: raw_series(): pl.pallas_call(functools.partial(raw_kernel, chunks), out_shape=(VMEM((SU...]
    ppermute x0 -> x7, waiting for transfers between devices: none -> 3.79 us  [swap(): return lax.ppermute(x, 'trials', [(i, i ^ bit) for i in range(group)])]
    div x3 -> x0, other arithmetic: 1.76 us -> none  [the longest x1 1.01 us: subband_series(): return time_series / jnp.sqrt(jnp.float32(channels))]
  transfers between devices with their start and end apart: 2 -> 7, of which waited for: 1 -> 4; matrix products, arithmetic and copies ran while one was open for 3% -> 0% of each run, Pallas kernels for 0% -> 9%
where the time goes in v2:
time: 20.3 us; the launch traced here: 20.1 us
  starting transfers between devices  10.6 us (52%)
  Pallas kernels  5.61 us (28%)
  waiting for transfers between devices  3.79 us (19%)
    ppermute x7, starting transfers between devices, swap(): return lax.ppermute(x, 'trials', [(i, i ^ bit) for i in range(group)])  10.6 us
    ppermute x7, waiting for transfers between devices, swap(): return lax.ppermute(x, 'trials', [(i, i ^ bit) for i in range(group)])  3.79 us
    pallas_call x1, Pallas kernels, raw_series(): pl.pallas_call(functools.partial(raw_kernel, chunks), out_shape=(VMEM((SU...  1.92 us
    pallas_call x1, Pallas kernels, boxcars(): pl.pallas_call(boxcar_kernel, out_shape=jax.ShapeDtypeStruct(shape, jnp.f...  0.94 us
    pallas_call x1, Pallas kernels, far_sums(): pl.pallas_call(functools.partial(far_kernel, masks, trials, group), out_s...  0.86 us
    pallas_call x1, Pallas kernels, tables(): pl.pallas_call(functools.partial(tables_kernel, channels), out_shape=(VME...  0.84 us
    pallas_call x1, Pallas kernels, to_scalars(): pl.pallas_call(scalars_kernel, out_shape=SMEM(x.shape, x.dtype), in_specs...  0.67 us
  transfers between devices with their start and end apart: 7, of which 4 were waited for; matrix products, arithmetic and copies ran while one was open for 0% of the time, Pallas kernels for 9%

profile of v2, /device:TPU:0, one launch (start us, length us, event | category | flops | bytes accessed | tf_op | source)
XLA Modules:
  0.0 20.1 jit_solution(9264715560723769343)
XLA Ops:
  0.0 0.0 copy-start
  0.0 1.9 %shard_map.46 = (f32[2,64,128]{2,1,0:T(8,128)S(1)}, s32[8,128]{1,0:T(8,128)S(1)}) custom-call(bf16[128,8192]{1,0:T(8,128)(2,1)} %x_hbm.1, s32[4,16]{1,0:T(4,128)} %delays_hbm.1), custom_call_target="tpu_custom_call" | custom-call | flops 33554432 | bytes 2097152 | tf_op jit(solution)/shard_map/pallas_call | solution.py:100
  1.9 4.0 %collective-permute-start.2 = (f32[2,64,128]{2,1,0:T(8,128)S(1)}, f32[2,64,128]{2,1,0:T(8,128)S(1)}, u32[]{:S(2)}, u32[]{:S(2)}) collective-permute-start(f32[2,64,128]{2,1,0:T(8,128)S(1)} %get-tuple-element.15.refs_0_), channel_id=1, source_target_pairs={{0,6},{1,7},{2,4},{3,5},{4,2},{5,3},{6,0},{7,1},{8,14},{9,15},{10,... | collective-permute-start | bytes 196616 | tf_op jit(solution)/shard_map/ppermute | solution.py:35
  6.0 0.4 %collective-permute-start.1 = (f32[2,64,128]{2,1,0:T(8,128)S(1)}, f32[2,64,128]{2,1,0:T(8,128)S(1)}, u32[]{:S(2)}, u32[]{:S(2)}) collective-permute-start(f32[2,64,128]{2,1,0:T(8,128)S(1)} %get-tuple-element.15.refs_0_), channel_id=1, source_target_pairs={{0,4},{1,5},{2,6},{3,7},{4,0},{5,1},{6,2},{7,3},{8,12},{9,13},{10,... | collective-permute-start | bytes 196616 | tf_op jit(solution)/shard_map/ppermute | solution.py:35
  6.4 0.2 collective-permute-start
  6.6 0.0 copy-done
  6.6 0.0 collective-permute-start.3
  6.6 1.2 %collective-permute-done.3.theirs = s32[4,16]{1,0:T(4,128)S(1)} collective-permute-done((s32[4,16]{1,0:T(4,128)S(1)}, s32[4,16]{1,0:T(4,128)S(1)}, u32[]{:S(2)}, u32[]{:S(2)}) %collective-permute-start.3) | collective-permute-done | bytes 288 | tf_op jit(solution)/shard_map/ppermute | solution.py:35
  7.8 2.9 %collective-permute-start.4 = (s32[2,8,128]{2,1,0:T(8,128)S(1)}, s32[2,8,128]{2,1,0:T(8,128)S(1)}, u32[]{:S(2)}, u32[]{:S(2)}) collective-permute-start(s32[2,8,128]{2,1,0:T(8,128)S(1)} %shard_map.47.x), channel_id=1, source_target_pairs={{0,8},{1,9},{2,10},{3,11},{4,12},{5,13},{6,14},{7,15},{8,0},{9,1},... | collective-permute-start | bytes 24584 | tf_op jit(solution)/shard_map/ppermute | solution.py:35
  10.7 0.7 %shard_map.48.refs_4_ = s32[2,8,128]{2,1,0:T(8,128)S(4)} custom-call(s32[2,8,128]{2,1,0:T(8,128)S(1)} %shard_map.47.x), custom_call_target="tpu_custom_call" | custom-call | bytes 1048576 | tf_op jit(solution)/shard_map/pallas_call | solution.py:140
  11.4 0.0 collective-permute-done.2.refs_3_
  11.4 0.0 collective-permute-done.1.refs_2_
  11.4 0.0 collective-permute-done.refs_1_
  11.4 0.4 %shard_map.49 = (f32[1,4,8,128]{3,2,1,0:T(8,128)S(1)}, f32[1,4,8,128]{3,2,1,0:T(8,128)S(1)}, f32[2,64,128]{2,1,0:T(8,128)S(1)}) custom-call(f32[2,64,128]{2,1,0:T(8,128)S(1)} %get-tuple-element.15.refs_0_, f32[2,64,128]{2,1,0:T(8,128)S(1)} %collective-permute-done.refs_1_, f32[2,64,128]{2,1,0:T(8,128)S(1)} %collective-permute-done.1.refs_2_, ...), custom_call_target="tpu_custom_call" | custom-call | bytes 1048576 | tf_op jit(solution)/shard_map/pallas_call | solution.py:215
  11.8 0.5 %collective-permute-done.4.refs_7_ = s32[2,8,128]{2,1,0:T(8,128)S(1)} collective-permute-done((s32[2,8,128]{2,1,0:T(8,128)S(1)}, s32[2,8,128]{2,1,0:T(8,128)S(1)}, u32[]{:S(2)}, u32[]{:S(2)}) %collective-permute-start.4) | collective-permute-done | bytes 8224 | tf_op jit(solution)/shard_map/ppermute | solution.py:35
  12.3 0.9 %shard_map.50 = (f32[2,4,8,128]{3,2,1,0:T(8,128)S(1)}, f32[2,4,8,128]{3,2,1,0:T(8,128)S(1)}) custom-call(f32[2,64,128]{2,1,0:T(8,128)S(1)} %get-tuple-element.15.refs_0_, f32[2,64,128]{2,1,0:T(8,128)S(1)} %collective-permute-done.refs_1_, f32[2,64,128]{2,1,0:T(8,128)S(1)} %collective-permute-done.1.refs_2_, ...), custom_call_target="tpu_custom_call" | custom-call | bytes 1048576 | tf_op jit(solution)/shard_map/pallas_call | solution.py:248
  13.2 0.1 collective-permute-start.5
  13.3 1.2 %collective-permute-done.5 = f32[2,4,8,128]{3,2,1,0:T(8,128)S(1)} collective-permute-done((f32[2,4,8,128]{3,2,1,0:T(8,128)S(1)}, f32[2,4,8,128]{3,2,1,0:T(8,128)S(1)}, u32[]{:S(2)}, u32[]{:S(2)}) %collective-permute-start.5) | collective-permute-done | bytes 32800 | tf_op jit(solution)/shard_map/ppermute | solution.py:35
  14.5 3.0 %collective-permute-start.6 = (f32[1,4,8,128]{3,2,1,0:T(8,128)S(1)}, f32[1,4,8,128]{3,2,1,0:T(8,128)S(1)}, u32[]{:S(2)}, u32[]{:S(2)}) collective-permute-start(f32[1,4,8,128]{3,2,1,0:T(8,128)S(1)} %get-tuple-element.25), channel_id=1, source_target_pairs={{0,8},{1,9},{2,10},{3,11},{4,12},{5,13},{6,14},{7,15},{8,0},{9,1},... | collective-permute-start | bytes 49160 | tf_op jit(solution)/shard_map/ppermute | solution.py:35
  17.5 0.8 %shard_map.51 = (bf16[256,1024]{1,0:T(8,128)(2,1)S(1)}, f32[8,128]{1,0:T(8,128)S(1)}, f32[8,128]{1,0:T(8,128)S(1)}) custom-call(s32[8]{0:T(128)} %widths.1, s32[16]{0:T(128)} %spans.1), custom_call_target="tpu_custom_call" | custom-call | bytes 1048576 | tf_op jit(solution)/shard_map/pallas_call | solution.py:164
  18.3 0.9 %collective-permute-done.6 = f32[1,4,8,128]{3,2,1,0:T(8,128)S(1)} collective-permute-done((f32[1,4,8,128]{3,2,1,0:T(8,128)S(1)}, f32[1,4,8,128]{3,2,1,0:T(8,128)S(1)}, u32[]{:S(2)}, u32[]{:S(2)}) %collective-permute-start.6) | collective-permute-done | bytes 16416 | tf_op jit(solution)/shard_map/ppermute | solution.py:35
  19.2 0.9 %shard_map.52 = f32[4,8,8,128]{3,2,1,0:T(8,128)} custom-call(f32[4,8,128]{2,1,0:T(8,128)S(1)} %get-tuple-element.26.a, f32[4,8,128]{2,1,0:T(8,128)S(1)} %bitcast.6, bf16[256,1024]{1,0:T(8,128)(2,1)S(1)} %get-tuple-element.22.bands, f32[8,128]{1,0:T(8,128)S(1)} %get-tuple-element.23.scale, f32[8,128]{1,0:T(8,128)S(1)} %get-tuple-element.24.mask), custom_call_target="tpu_custom_call" | custom-call | bytes 1048576 | tf_op jit(solution)/shard_map/pallas_call | solution.py:284
  (3 shorter events, 0.0 us)
Async XLA Ops:
  0.0 6.6 %copy-start = (s32[4,16]{1,0:T(4,128)S(1)}, s32[4,16]{1,0:T(4,128)}, u32[]{:S(2)}) copy-start(s32[4,16]{1,0:T(4,128)} %delays_hbm.1) | copy-start | bytes 772
  1.9 9.4 %collective-permute-start.2 = (f32[2,64,128]{2,1,0:T(8,128)S(1)}, f32[2,64,128]{2,1,0:T(8,128)S(1)}, u32[]{:S(2)}, u32[]{:S(2)}) collective-permute-start(f32[2,64,128]{2,1,0:T(8,128)S(1)} %get-tuple-element.15.refs_0_), channel_id=1, source_target_pairs={{0,6},{1,7},{2,4},{3,5},{4,2},{5,3},{6,0},{7,1},{8,14},{9,15},{10,... | collective-permute-start | bytes 196616 | tf_op jit(solution)/shard_map/ppermute | solution.py:35
  6.0 5.4 %collective-permute-start.1 = (f32[2,64,128]{2,1,0:T(8,128)S(1)}, f32[2,64,128]{2,1,0:T(8,128)S(1)}, u32[]{:S(2)}, u32[]{:S(2)}) collective-permute-start(f32[2,64,128]{2,1,0:T(8,128)S(1)} %get-tuple-element.15.refs_0_), channel_id=1, source_target_pairs={{0,4},{1,5},{2,6},{3,7},{4,0},{5,1},{6,2},{7,3},{8,12},{9,13},{10,... | collective-permute-start | bytes 196616 | tf_op jit(solution)/shard_map/ppermute | solution.py:35
  6.4 5.0 %collective-permute-start = (f32[2,64,128]{2,1,0:T(8,128)S(1)}, f32[2,64,128]{2,1,0:T(8,128)S(1)}, u32[]{:S(2)}, u32[]{:S(2)}) collective-permute-start(f32[2,64,128]{2,1,0:T(8,128)S(1)} %get-tuple-element.15.refs_0_), channel_id=1, source_target_pairs={{0,2},{1,3},{2,0},{3,1},{4,6},{5,7},{6,4},{7,5},{8,10},{9,11},{10,... | collective-permute-start | bytes 196616 | tf_op jit(solution)/shard_map/ppermute | solution.py:35
  6.6 1.2 %collective-permute-start.3 = (s32[4,16]{1,0:T(4,128)S(1)}, s32[4,16]{1,0:T(4,128)S(1)}, u32[]{:S(2)}, u32[]{:S(2)}) collective-permute-start(s32[4,16]{1,0:T(4,128)S(1)} %copy-done), channel_id=1, source_target_pairs={{0,1},{1,0},{2,3},{3,2},{4,5},{5,4},{6,7},{7,6},{8,9},{9,8},{10,11... | collective-permute-start | bytes 776 | tf_op jit(solution)/shard_map/ppermute | solution.py:35
  7.8 4.5 %collective-permute-start.4 = (s32[2,8,128]{2,1,0:T(8,128)S(1)}, s32[2,8,128]{2,1,0:T(8,128)S(1)}, u32[]{:S(2)}, u32[]{:S(2)}) collective-permute-start(s32[2,8,128]{2,1,0:T(8,128)S(1)} %shard_map.47.x), channel_id=1, source_target_pairs={{0,8},{1,9},{2,10},{3,11},{4,12},{5,13},{6,14},{7,15},{8,0},{9,1},... | collective-permute-start | bytes 24584 | tf_op jit(solution)/shard_map/ppermute | solution.py:35
  13.2 1.3 %collective-permute-start.5 = (f32[2,4,8,128]{3,2,1,0:T(8,128)S(1)}, f32[2,4,8,128]{3,2,1,0:T(8,128)S(1)}, u32[]{:S(2)}, u32[]{:S(2)}) collective-permute-start(f32[2,4,8,128]{3,2,1,0:T(8,128)S(1)} %get-tuple-element.21), channel_id=1, source_target_pairs={{0,1},{1,0},{2,3},{3,2},{4,5},{5,4},{6,7},{7,6},{8,9},{9,8},{10,11... | collective-permute-start | bytes 98312 | tf_op jit(solution)/shard_map/ppermute | solution.py:35
  14.5 4.7 %collective-permute-start.6 = (f32[1,4,8,128]{3,2,1,0:T(8,128)S(1)}, f32[1,4,8,128]{3,2,1,0:T(8,128)S(1)}, u32[]{:S(2)}, u32[]{:S(2)}) collective-permute-start(f32[1,4,8,128]{3,2,1,0:T(8,128)S(1)} %get-tuple-element.25), channel_id=1, source_target_pairs={{0,8},{1,9},{2,10},{3,11},{4,12},{5,13},{6,14},{7,15},{8,0},{9,1},... | collective-permute-start | bytes 49160 | tf_op jit(solution)/shard_map/ppermute | solution.py:35

commit v3 on v2

--- a/solution.py
+++ b/solution.py
@@ -224,13 +224,20 @@
 def far_kernel(masks, trials, group, *refs):
     known = len(masks)
     raw, (mean, keep_near, send_near, far_in, keep, send, far, sem) = refs[:known], refs[known:]
-    copy = pltpu.make_async_copy(far_in, far, sem)
-    copy.start()
     core = lax.axis_index("trials") & 1
     chips = far.shape[0] // 2
+    if chips == 1:
+        for row in range(2):
+            tile = far_in[row]
+            for i in range(trials):
+                for s in range(group):
+                    far[row, i, s] = tile[i, s]
+    else:
+        copy = pltpu.make_async_copy(far_in, far, sem)
+        copy.start()
+        copy.wait()
     keep[:1] = keep_near[...]
     send[:1] = send_near[...]
-    copy.wait()
 
     def chip(e):
         windows(send, e + 1, raw, masks, mean, far, 2 * e + 1 - core, trials, group)
@@ -300,8 +307,9 @@
     far_bits = [b for b in (8, 16, 32, 64, 128, 256) if b < group]
 
     raw, rows = raw_series(spectra, delays)
+    raw, theirs = lax.optimization_barrier((raw, swap(delays, 1, group)))
     raws = [raw] + [swap(raw, m, group) for m in masks[1:]]
-    owned = pack_delays(rows, swap(delays, 1, group))
+    owned = pack_delays(rows, theirs)
     near = to_scalars(owned)
     for b in far_bits:
         owned = jnp.concatenate([owned, swap(owned, b, group)])[2 if b == far_bits[-1] else 0 :]

time: 20.3 us -> 18.7 us (0.921)
  waiting for transfers between devices: 3.79 us -> 2.66 us
  Pallas kernels: 5.61 us -> 5.19 us
    ppermute x7, waiting for transfers between devices: 3.79 us -> 2.66 us  [swap(): return lax.ppermute(x, 'trials', [(i, i ^ bit) for i in range(group)])]
    pallas_call x1, Pallas kernels: 0.86 us -> 0.44 us  [far_sums(): pl.pallas_call(functools.partial(far_kernel, masks, trials, group), out_s...]
  transfers between devices with their start and end apart: 7 -> 7, of which waited for: 4 -> 5; matrix products, arithmetic and copies ran while one was open for 0% -> 0% of each run, Pallas kernels for 9% -> 20%
where the time goes in v3:
time: 18.7 us; the launch traced here: 18.6 us
  starting transfers between devices  10.6 us (57%)
  Pallas kernels  5.19 us (28%)
  waiting for transfers between devices  2.66 us (14%)
    ppermute x7, starting transfers between devices, swap(): return lax.ppermute(x, 'trials', [(i, i ^ bit) for i in range(group)])  10.6 us
    ppermute x7, waiting for transfers between devices, swap(): return lax.ppermute(x, 'trials', [(i, i ^ bit) for i in range(group)])  2.66 us
    pallas_call x1, Pallas kernels, raw_series(): pl.pallas_call(functools.partial(raw_kernel, chunks), out_shape=(VMEM((SU...  1.91 us
    pallas_call x1, Pallas kernels, boxcars(): pl.pallas_call(boxcar_kernel, out_shape=jax.ShapeDtypeStruct(shape, jnp.f...  0.95 us
    pallas_call x1, Pallas kernels, tables(): pl.pallas_call(functools.partial(tables_kernel, channels), out_shape=(VME...  0.84 us
    pallas_call x1, Pallas kernels, to_scalars(): pl.pallas_call(scalars_kernel, out_shape=SMEM(x.shape, x.dtype), in_specs...  0.67 us
    pallas_call x1, Pallas kernels, far_sums(): pl.pallas_call(functools.partial(far_kernel, masks, trials, group), out_s...  0.44 us
    pallas_call x1, Pallas kernels, near_sums(): pl.pallas_call(functools.partial(near_kernel, masks, trials, group, CH_SU...  0.38 us
  transfers between devices with their start and end apart: 7, of which 5 were waited for; matrix products, arithmetic and copies ran while one was open for 0% of the time, Pallas kernels for 20%

profile of v3, /device:TPU:0, one launch (start us, length us, event | category | flops | bytes accessed | tf_op | source)
XLA Modules:
  0.0 18.6 jit_solution(12050357725509271736)
XLA Ops:
  0.0 0.5 %collective-permute-start = (s32[4,16]{1,0:T(4,128)}, s32[4,16]{1,0:T(4,128)S(1)}, u32[]{:S(2)}, u32[]{:S(2)}) collective-permute-start(s32[4,16]{1,0:T(4,128)} %delays_hbm.1), channel_id=1, source_target_pairs={{0,1},{1,0},{2,3},{3,2},{4,5},{5,4},{6,7},{7,6},{8,9},{9,8},{10,11... | collective-permute-start | bytes 776 | tf_op jit(solution)/shard_map/ppermute | solution.py:35
  0.5 1.9 %shard_map.46 = (f32[2,64,128]{2,1,0:T(8,128)S(1)}, s32[8,128]{1,0:T(8,128)S(1)}) custom-call(bf16[128,8192]{1,0:T(8,128)(2,1)} %x_hbm.1, s32[4,16]{1,0:T(4,128)} %delays_hbm.1), custom_call_target="tpu_custom_call" | custom-call | flops 33554432 | bytes 2097152 | tf_op jit(solution)/shard_map/pallas_call | solution.py:100
  2.4 0.0 collective-permute-done.theirs
  2.4 3.6 %collective-permute-start.3 = (f32[2,64,128]{2,1,0:T(8,128)S(1)}, f32[2,64,128]{2,1,0:T(8,128)S(1)}, u32[]{:S(2)}, u32[]{:S(2)}) collective-permute-start(f32[2,64,128]{2,1,0:T(8,128)S(1)} %get-tuple-element.18.refs_0_), channel_id=1, source_target_pairs={{0,6},{1,7},{2,4},{3,5},{4,2},{5,3},{6,0},{7,1},{8,14},{9,15},{10,... | collective-permute-start | bytes 196616 | tf_op jit(solution)/shard_map/ppermute | solution.py:35
  6.0 0.4 %collective-permute-start.2 = (f32[2,64,128]{2,1,0:T(8,128)S(1)}, f32[2,64,128]{2,1,0:T(8,128)S(1)}, u32[]{:S(2)}, u32[]{:S(2)}) collective-permute-start(f32[2,64,128]{2,1,0:T(8,128)S(1)} %get-tuple-element.18.refs_0_), channel_id=1, source_target_pairs={{0,4},{1,5},{2,6},{3,7},{4,0},{5,1},{6,2},{7,3},{8,12},{9,13},{10,... | collective-permute-start | bytes 196616 | tf_op jit(solution)/shard_map/ppermute | solution.py:35
  6.4 0.2 %collective-permute-start.1 = (f32[2,64,128]{2,1,0:T(8,128)S(1)}, f32[2,64,128]{2,1,0:T(8,128)S(1)}, u32[]{:S(2)}, u32[]{:S(2)}) collective-permute-start(f32[2,64,128]{2,1,0:T(8,128)S(1)} %get-tuple-element.18.refs_0_), channel_id=1, source_target_pairs={{0,2},{1,3},{2,0},{3,1},{4,6},{5,7},{6,4},{7,5},{8,10},{9,11},{10,... | collective-permute-start | bytes 196616 | tf_op jit(solution)/shard_map/ppermute | solution.py:35
  6.6 2.9 %collective-permute-start.4 = (s32[2,8,128]{2,1,0:T(8,128)S(1)}, s32[2,8,128]{2,1,0:T(8,128)S(1)}, u32[]{:S(2)}, u32[]{:S(2)}) collective-permute-start(s32[2,8,128]{2,1,0:T(8,128)S(1)} %shard_map.47.x), channel_id=1, source_target_pairs={{0,8},{1,9},{2,10},{3,11},{4,12},{5,13},{6,14},{7,15},{8,0},{9,1},... | collective-permute-start | bytes 24584 | tf_op jit(solution)/shard_map/ppermute | solution.py:35
  9.5 0.7 %shard_map.48.refs_4_ = s32[2,8,128]{2,1,0:T(8,128)S(4)} custom-call(s32[2,8,128]{2,1,0:T(8,128)S(1)} %shard_map.47.x), custom_call_target="tpu_custom_call" | custom-call | bytes 1048576 | tf_op jit(solution)/shard_map/pallas_call | solution.py:140
  10.2 0.0 collective-permute-done.3.refs_3_
  10.2 0.2 collective-permute-done.2.refs_2_
  10.4 0.3 %collective-permute-done.1.refs_1_ = f32[2,64,128]{2,1,0:T(8,128)S(1)} collective-permute-done((f32[2,64,128]{2,1,0:T(8,128)S(1)}, f32[2,64,128]{2,1,0:T(8,128)S(1)}, u32[]{:S(2)}, u32[]{:S(2)}) %collective-permute-start.1) | collective-permute-done | bytes 65568 | tf_op jit(solution)/shard_map/ppermute | solution.py:35
  10.7 0.4 %shard_map.49 = (f32[1,4,8,128]{3,2,1,0:T(8,128)S(1)}, f32[1,4,8,128]{3,2,1,0:T(8,128)S(1)}, f32[2,64,128]{2,1,0:T(8,128)S(1)}) custom-call(f32[2,64,128]{2,1,0:T(8,128)S(1)} %get-tuple-element.18.refs_0_, f32[2,64,128]{2,1,0:T(8,128)S(1)} %collective-permute-done.1.refs_1_, f32[2,64,128]{2,1,0:T(8,128)S(1)} %collective-permute-done.2.refs_2_, ...), custom_call_target="tpu_custom_call" | custom-call | bytes 1048576 | tf_op jit(solution)/shard_map/pallas_call | solution.py:215
  11.1 0.1 collective-permute-done.4.refs_7_
  11.2 0.4 %shard_map.50 = (f32[2,4,8,128]{3,2,1,0:T(8,128)S(1)}, f32[2,4,8,128]{3,2,1,0:T(8,128)S(1)}) custom-call(f32[2,64,128]{2,1,0:T(8,128)S(1)} %get-tuple-element.18.refs_0_, f32[2,64,128]{2,1,0:T(8,128)S(1)} %collective-permute-done.1.refs_1_, f32[2,64,128]{2,1,0:T(8,128)S(1)} %collective-permute-done.2.refs_2_, ...), custom_call_target="tpu_custom_call" | custom-call | bytes 1048576 | tf_op jit(solution)/shard_map/pallas_call | solution.py:255
  11.6 0.1 collective-permute-start.5
  11.7 1.2 %collective-permute-done.5 = f32[2,4,8,128]{3,2,1,0:T(8,128)S(1)} collective-permute-done((f32[2,4,8,128]{3,2,1,0:T(8,128)S(1)}, f32[2,4,8,128]{3,2,1,0:T(8,128)S(1)}, u32[]{:S(2)}, u32[]{:S(2)}) %collective-permute-start.5) | collective-permute-done | bytes 32800 | tf_op jit(solution)/shard_map/ppermute | solution.py:35
  12.9 3.0 %collective-permute-start.6 = (f32[1,4,8,128]{3,2,1,0:T(8,128)S(1)}, f32[1,4,8,128]{3,2,1,0:T(8,128)S(1)}, u32[]{:S(2)}, u32[]{:S(2)}) collective-permute-start(f32[1,4,8,128]{3,2,1,0:T(8,128)S(1)} %get-tuple-element.29), channel_id=1, source_target_pairs={{0,8},{1,9},{2,10},{3,11},{4,12},{5,13},{6,14},{7,15},{8,0},{9,1},... | collective-permute-start | bytes 49160 | tf_op jit(solution)/shard_map/ppermute | solution.py:35
  15.9 0.8 %shard_map.51 = (bf16[256,1024]{1,0:T(8,128)(2,1)S(1)}, f32[8,128]{1,0:T(8,128)S(1)}, f32[8,128]{1,0:T(8,128)S(1)}) custom-call(s32[8]{0:T(128)} %widths.1, s32[16]{0:T(128)} %spans.1), custom_call_target="tpu_custom_call" | custom-call | bytes 1048576 | tf_op jit(solution)/shard_map/pallas_call | solution.py:164
  16.7 0.9 %collective-permute-done.6 = f32[1,4,8,128]{3,2,1,0:T(8,128)S(1)} collective-permute-done((f32[1,4,8,128]{3,2,1,0:T(8,128)S(1)}, f32[1,4,8,128]{3,2,1,0:T(8,128)S(1)}, u32[]{:S(2)}, u32[]{:S(2)}) %collective-permute-start.6) | collective-permute-done | bytes 16416 | tf_op jit(solution)/shard_map/ppermute | solution.py:35
  17.6 0.9 %shard_map.52 = f32[4,8,8,128]{3,2,1,0:T(8,128)} custom-call(f32[4,8,128]{2,1,0:T(8,128)S(1)} %get-tuple-element.30.a, f32[4,8,128]{2,1,0:T(8,128)S(1)} %bitcast.6, bf16[256,1024]{1,0:T(8,128)(2,1)S(1)} %get-tuple-element.26.bands, f32[8,128]{1,0:T(8,128)S(1)} %get-tuple-element.27.scale, f32[8,128]{1,0:T(8,128)S(1)} %get-tuple-element.28.mask), custom_call_target="tpu_custom_call" | custom-call | bytes 1048576 | tf_op jit(solution)/shard_map/pallas_call | solution.py:291
  (3 shorter events, 0.0 us)
Async XLA Ops:
  0.0 2.4 %collective-permute-start = (s32[4,16]{1,0:T(4,128)}, s32[4,16]{1,0:T(4,128)S(1)}, u32[]{:S(2)}, u32[]{:S(2)}) collective-permute-start(s32[4,16]{1,0:T(4,128)} %delays_hbm.1), channel_id=1, source_target_pairs={{0,1},{1,0},{2,3},{3,2},{4,5},{5,4},{6,7},{7,6},{8,9},{9,8},{10,11... | collective-permute-start | bytes 776 | tf_op jit(solution)/shard_map/ppermute | solution.py:35
  2.4 7.8 %collective-permute-start.3 = (f32[2,64,128]{2,1,0:T(8,128)S(1)}, f32[2,64,128]{2,1,0:T(8,128)S(1)}, u32[]{:S(2)}, u32[]{:S(2)}) collective-permute-start(f32[2,64,128]{2,1,0:T(8,128)S(1)} %get-tuple-element.18.refs_0_), channel_id=1, source_target_pairs={{0,6},{1,7},{2,4},{3,5},{4,2},{5,3},{6,0},{7,1},{8,14},{9,15},{10,... | collective-permute-start | bytes 196616 | tf_op jit(solution)/shard_map/ppermute | solution.py:35
  6.0 4.4 %collective-permute-start.2 = (f32[2,64,128]{2,1,0:T(8,128)S(1)}, f32[2,64,128]{2,1,0:T(8,128)S(1)}, u32[]{:S(2)}, u32[]{:S(2)}) collective-permute-start(f32[2,64,128]{2,1,0:T(8,128)S(1)} %get-tuple-element.18.refs_0_), channel_id=1, source_target_pairs={{0,4},{1,5},{2,6},{3,7},{4,0},{5,1},{6,2},{7,3},{8,12},{9,13},{10,... | collective-permute-start | bytes 196616 | tf_op jit(solution)/shard_map/ppermute | solution.py:35
  6.4 4.3 %collective-permute-start.1 = (f32[2,64,128]{2,1,0:T(8,128)S(1)}, f32[2,64,128]{2,1,0:T(8,128)S(1)}, u32[]{:S(2)}, u32[]{:S(2)}) collective-permute-start(f32[2,64,128]{2,1,0:T(8,128)S(1)} %get-tuple-element.18.refs_0_), channel_id=1, source_target_pairs={{0,2},{1,3},{2,0},{3,1},{4,6},{5,7},{6,4},{7,5},{8,10},{9,11},{10,... | collective-permute-start | bytes 196616 | tf_op jit(solution)/shard_map/ppermute | solution.py:35
  6.6 4.5 %collective-permute-start.4 = (s32[2,8,128]{2,1,0:T(8,128)S(1)}, s32[2,8,128]{2,1,0:T(8,128)S(1)}, u32[]{:S(2)}, u32[]{:S(2)}) collective-permute-start(s32[2,8,128]{2,1,0:T(8,128)S(1)} %shard_map.47.x), channel_id=1, source_target_pairs={{0,8},{1,9},{2,10},{3,11},{4,12},{5,13},{6,14},{7,15},{8,0},{9,1},... | collective-permute-start | bytes 24584 | tf_op jit(solution)/shard_map/ppermute | solution.py:35
  11.6 1.3 %collective-permute-start.5 = (f32[2,4,8,128]{3,2,1,0:T(8,128)S(1)}, f32[2,4,8,128]{3,2,1,0:T(8,128)S(1)}, u32[]{:S(2)}, u32[]{:S(2)}) collective-permute-start(f32[2,4,8,128]{3,2,1,0:T(8,128)S(1)} %get-tuple-element.25), channel_id=1, source_target_pairs={{0,1},{1,0},{2,3},{3,2},{4,5},{5,4},{6,7},{7,6},{8,9},{9,8},{10,11... | collective-permute-start | bytes 98312 | tf_op jit(solution)/shard_map/ppermute | solution.py:35
  12.9 4.7 %collective-permute-start.6 = (f32[1,4,8,128]{3,2,1,0:T(8,128)S(1)}, f32[1,4,8,128]{3,2,1,0:T(8,128)S(1)}, u32[]{:S(2)}, u32[]{:S(2)}) collective-permute-start(f32[1,4,8,128]{3,2,1,0:T(8,128)S(1)} %get-tuple-element.29), channel_id=1, source_target_pairs={{0,8},{1,9},{2,10},{3,11},{4,12},{5,13},{6,14},{7,15},{8,0},{9,1},... | collective-permute-start | bytes 49160 | tf_op jit(solution)/shard_map/ppermute | solution.py:35

commit v4 on v3

--- a/solution.py
+++ b/solution.py
@@ -174,7 +174,7 @@
     )(widths, spans)
 
 
-def windows(out, e, raw, masks, mean, delays, row, trials, group):
+def windows(out, raw, masks, mean, delays, row, trials, group):
     me = lax.axis_index("trials")
     for i in range(trials):
         j = i % SUBT
@@ -191,7 +191,7 @@
             less = lax.fori_loop(
                 0, group, lambda s, v: v + mean[j, pl.ds(delays[row, i, s], SPAN), :], jnp.zeros_like(acc)
             )
-        out[e, i] = acc - less
+        out[i] = acc - less
 
 
 def near_kernel(masks, trials, group, channels, *refs):
@@ -206,12 +206,12 @@
         total = total + shifted(total, k)
     mean[1] = total
     core = lax.axis_index("trials") & 1
-    windows(keep, 0, raw, masks, mean, near, core, trials, group)
-    windows(send, 0, raw, masks, mean, near, 1 - core, trials, group)
+    windows(keep, raw, masks, mean, near, core, trials, group)
+    windows(send, raw, masks, mean, near, 1 - core, trials, group)
 
 
 def near_sums(raw, masks, near, trials, group):
-    one = VMEM((1, trials, SPAN, LANES), jnp.float32)
+    one = VMEM((trials, SPAN, LANES), jnp.float32)
     return pl.pallas_call(
         functools.partial(near_kernel, masks, trials, group, CH_SUB * group),
         out_shape=(one, one, VMEM(raw[0].shape, jnp.float32)),
@@ -221,45 +221,36 @@
     )(*[in_vmem(r) for r in raw], in_smem(near))
 
 
-def far_kernel(masks, trials, group, *refs):
+def far_kernel(masks, trials, group, other, *refs):
     known = len(masks)
-    raw, (mean, keep_near, send_near, far_in, keep, send, far, sem) = refs[:known], refs[known:]
-    core = lax.axis_index("trials") & 1
-    chips = far.shape[0] // 2
+    raw, (mean, far_in, out, far, sem) = refs[:known], refs[known:]
+    which = (lax.axis_index("trials") & 1) ^ other
+    chips = out.shape[0]
     if chips == 1:
-        for row in range(2):
-            tile = far_in[row]
-            for i in range(trials):
-                for s in range(group):
-                    far[row, i, s] = tile[i, s]
+        tile = far_in[which]
+        for i in range(trials):
+            for s in range(group):
+                far[0, i, s] = tile[i, s]
+        windows(out.at[0], raw, masks, mean, far, 0, trials, group)
     else:
         copy = pltpu.make_async_copy(far_in, far, sem)
         copy.start()
         copy.wait()
-    keep[:1] = keep_near[...]
-    send[:1] = send_near[...]
-
-    def chip(e):
-        windows(send, e + 1, raw, masks, mean, far, 2 * e + 1 - core, trials, group)
-        windows(keep, e + 1, raw, masks, mean, far, 2 * e + core, trials, group)
-
-    if chips == 1:
-        chip(0)
-    else:
-        pl.loop(0, chips)(chip)
-
-
-def far_sums(raw, masks, mean, keep, send, far, group):
-    trials = keep.shape[1]
-    half = VMEM((far.shape[0] // 2 + 1, trials, SPAN, LANES), jnp.float32)
-    return pl.pallas_call(
-        functools.partial(far_kernel, masks, trials, group),
-        out_shape=(half, half),
-        in_specs=[IN_VMEM] * (len(raw) + 4),
-        out_specs=(IN_VMEM,) * 2,
+
+        @pl.loop(0, chips)
+        def _(e):
+            windows(out.at[e], raw, masks, mean, far, 2 * e + which, trials, group)
+
+
+def far_sums(other, raw, masks, mean, far, trials, group):
+    return pl.pallas_call(
+        functools.partial(far_kernel, masks, trials, group, other),
+        out_shape=VMEM((far.shape[0] // 2, trials, SPAN, LANES), jnp.float32),
+        in_specs=[IN_VMEM] * (len(raw) + 2),
+        out_specs=IN_VMEM,
         scratch_shapes=[pltpu.SMEM(far.shape, jnp.int32), pltpu.SemaphoreType.DMA(())],
         cost_estimate=cost(0, 1 << 20),
-    )(*[in_vmem(v) for v in (*raw, mean, keep, send, far)])
+    )(*[in_vmem(v) for v in (*raw, mean, far)])
 
 
 def boxcar_kernel(a, b, bands, scale, mask, out, y, sems):
@@ -316,13 +307,15 @@
     boxes = tables(widths, spans, channels)
 
     keep, send, mean = near_sums(raws, masks, near, trials, group)
-    keep, send = far_sums(raws, masks, mean, keep, send, owned, group)
-    theirs = swap(send, 1, group)
+    here = keep + swap(send, 1, group)
+    far = swap(far_sums(1, raws, masks, mean, owned, trials, group), 1, group)
+    far = far + far_sums(0, raws, masks, mean, owned, trials, group)
+    sums = jnp.concatenate([here[None], far])
     for b in reversed(far_bits):
-        sums = keep + theirs
         half = sums.shape[0] // 2
-        keep, theirs = sums[:half], swap(sums[half:], b, group)
-    return boxcars(keep[0], theirs[0], *boxes)
+        mine, theirs = sums[:half], swap(sums[half:], b, group)
+        sums = mine + theirs
+    return boxcars(mine[0], theirs[0], *boxes)
 
 
 def solution(mesh):

time: 18.7 us -> 18.4 us (0.984)
  waiting for transfers between devices: 2.66 us -> 1.9 us
  starting transfers between devices: 10.6 us -> 11.1 us
    ppermute x7 -> x8, waiting for transfers between devices: 2.66 us -> 1.9 us  [swap(): return lax.ppermute(x, 'trials', [(i, i ^ bit) for i in range(group)])]
    ppermute x7 -> x8, starting transfers between devices: 10.6 us -> 11.1 us  [swap(): return lax.ppermute(x, 'trials', [(i, i ^ bit) for i in range(group)])]
    pallas_call x1 -> x2, Pallas kernels: 0.44 us -> 0.43 us  [far_sums(): pl.pallas_call(functools.partial(far_kernel, masks, trials, group, other)...]
  transfers between devices with their start and end apart: 7 -> 8, of which waited for: 5 -> 5; matrix products, arithmetic and copies ran while one was open for 0% -> 0% of each run, Pallas kernels for 20% -> 22%
where the time goes in v4:
time: 18.4 us; the launch traced here: 18.2 us
  starting transfers between devices  11.1 us (60%)
  Pallas kernels  5.17 us (28%)
  waiting for transfers between devices  1.9 us (10%)
    ppermute x8, starting transfers between devices, swap(): return lax.ppermute(x, 'trials', [(i, i ^ bit) for i in range(group)])  11.1 us
    pallas_call x1, Pallas kernels, raw_series(): pl.pallas_call(functools.partial(raw_kernel, chunks), out_shape=(VMEM((SU...  1.91 us
    ppermute x8, waiting for transfers between devices, swap(): return lax.ppermute(x, 'trials', [(i, i ^ bit) for i in range(group)])  1.9 us
    pallas_call x1, Pallas kernels, boxcars(): pl.pallas_call(boxcar_kernel, out_shape=jax.ShapeDtypeStruct(shape, jnp.f...  0.94 us
    pallas_call x1, Pallas kernels, tables(): pl.pallas_call(functools.partial(tables_kernel, channels), out_shape=(VME...  0.84 us
    pallas_call x1, Pallas kernels, to_scalars(): pl.pallas_call(scalars_kernel, out_shape=SMEM(x.shape, x.dtype), in_specs...  0.67 us
    pallas_call x2, Pallas kernels, far_sums(): pl.pallas_call(functools.partial(far_kernel, masks, trials, group, other)...  0.43 us
    pallas_call x1, Pallas kernels, near_sums(): pl.pallas_call(functools.partial(near_kernel, masks, trials, group, CH_SU...  0.38 us
  transfers between devices with their start and end apart: 8, of which 5 were waited for; matrix products, arithmetic and copies ran while one was open for 0% of the time, Pallas kernels for 22%

profile of v4, /device:TPU:0, one launch (start us, length us, event | category | flops | bytes accessed | tf_op | source)
XLA Modules:
  0.0 18.2 jit_solution(10762567016998830980)
XLA Ops:
  0.0 0.5 %collective-permute-start = (s32[4,16]{1,0:T(4,128)}, s32[4,16]{1,0:T(4,128)S(1)}, u32[]{:S(2)}, u32[]{:S(2)}) collective-permute-start(s32[4,16]{1,0:T(4,128)} %delays_hbm.1), channel_id=1, source_target_pairs={{0,1},{1,0},{2,3},{3,2},{4,5},{5,4},{6,7},{7,6},{8,9},{9,8},{10,11... | collective-permute-start | bytes 776 | tf_op jit(solution)/shard_map/ppermute | solution.py:35
  0.5 1.9 %shard_map.46 = (f32[2,64,128]{2,1,0:T(8,128)S(1)}, s32[8,128]{1,0:T(8,128)S(1)}) custom-call(bf16[128,8192]{1,0:T(8,128)(2,1)} %x_hbm.1, s32[4,16]{1,0:T(4,128)} %delays_hbm.1), custom_call_target="tpu_custom_call" | custom-call | flops 33554432 | bytes 2097152 | tf_op jit(solution)/shard_map/pallas_call | solution.py:100
  2.4 0.0 collective-permute-done.theirs
  2.4 3.6 %collective-permute-start.3 = (f32[2,64,128]{2,1,0:T(8,128)S(1)}, f32[2,64,128]{2,1,0:T(8,128)S(1)}, u32[]{:S(2)}, u32[]{:S(2)}) collective-permute-start(f32[2,64,128]{2,1,0:T(8,128)S(1)} %get-tuple-element.16.refs_0_), channel_id=1, source_target_pairs={{0,6},{1,7},{2,4},{3,5},{4,2},{5,3},{6,0},{7,1},{8,14},{9,15},{10,... | collective-permute-start | bytes 196616 | tf_op jit(solution)/shard_map/ppermute | solution.py:35
  6.0 0.4 %collective-permute-start.2 = (f32[2,64,128]{2,1,0:T(8,128)S(1)}, f32[2,64,128]{2,1,0:T(8,128)S(1)}, u32[]{:S(2)}, u32[]{:S(2)}) collective-permute-start(f32[2,64,128]{2,1,0:T(8,128)S(1)} %get-tuple-element.16.refs_0_), channel_id=1, source_target_pairs={{0,4},{1,5},{2,6},{3,7},{4,0},{5,1},{6,2},{7,3},{8,12},{9,13},{10,... | collective-permute-start | bytes 196616 | tf_op jit(solution)/shard_map/ppermute | solution.py:35
  6.4 0.2 %collective-permute-start.1 = (f32[2,64,128]{2,1,0:T(8,128)S(1)}, f32[2,64,128]{2,1,0:T(8,128)S(1)}, u32[]{:S(2)}, u32[]{:S(2)}) collective-permute-start(f32[2,64,128]{2,1,0:T(8,128)S(1)} %get-tuple-element.16.refs_0_), channel_id=1, source_target_pairs={{0,2},{1,3},{2,0},{3,1},{4,6},{5,7},{6,4},{7,5},{8,10},{9,11},{10,... | collective-permute-start | bytes 196616 | tf_op jit(solution)/shard_map/ppermute | solution.py:35
  6.6 2.9 %collective-permute-start.5 = (s32[2,8,128]{2,1,0:T(8,128)S(1)}, s32[2,8,128]{2,1,0:T(8,128)S(1)}, u32[]{:S(2)}, u32[]{:S(2)}) collective-permute-start(s32[2,8,128]{2,1,0:T(8,128)S(1)} %shard_map.47.x), channel_id=1, source_target_pairs={{0,8},{1,9},{2,10},{3,11},{4,12},{5,13},{6,14},{7,15},{8,0},{9,1},... | collective-permute-start | bytes 24584 | tf_op jit(solution)/shard_map/ppermute | solution.py:35
  9.5 0.7 %shard_map.48.refs_4_ = s32[2,8,128]{2,1,0:T(8,128)S(4)} custom-call(s32[2,8,128]{2,1,0:T(8,128)S(1)} %shard_map.47.x), custom_call_target="tpu_custom_call" | custom-call | bytes 1048576 | tf_op jit(solution)/shard_map/pallas_call | solution.py:140
  10.2 0.0 collective-permute-done.3.refs_3_
  10.2 0.2 collective-permute-done.2.refs_2_
  10.4 0.3 %collective-permute-done.1.refs_1_ = f32[2,64,128]{2,1,0:T(8,128)S(1)} collective-permute-done((f32[2,64,128]{2,1,0:T(8,128)S(1)}, f32[2,64,128]{2,1,0:T(8,128)S(1)}, u32[]{:S(2)}, u32[]{:S(2)}) %collective-permute-start.1) | collective-permute-done | bytes 65568 | tf_op jit(solution)/shard_map/ppermute | solution.py:35
  10.7 0.4 %shard_map.49 = (f32[4,8,128]{2,1,0:T(8,128)S(1)}, f32[4,8,128]{2,1,0:T(8,128)S(1)}, f32[2,64,128]{2,1,0:T(8,128)S(1)}) custom-call(f32[2,64,128]{2,1,0:T(8,128)S(1)} %get-tuple-element.16.refs_0_, f32[2,64,128]{2,1,0:T(8,128)S(1)} %collective-permute-done.1.refs_1_, f32[2,64,128]{2,1,0:T(8,128)S(1)} %collective-permute-done.2.refs_2_, ...), custom_call_target="tpu_custom_call" | custom-call | bytes 1048576 | tf_op jit(solution)/shard_map/pallas_call | solution.py:215
  11.1 0.1 collective-permute-done.5.refs_5_
  11.2 0.2 %shard_map.50 = f32[1,4,8,128]{3,2,1,0:T(8,128)S(1)} custom-call(f32[2,64,128]{2,1,0:T(8,128)S(1)} %get-tuple-element.16.refs_0_, f32[2,64,128]{2,1,0:T(8,128)S(1)} %collective-permute-done.1.refs_1_, f32[2,64,128]{2,1,0:T(8,128)S(1)} %collective-permute-done.2.refs_2_, f32[2,64,128]{2,1,0:T(8,128)S(1)} %collective-permute-done.3.refs_3_, ...), custom_call_target="tpu_custom_call" | custom-call | bytes 1048576 | tf_op jit(solution)/shard_map/pallas_call | solution.py:246
  11.4 0.1 collective-permute-start.6
  11.5 0.5 %collective-permute-start.4 = (f32[4,8,128]{2,1,0:T(8,128)S(1)}, f32[4,8,128]{2,1,0:T(8,128)S(1)}, u32[]{:S(2)}, u32[]{:S(2)}) collective-permute-start(f32[4,8,128]{2,1,0:T(8,128)S(1)} %get-tuple-element.20), channel_id=1, source_target_pairs={{0,1},{1,0},{2,3},{3,2},{4,5},{5,4},{6,7},{7,6},{8,9},{9,8},{10,11... | collective-permute-start | bytes 49160 | tf_op jit(solution)/shard_map/ppermute | solution.py:35
  12.0 0.2 %shard_map.51 = f32[1,4,8,128]{3,2,1,0:T(8,128)S(1)} custom-call(f32[2,64,128]{2,1,0:T(8,128)S(1)} %get-tuple-element.16.refs_0_, f32[2,64,128]{2,1,0:T(8,128)S(1)} %collective-permute-done.1.refs_1_, f32[2,64,128]{2,1,0:T(8,128)S(1)} %collective-permute-done.2.refs_2_, f32[2,64,128]{2,1,0:T(8,128)S(1)} %collective-permute-done.3.refs_3_, ...), custom_call_target="tpu_custom_call" | custom-call | bytes 1048576 | tf_op jit(solution)/shard_map/pallas_call | solution.py:246
  12.2 0.5 %collective-permute-done.6 = f32[1,4,8,128]{3,2,1,0:T(8,128)S(1)} collective-permute-done((f32[1,4,8,128]{3,2,1,0:T(8,128)S(1)}, f32[1,4,8,128]{3,2,1,0:T(8,128)S(1)}, u32[]{:S(2)}, u32[]{:S(2)}) %collective-permute-start.6) | collective-permute-done | bytes 16416 | tf_op jit(solution)/shard_map/ppermute | solution.py:35
  12.6 2.9 %collective-permute-start.7 = (f32[1,4,8,128]{3,2,1,0:T(8,128)S(1)}, f32[1,4,8,128]{3,2,1,0:T(8,128)S(1)}, u32[]{:S(2)}, u32[]{:S(2)}) collective-permute-start(f32[1,4,8,128]{3,2,1,0:T(8,128)S(1)} %add.7), channel_id=1, source_target_pairs={{0,8},{1,9},{2,10},{3,11},{4,12},{5,13},{6,14},{7,15},{8,0},{9,1},... | collective-permute-start | bytes 49160 | tf_op jit(solution)/shard_map/ppermute | solution.py:35
  15.6 0.8 %shard_map.52 = (bf16[256,1024]{1,0:T(8,128)(2,1)S(1)}, f32[8,128]{1,0:T(8,128)S(1)}, f32[8,128]{1,0:T(8,128)S(1)}) custom-call(s32[8]{0:T(128)} %widths.1, s32[16]{0:T(128)} %spans.1), custom_call_target="tpu_custom_call" | custom-call | bytes 1048576 | tf_op jit(solution)/shard_map/pallas_call | solution.py:164
  16.4 0.0 collective-permute-done.4
  16.4 0.9 %collective-permute-done.7 = f32[1,4,8,128]{3,2,1,0:T(8,128)S(1)} collective-permute-done((f32[1,4,8,128]{3,2,1,0:T(8,128)S(1)}, f32[1,4,8,128]{3,2,1,0:T(8,128)S(1)}, u32[]{:S(2)}, u32[]{:S(2)}) %collective-permute-start.7) | collective-permute-done | bytes 16416 | tf_op jit(solution)/shard_map/ppermute | solution.py:35
  17.3 0.9 %shard_map.53 = f32[4,8,8,128]{3,2,1,0:T(8,128)} custom-call(f32[4,8,128]{2,1,0:T(8,128)S(1)} %add.6.a, f32[4,8,128]{2,1,0:T(8,128)S(1)} %bitcast.4, bf16[256,1024]{1,0:T(8,128)(2,1)S(1)} %get-tuple-element.22.bands, f32[8,128]{1,0:T(8,128)S(1)} %get-tuple-element.23.scale, f32[8,128]{1,0:T(8,128)S(1)} %get-tuple-element.24.mask), custom_call_target="tpu_custom_call" | custom-call | bytes 1048576 | tf_op jit(solution)/shard_map/pallas_call | solution.py:282
  (3 shorter events, 0.0 us)
Async XLA Ops:
  0.0 2.4 %collective-permute-start = (s32[4,16]{1,0:T(4,128)}, s32[4,16]{1,0:T(4,128)S(1)}, u32[]{:S(2)}, u32[]{:S(2)}) collective-permute-start(s32[4,16]{1,0:T(4,128)} %delays_hbm.1), channel_id=1, source_target_pairs={{0,1},{1,0},{2,3},{3,2},{4,5},{5,4},{6,7},{7,6},{8,9},{9,8},{10,11... | collective-permute-start | bytes 776 | tf_op jit(solution)/shard_map/ppermute | solution.py:35
  2.4 7.8 %collective-permute-start.3 = (f32[2,64,128]{2,1,0:T(8,128)S(1)}, f32[2,64,128]{2,1,0:T(8,128)S(1)}, u32[]{:S(2)}, u32[]{:S(2)}) collective-permute-start(f32[2,64,128]{2,1,0:T(8,128)S(1)} %get-tuple-element.16.refs_0_), channel_id=1, source_target_pairs={{0,6},{1,7},{2,4},{3,5},{4,2},{5,3},{6,0},{7,1},{8,14},{9,15},{10,... | collective-permute-start | bytes 196616 | tf_op jit(solution)/shard_map/ppermute | solution.py:35
  6.0 4.4 %collective-permute-start.2 = (f32[2,64,128]{2,1,0:T(8,128)S(1)}, f32[2,64,128]{2,1,0:T(8,128)S(1)}, u32[]{:S(2)}, u32[]{:S(2)}) collective-permute-start(f32[2,64,128]{2,1,0:T(8,128)S(1)} %get-tuple-element.16.refs_0_), channel_id=1, source_target_pairs={{0,4},{1,5},{2,6},{3,7},{4,0},{5,1},{6,2},{7,3},{8,12},{9,13},{10,... | collective-permute-start | bytes 196616 | tf_op jit(solution)/shard_map/ppermute | solution.py:35
  6.4 4.3 %collective-permute-start.1 = (f32[2,64,128]{2,1,0:T(8,128)S(1)}, f32[2,64,128]{2,1,0:T(8,128)S(1)}, u32[]{:S(2)}, u32[]{:S(2)}) collective-permute-start(f32[2,64,128]{2,1,0:T(8,128)S(1)} %get-tuple-element.16.refs_0_), channel_id=1, source_target_pairs={{0,2},{1,3},{2,0},{3,1},{4,6},{5,7},{6,4},{7,5},{8,10},{9,11},{10,... | collective-permute-start | bytes 196616 | tf_op jit(solution)/shard_map/ppermute | solution.py:35
  6.6 4.5 %collective-permute-start.5 = (s32[2,8,128]{2,1,0:T(8,128)S(1)}, s32[2,8,128]{2,1,0:T(8,128)S(1)}, u32[]{:S(2)}, u32[]{:S(2)}) collective-permute-start(s32[2,8,128]{2,1,0:T(8,128)S(1)} %shard_map.47.x), channel_id=1, source_target_pairs={{0,8},{1,9},{2,10},{3,11},{4,12},{5,13},{6,14},{7,15},{8,0},{9,1},... | collective-permute-start | bytes 24584 | tf_op jit(solution)/shard_map/ppermute | solution.py:35
  11.4 1.2 %collective-permute-start.6 = (f32[1,4,8,128]{3,2,1,0:T(8,128)S(1)}, f32[1,4,8,128]{3,2,1,0:T(8,128)S(1)}, u32[]{:S(2)}, u32[]{:S(2)}) collective-permute-start(f32[1,4,8,128]{3,2,1,0:T(8,128)S(1)} %shard_map.50), channel_id=1, source_target_pairs={{0,1},{1,0},{2,3},{3,2},{4,5},{5,4},{6,7},{7,6},{8,9},{9,8},{10,11... | collective-permute-start | bytes 49160 | tf_op jit(solution)/shard_map/ppermute | solution.py:35
  11.5 4.9 %collective-permute-start.4 = (f32[4,8,128]{2,1,0:T(8,128)S(1)}, f32[4,8,128]{2,1,0:T(8,128)S(1)}, u32[]{:S(2)}, u32[]{:S(2)}) collective-permute-start(f32[4,8,128]{2,1,0:T(8,128)S(1)} %get-tuple-element.20), channel_id=1, source_target_pairs={{0,1},{1,0},{2,3},{3,2},{4,5},{5,4},{6,7},{7,6},{8,9},{9,8},{10,11... | collective-permute-start | bytes 49160 | tf_op jit(solution)/shard_map/ppermute | solution.py:35
  12.6 4.6 %collective-permute-start.7 = (f32[1,4,8,128]{3,2,1,0:T(8,128)S(1)}, f32[1,4,8,128]{3,2,1,0:T(8,128)S(1)}, u32[]{:S(2)}, u32[]{:S(2)}) collective-permute-start(f32[1,4,8,128]{3,2,1,0:T(8,128)S(1)} %add.7), channel_id=1, source_target_pairs={{0,8},{1,9},{2,10},{3,11},{4,12},{5,13},{6,14},{7,15},{8,0},{9,1},... | collective-permute-start | bytes 49160 | tf_op jit(solution)/shard_map/ppermute | solution.py:35

commit v5 on v4

--- a/solution.py
+++ b/solution.py
@@ -111,39 +111,17 @@
     )(spectra, delays)
 
 
-def pack_kernel(mine, theirs, both):
-    core = lax.axis_index("trials") & 1
-    first = core == 0
-    both[...] = jnp.zeros_like(both)
-    rows, cols = theirs.shape
-    both[0, :rows, :cols] = jnp.where(first, mine[:rows, :cols], theirs[...])
-    both[1, :rows, :cols] = jnp.where(first, theirs[...], mine[:rows, :cols])
-
-
-def pack_delays(mine, theirs):
-    return pl.pallas_call(
-        pack_kernel,
-        out_shape=VMEM((2,) + mine.shape, jnp.int32),
-        in_specs=[IN_VMEM] * 2,
+def pass_kernel(x, out):
+    out[...] = x[...]
+
+
+def pass_on(x):
+    return pl.pallas_call(
+        pass_kernel,
+        out_shape=VMEM(x.shape, x.dtype),
+        in_specs=[IN_VMEM],
         out_specs=IN_VMEM,
-        cost_estimate=cost(0, 1 << 20),
-    )(in_vmem(mine), in_vmem(theirs))
-
-
-def scalars_kernel(x, out, sem):
-    copy = pltpu.make_async_copy(x, out, sem)
-    copy.start()
-    copy.wait()
-
-
-def to_scalars(x):
-    return pl.pallas_call(
-        scalars_kernel,
-        out_shape=SMEM(x.shape, x.dtype),
-        in_specs=[IN_VMEM],
-        out_specs=IN_SMEM,
-        scratch_shapes=[pltpu.SemaphoreType.DMA(())],
-        cost_estimate=cost(0, 1 << 20),
+        cost_estimate=cost(1 << 34, 1 << 24),
     )(in_vmem(x))
 
 
@@ -174,29 +152,36 @@
     )(widths, spans)
 
 
-def windows(out, raw, masks, mean, delays, row, trials, group):
+def windows(out, raw, masks, mean, rows, delays, trials, group):
     me = lax.axis_index("trials")
+    if group <= 16:
+        tile = rows[...]
+        for i in range(trials):
+            for s in range(group):
+                delays[i, s] = tile[i, s]
+    else:
+        pltpu.sync_copy(rows, delays)
     for i in range(trials):
         j = i % SUBT
         acc = None
         for a, ref in enumerate(raw):
-            cut = ref[j, pl.ds(delays[row, i, me ^ masks[a]], SPAN), :]
+            cut = ref[j, pl.ds(delays[i, me ^ masks[a]], SPAN), :]
             acc = cut if acc is None else acc + cut
         less = None
         if group <= 16:
             for s in range(group):
-                cut = mean[j, pl.ds(delays[row, i, s], SPAN), :]
+                cut = mean[j, pl.ds(delays[i, s], SPAN), :]
                 less = cut if less is None else less + cut
         else:
             less = lax.fori_loop(
-                0, group, lambda s, v: v + mean[j, pl.ds(delays[row, i, s], SPAN), :], jnp.zeros_like(acc)
+                0, group, lambda s, v: v + mean[j, pl.ds(delays[i, s], SPAN), :], jnp.zeros_like(acc)
             )
         out[i] = acc - less
 
 
-def near_kernel(masks, trials, group, channels, *refs):
+def far_kernel(masks, trials, group, channels, *refs):
     known = len(masks)
-    raw, (near, keep, send, mean) = refs[:known], refs[known:]
+    raw, (far, out, mean, delays) = refs[:known], refs[known:]
     total = raw[0][0]
     for a in range(1, known):
         total = total + raw[a][0]
@@ -205,52 +190,42 @@
     for k in (1, 2, 4):
         total = total + shifted(total, k)
     mean[1] = total
-    core = lax.axis_index("trials") & 1
-    windows(keep, raw, masks, mean, near, core, trials, group)
-    windows(send, raw, masks, mean, near, 1 - core, trials, group)
-
-
-def near_sums(raw, masks, near, trials, group):
-    one = VMEM((trials, SPAN, LANES), jnp.float32)
-    return pl.pallas_call(
-        functools.partial(near_kernel, masks, trials, group, CH_SUB * group),
-        out_shape=(one, one, VMEM(raw[0].shape, jnp.float32)),
-        in_specs=[IN_VMEM] * len(raw) + [IN_SMEM],
-        out_specs=(IN_VMEM,) * 3,
-        cost_estimate=cost(0, 1 << 20),
-    )(*[in_vmem(r) for r in raw], in_smem(near))
-
-
-def far_kernel(masks, trials, group, other, *refs):
+
+    def one(e):
+        windows(out.at[e], raw, masks, mean, far.at[e], delays, trials, group)
+
+    if out.shape[0] == 1:
+        one(0)
+    else:
+        pl.loop(0, out.shape[0])(one)
+
+
+def far_sums(raw, masks, far, trials, group):
+    return pl.pallas_call(
+        functools.partial(far_kernel, masks, trials, group, CH_SUB * group),
+        out_shape=(VMEM((far.shape[0], trials, SPAN, LANES), jnp.float32), VMEM(raw[0].shape, jnp.float32)),
+        in_specs=[IN_VMEM] * (len(raw) + 1),
+        out_specs=(IN_VMEM,) * 2,
+        scratch_shapes=[pltpu.SMEM(far.shape[1:], jnp.int32)],
+        cost_estimate=cost(0, 1 << 20),
+    )(*[in_vmem(v) for v in (*raw, far)])
+
+
+def near_kernel(masks, trials, group, *refs):
     known = len(masks)
-    raw, (mean, far_in, out, far, sem) = refs[:known], refs[known:]
-    which = (lax.axis_index("trials") & 1) ^ other
-    chips = out.shape[0]
-    if chips == 1:
-        tile = far_in[which]
-        for i in range(trials):
-            for s in range(group):
-                far[0, i, s] = tile[i, s]
-        windows(out.at[0], raw, masks, mean, far, 0, trials, group)
-    else:
-        copy = pltpu.make_async_copy(far_in, far, sem)
-        copy.start()
-        copy.wait()
-
-        @pl.loop(0, chips)
-        def _(e):
-            windows(out.at[e], raw, masks, mean, far, 2 * e + which, trials, group)
-
-
-def far_sums(other, raw, masks, mean, far, trials, group):
-    return pl.pallas_call(
-        functools.partial(far_kernel, masks, trials, group, other),
-        out_shape=VMEM((far.shape[0] // 2, trials, SPAN, LANES), jnp.float32),
+    raw, (mean, rows, out, delays) = refs[:known], refs[known:]
+    windows(out, raw, masks, mean, rows, delays, trials, group)
+
+
+def near_sums(raw, masks, mean, rows, trials, group):
+    return pl.pallas_call(
+        functools.partial(near_kernel, masks, trials, group),
+        out_shape=VMEM((trials, SPAN, LANES), jnp.float32),
         in_specs=[IN_VMEM] * (len(raw) + 2),
         out_specs=IN_VMEM,
-        scratch_shapes=[pltpu.SMEM(far.shape, jnp.int32), pltpu.SemaphoreType.DMA(())],
-        cost_estimate=cost(0, 1 << 20),
-    )(*[in_vmem(v) for v in (*raw, mean, far)])
+        scratch_shapes=[pltpu.SMEM(rows.shape, jnp.int32)],
+        cost_estimate=cost(0, 1 << 20),
+    )(*[in_vmem(v) for v in (*raw, mean, rows)])
 
 
 def boxcar_kernel(a, b, bands, scale, mask, out, y, sems):
@@ -294,23 +269,20 @@
     group = lax.axis_size("trials")
     channels = CH_SUB * group
     trials = delays.shape[0]
+    far_bits = [b for b in (8, 16, 32, 64, 128, 256) if b < group]
+
+    raw, rows = raw_series(spectra, delays)
     masks = (0, 2, 4, 6)
-    far_bits = [b for b in (8, 16, 32, 64, 128, 256) if b < group]
-
-    raw, rows = raw_series(spectra, delays)
-    raw, theirs = lax.optimization_barrier((raw, swap(delays, 1, group)))
     raws = [raw] + [swap(raw, m, group) for m in masks[1:]]
-    owned = pack_delays(rows, theirs)
-    near = to_scalars(owned)
+    raws = raws + [swap(r, 1, group) for r in raws]
+    masks = masks + tuple(m ^ 1 for m in masks)
+    owned = rows[None]
     for b in far_bits:
-        owned = jnp.concatenate([owned, swap(owned, b, group)])[2 if b == far_bits[-1] else 0 :]
+        owned = jnp.concatenate([owned, swap(owned, b, group)])
     boxes = tables(widths, spans, channels)
 
-    keep, send, mean = near_sums(raws, masks, near, trials, group)
-    here = keep + swap(send, 1, group)
-    far = swap(far_sums(1, raws, masks, mean, owned, trials, group), 1, group)
-    far = far + far_sums(0, raws, masks, mean, owned, trials, group)
-    sums = jnp.concatenate([here[None], far])
+    far, mean = far_sums(raws, masks, pass_on(owned[1:]), trials, group)
+    sums = jnp.concatenate([near_sums(raws, masks, mean, rows, trials, group)[None], far])
     for b in reversed(far_bits):
         half = sums.shape[0] // 2
         mine, theirs = sums[:half], swap(sums[half:], b, group)

time: 18.4 us -> 18.1 us (0.984)
  waiting for transfers between devices: 1.9 us -> 2.79 us
  Pallas kernels: 5.17 us -> 4.28 us
  starting transfers between devices: 11.1 us -> 10.8 us
    ppermute x8 -> x9, waiting for transfers between devices: 1.9 us -> 2.79 us  [swap(): return lax.ppermute(x, 'trials', [(i, i ^ bit) for i in range(group)])]
    pallas_call x5 -> x3, Pallas kernels: 1.48 us -> 0.6 us  [the longest x1 0.35 us: far_sums(): pl.pallas_call(functools.partial(far_kernel, masks, trials, group, CH_SUB...]
    ppermute x8 -> x9, starting transfers between devices: 11.1 us -> 10.8 us  [swap(): return lax.ppermute(x, 'trials', [(i, i ^ bit) for i in range(group)])]
  transfers between devices with their start and end apart: 8 -> 9, of which waited for: 5 -> 6; matrix products, arithmetic and copies ran while one was open for 0% -> 0% of each run, Pallas kernels for 22% -> 6%
where the time goes in v5:
time: 18.1 us; the launch traced here: 17.9 us
  starting transfers between devices  10.8 us (60%)
  Pallas kernels  4.28 us (24%)
  waiting for transfers between devices  2.79 us (15%)
    ppermute x9, starting transfers between devices, swap(): return lax.ppermute(x, 'trials', [(i, i ^ bit) for i in range(group)])  10.8 us
    ppermute x9, waiting for transfers between devices, swap(): return lax.ppermute(x, 'trials', [(i, i ^ bit) for i in range(group)])  2.79 us
    pallas_call x1, Pallas kernels, raw_series(): pl.pallas_call(functools.partial(raw_kernel, chunks), out_shape=(VMEM((SU...  1.91 us
    pallas_call x1, Pallas kernels, boxcars(): pl.pallas_call(boxcar_kernel, out_shape=jax.ShapeDtypeStruct(shape, jnp.f...  0.94 us
    pallas_call x1, Pallas kernels, tables(): pl.pallas_call(functools.partial(tables_kernel, channels), out_shape=(VME...  0.84 us
  transfers between devices with their start and end apart: 9, of which 6 were waited for; matrix products, arithmetic and copies ran while one was open for 0% of the time, Pallas kernels for 6%

profile of v5, /device:TPU:0, one launch (start us, length us, event | category | flops | bytes accessed | tf_op | source)
XLA Modules:
  0.0 17.9 jit_solution(14431049173762950925)
XLA Ops:
  0.0 1.9 %shard_map.46 = (f32[2,64,128]{2,1,0:T(8,128)S(1)}, s32[8,128]{1,0:T(8,128)S(1)}) custom-call(bf16[128,8192]{1,0:T(8,128)(2,1)} %x_hbm.1, s32[4,16]{1,0:T(4,128)} %delays_hbm.1), custom_call_target="tpu_custom_call" | custom-call | flops 33554432 | bytes 2097152 | tf_op jit(solution)/shard_map/pallas_call | solution.py:100
  1.9 4.0 %collective-permute-start.2 = (f32[2,64,128]{2,1,0:T(8,128)S(1)}, f32[2,64,128]{2,1,0:T(8,128)S(1)}, u32[]{:S(2)}, u32[]{:S(2)}) collective-permute-start(f32[2,64,128]{2,1,0:T(8,128)S(1)} %get-tuple-element.12.refs_0_), channel_id=1, source_target_pairs={{0,6},{1,7},{2,4},{3,5},{4,2},{5,3},{6,0},{7,1},{8,14},{9,15},{10,... | collective-permute-start | bytes 196616 | tf_op jit(solution)/shard_map/ppermute | solution.py:35
  6.0 0.4 %collective-permute-start.1 = (f32[2,64,128]{2,1,0:T(8,128)S(1)}, f32[2,64,128]{2,1,0:T(8,128)S(1)}, u32[]{:S(2)}, u32[]{:S(2)}) collective-permute-start(f32[2,64,128]{2,1,0:T(8,128)S(1)} %get-tuple-element.12.refs_0_), channel_id=1, source_target_pairs={{0,4},{1,5},{2,6},{3,7},{4,0},{5,1},{6,2},{7,3},{8,12},{9,13},{10,... | collective-permute-start | bytes 196616 | tf_op jit(solution)/shard_map/ppermute | solution.py:35
  6.4 0.2 %collective-permute-start = (f32[2,64,128]{2,1,0:T(8,128)S(1)}, f32[2,64,128]{2,1,0:T(8,128)S(1)}, u32[]{:S(2)}, u32[]{:S(2)}) collective-permute-start(f32[2,64,128]{2,1,0:T(8,128)S(1)} %get-tuple-element.12.refs_0_), channel_id=1, source_target_pairs={{0,2},{1,3},{2,0},{3,1},{4,6},{5,7},{6,4},{7,5},{8,10},{9,11},{10,... | collective-permute-start | bytes 196616 | tf_op jit(solution)/shard_map/ppermute | solution.py:35
  6.6 2.9 %collective-permute-start.7 = (s32[1,8,128]{2,1,0:T(8,128)S(1)}, s32[1,8,128]{2,1,0:T(8,128)S(1)}, u32[]{:S(2)}, u32[]{:S(2)}) collective-permute-start(s32[1,8,128]{2,1,0:T(8,128)S(1)} %bitcast.6), channel_id=1, source_target_pairs={{0,8},{1,9},{2,10},{3,11},{4,12},{5,13},{6,14},{7,15},{8,0},{9,1},... | collective-permute-start | bytes 12296 | tf_op jit(solution)/shard_map/ppermute | solution.py:35
  9.5 0.0 collective-permute-start.3
  9.5 0.0 collective-permute-done.2.refs_3_
  9.5 0.5 %collective-permute-start.6 = (f32[2,64,128]{2,1,0:T(8,128)S(1)}, f32[2,64,128]{2,1,0:T(8,128)S(1)}, u32[]{:S(2)}, u32[]{:S(2)}) collective-permute-start(f32[2,64,128]{2,1,0:T(8,128)S(1)} %collective-permute-done.2.refs_3_), channel_id=1, source_target_pairs={{0,1},{1,0},{2,3},{3,2},{4,5},{5,4},{6,7},{7,6},{8,9},{9,8},{10,11... | collective-permute-start | bytes 196616 | tf_op jit(solution)/shard_map/ppermute | solution.py:35
  10.0 0.2 %collective-permute-done.1.refs_2_ = f32[2,64,128]{2,1,0:T(8,128)S(1)} collective-permute-done((f32[2,64,128]{2,1,0:T(8,128)S(1)}, f32[2,64,128]{2,1,0:T(8,128)S(1)}, u32[]{:S(2)}, u32[]{:S(2)}) %collective-permute-start.1) | collective-permute-done | bytes 65568 | tf_op jit(solution)/shard_map/ppermute | solution.py:35
  10.2 0.0 collective-permute-start.5
  10.2 0.4 %collective-permute-done.refs_1_ = f32[2,64,128]{2,1,0:T(8,128)S(1)} collective-permute-done((f32[2,64,128]{2,1,0:T(8,128)S(1)}, f32[2,64,128]{2,1,0:T(8,128)S(1)}, u32[]{:S(2)}, u32[]{:S(2)}) %collective-permute-start) | collective-permute-done | bytes 65568 | tf_op jit(solution)/shard_map/ppermute | solution.py:35
  10.7 0.1 collective-permute-start.4
  10.7 0.4 %collective-permute-done.7.x = s32[1,8,128]{2,1,0:T(8,128)S(1)} collective-permute-done((s32[1,8,128]{2,1,0:T(8,128)S(1)}, s32[1,8,128]{2,1,0:T(8,128)S(1)}, u32[]{:S(2)}, u32[]{:S(2)}) %collective-permute-start.7) | collective-permute-done | bytes 4128 | tf_op jit(solution)/shard_map/ppermute | solution.py:35
  11.1 0.0 collective-permute-done.3.refs_4_
  11.1 0.0 collective-permute-done.6.refs_7_
  11.1 0.4 %collective-permute-done.5.refs_6_ = f32[2,64,128]{2,1,0:T(8,128)S(1)} collective-permute-done((f32[2,64,128]{2,1,0:T(8,128)S(1)}, f32[2,64,128]{2,1,0:T(8,128)S(1)}, u32[]{:S(2)}, u32[]{:S(2)}) %collective-permute-start.5) | collective-permute-done | bytes 65568 | tf_op jit(solution)/shard_map/ppermute | solution.py:35
  11.5 0.4 %collective-permute-done.4.refs_5_ = f32[2,64,128]{2,1,0:T(8,128)S(1)} collective-permute-done((f32[2,64,128]{2,1,0:T(8,128)S(1)}, f32[2,64,128]{2,1,0:T(8,128)S(1)}, u32[]{:S(2)}, u32[]{:S(2)}) %collective-permute-start.4) | collective-permute-done | bytes 65568 | tf_op jit(solution)/shard_map/ppermute | solution.py:35
  11.9 0.4 %shard_map.48 = (f32[1,4,8,128]{3,2,1,0:T(8,128)S(1)}, f32[2,64,128]{2,1,0:T(8,128)S(1)}) custom-call(f32[2,64,128]{2,1,0:T(8,128)S(1)} %get-tuple-element.12.refs_0_, f32[2,64,128]{2,1,0:T(8,128)S(1)} %collective-permute-done.refs_1_, f32[2,64,128]{2,1,0:T(8,128)S(1)} %collective-permute-done.1.refs_2_, f32[2,64,128]{2,1,0:T(8,128)S(1)} %collective-permute-done.2.refs_3_, ...), custom_call_target="tpu_custom_call" | custom-call | bytes 1048576 | tf_op jit(solution)/shard_map/pallas_call | solution.py:204
  12.3 2.7 %collective-permute-start.8 = (f32[1,4,8,128]{3,2,1,0:T(8,128)S(1)}, f32[1,4,8,128]{3,2,1,0:T(8,128)S(1)}, u32[]{:S(2)}, u32[]{:S(2)}) collective-permute-start(f32[1,4,8,128]{3,2,1,0:T(8,128)S(1)} %get-tuple-element.15), channel_id=1, source_target_pairs={{0,8},{1,9},{2,10},{3,11},{4,12},{5,13},{6,14},{7,15},{8,0},{9,1},... | collective-permute-start | bytes 49160 | tf_op jit(solution)/shard_map/ppermute | solution.py:35
  14.9 0.8 %shard_map.50 = (bf16[256,1024]{1,0:T(8,128)(2,1)S(1)}, f32[8,128]{1,0:T(8,128)S(1)}, f32[8,128]{1,0:T(8,128)S(1)}) custom-call(s32[8]{0:T(128)} %widths.1, s32[16]{0:T(128)} %spans.1), custom_call_target="tpu_custom_call" | custom-call | bytes 1048576 | tf_op jit(solution)/shard_map/pallas_call | solution.py:142
  15.8 0.2 %shard_map.49.a = f32[4,8,128]{2,1,0:T(8,128)S(1)} custom-call(f32[2,64,128]{2,1,0:T(8,128)S(1)} %get-tuple-element.12.refs_0_, f32[2,64,128]{2,1,0:T(8,128)S(1)} %collective-permute-done.refs_1_, f32[2,64,128]{2,1,0:T(8,128)S(1)} %collective-permute-done.1.refs_2_, f32[2,64,128]{2,1,0:T(8,128)S(1)} %collective-permute-done.2.refs_3_, ...), custom_call_target="tpu_custom_call" | custom-call | bytes 1048576 | tf_op jit(solution)/shard_map/pallas_call | solution.py:221
  16.0 1.0 %collective-permute-done.8 = f32[1,4,8,128]{3,2,1,0:T(8,128)S(1)} collective-permute-done((f32[1,4,8,128]{3,2,1,0:T(8,128)S(1)}, f32[1,4,8,128]{3,2,1,0:T(8,128)S(1)}, u32[]{:S(2)}, u32[]{:S(2)}) %collective-permute-start.8) | collective-permute-done | bytes 16416 | tf_op jit(solution)/shard_map/ppermute | solution.py:35
  17.0 0.9 %shard_map.51 = f32[4,8,8,128]{3,2,1,0:T(8,128)} custom-call(f32[4,8,128]{2,1,0:T(8,128)S(1)} %shard_map.49.a, f32[4,8,128]{2,1,0:T(8,128)S(1)} %bitcast.5, bf16[256,1024]{1,0:T(8,128)(2,1)S(1)} %get-tuple-element.16.bands, f32[8,128]{1,0:T(8,128)S(1)} %get-tuple-element.17.scale, f32[8,128]{1,0:T(8,128)S(1)} %get-tuple-element.18.mask), custom_call_target="tpu_custom_call" | custom-call | bytes 1048576 | tf_op jit(solution)/shard_map/pallas_call | solution.py:257
  (1 shorter events, 0.0 us)
Async XLA Ops:
  1.9 7.6 %collective-permute-start.2 = (f32[2,64,128]{2,1,0:T(8,128)S(1)}, f32[2,64,128]{2,1,0:T(8,128)S(1)}, u32[]{:S(2)}, u32[]{:S(2)}) collective-permute-start(f32[2,64,128]{2,1,0:T(8,128)S(1)} %get-tuple-element.12.refs_0_), channel_id=1, source_target_pairs={{0,6},{1,7},{2,4},{3,5},{4,2},{5,3},{6,0},{7,1},{8,14},{9,15},{10,... | collective-permute-start | bytes 196616 | tf_op jit(solution)/shard_map/ppermute | solution.py:35
  6.0 4.3 %collective-permute-start.1 = (f32[2,64,128]{2,1,0:T(8,128)S(1)}, f32[2,64,128]{2,1,0:T(8,128)S(1)}, u32[]{:S(2)}, u32[]{:S(2)}) collective-permute-start(f32[2,64,128]{2,1,0:T(8,128)S(1)} %get-tuple-element.12.refs_0_), channel_id=1, source_target_pairs={{0,4},{1,5},{2,6},{3,7},{4,0},{5,1},{6,2},{7,3},{8,12},{9,13},{10,... | collective-permute-start | bytes 196616 | tf_op jit(solution)/shard_map/ppermute | solution.py:35
  6.4 4.3 %collective-permute-start = (f32[2,64,128]{2,1,0:T(8,128)S(1)}, f32[2,64,128]{2,1,0:T(8,128)S(1)}, u32[]{:S(2)}, u32[]{:S(2)}) collective-permute-start(f32[2,64,128]{2,1,0:T(8,128)S(1)} %get-tuple-element.12.refs_0_), channel_id=1, source_target_pairs={{0,2},{1,3},{2,0},{3,1},{4,6},{5,7},{6,4},{7,5},{8,10},{9,11},{10,... | collective-permute-start | bytes 196616 | tf_op jit(solution)/shard_map/ppermute | solution.py:35
  6.6 4.5 %collective-permute-start.7 = (s32[1,8,128]{2,1,0:T(8,128)S(1)}, s32[1,8,128]{2,1,0:T(8,128)S(1)}, u32[]{:S(2)}, u32[]{:S(2)}) collective-permute-start(s32[1,8,128]{2,1,0:T(8,128)S(1)} %bitcast.6), channel_id=1, source_target_pairs={{0,8},{1,9},{2,10},{3,11},{4,12},{5,13},{6,14},{7,15},{8,0},{9,1},... | collective-permute-start | bytes 12296 | tf_op jit(solution)/shard_map/ppermute | solution.py:35
  9.5 1.6 %collective-permute-start.3 = (f32[2,64,128]{2,1,0:T(8,128)S(1)}, f32[2,64,128]{2,1,0:T(8,128)S(1)}, u32[]{:S(2)}, u32[]{:S(2)}) collective-permute-start(f32[2,64,128]{2,1,0:T(8,128)S(1)} %get-tuple-element.12.refs_0_), channel_id=1, source_target_pairs={{0,1},{1,0},{2,3},{3,2},{4,5},{5,4},{6,7},{7,6},{8,9},{9,8},{10,11... | collective-permute-start | bytes 196616 | tf_op jit(solution)/shard_map/ppermute | solution.py:35
  9.5 1.6 %collective-permute-start.6 = (f32[2,64,128]{2,1,0:T(8,128)S(1)}, f32[2,64,128]{2,1,0:T(8,128)S(1)}, u32[]{:S(2)}, u32[]{:S(2)}) collective-permute-start(f32[2,64,128]{2,1,0:T(8,128)S(1)} %collective-permute-done.2.refs_3_), channel_id=1, source_target_pairs={{0,1},{1,0},{2,3},{3,2},{4,5},{5,4},{6,7},{7,6},{8,9},{9,8},{10,11... | collective-permute-start | bytes 196616 | tf_op jit(solution)/shard_map/ppermute | solution.py:35
  10.2 1.3 %collective-permute-start.5 = (f32[2,64,128]{2,1,0:T(8,128)S(1)}, f32[2,64,128]{2,1,0:T(8,128)S(1)}, u32[]{:S(2)}, u32[]{:S(2)}) collective-permute-start(f32[2,64,128]{2,1,0:T(8,128)S(1)} %collective-permute-done.1.refs_2_), channel_id=1, source_target_pairs={{0,1},{1,0},{2,3},{3,2},{4,5},{5,4},{6,7},{7,6},{8,9},{9,8},{10,11... | collective-permute-start | bytes 196616 | tf_op jit(solution)/shard_map/ppermute | solution.py:35
  10.7 1.3 %collective-permute-start.4 = (f32[2,64,128]{2,1,0:T(8,128)S(1)}, f32[2,64,128]{2,1,0:T(8,128)S(1)}, u32[]{:S(2)}, u32[]{:S(2)}) collective-permute-start(f32[2,64,128]{2,1,0:T(8,128)S(1)} %collective-permute-done.refs_1_), channel_id=1, source_target_pairs={{0,1},{1,0},{2,3},{3,2},{4,5},{5,4},{6,7},{7,6},{8,9},{9,8},{10,11... | collective-permute-start | bytes 196616 | tf_op jit(solution)/shard_map/ppermute | solution.py:35
  12.3 4.7 %collective-permute-start.8 = (f32[1,4,8,128]{3,2,1,0:T(8,128)S(1)}, f32[1,4,8,128]{3,2,1,0:T(8,128)S(1)}, u32[]{:S(2)}, u32[]{:S(2)}) collective-permute-start(f32[1,4,8,128]{3,2,1,0:T(8,128)S(1)} %get-tuple-element.15), channel_id=1, source_target_pairs={{0,8},{1,9},{2,10},{3,11},{4,12},{5,13},{6,14},{7,15},{8,0},{9,1},... | collective-permute-start | bytes 49160 | tf_op jit(solution)/shard_map/ppermute | solution.py:35

commit v6 on v5

--- a/solution.py
+++ b/solution.py
@@ -111,17 +111,24 @@
     )(spectra, delays)
 
 
-def pass_kernel(x, out):
-    out[...] = x[...]
-
-
-def pass_on(x):
-    return pl.pallas_call(
-        pass_kernel,
-        out_shape=VMEM(x.shape, x.dtype),
+def scalars_kernel(trials, group, x, out):
+    if x.shape[0] * group <= 16:
+        for e in range(x.shape[0]):
+            tile = x[e]
+            for i in range(trials):
+                for s in range(group):
+                    out[e, i, s] = tile[i, s]
+    else:
+        pltpu.sync_copy(x, out)
+
+
+def to_scalars(x, trials, group, estimate):
+    return pl.pallas_call(
+        functools.partial(scalars_kernel, trials, group),
+        out_shape=SMEM(x.shape, x.dtype),
         in_specs=[IN_VMEM],
-        out_specs=IN_VMEM,
-        cost_estimate=cost(1 << 34, 1 << 24),
+        out_specs=IN_SMEM,
+        cost_estimate=estimate,
     )(in_vmem(x))
 
 
@@ -152,36 +159,29 @@
     )(widths, spans)
 
 
-def windows(out, raw, masks, mean, rows, delays, trials, group):
+def windows(out, raw, masks, mean, delays, e, trials, group):
     me = lax.axis_index("trials")
-    if group <= 16:
-        tile = rows[...]
-        for i in range(trials):
-            for s in range(group):
-                delays[i, s] = tile[i, s]
-    else:
-        pltpu.sync_copy(rows, delays)
     for i in range(trials):
         j = i % SUBT
         acc = None
         for a, ref in enumerate(raw):
-            cut = ref[j, pl.ds(delays[i, me ^ masks[a]], SPAN), :]
+            cut = ref[j, pl.ds(delays[e, i, me ^ masks[a]], SPAN), :]
             acc = cut if acc is None else acc + cut
         less = None
         if group <= 16:
             for s in range(group):
-                cut = mean[j, pl.ds(delays[i, s], SPAN), :]
+                cut = mean[j, pl.ds(delays[e, i, s], SPAN), :]
                 less = cut if less is None else less + cut
         else:
             less = lax.fori_loop(
-                0, group, lambda s, v: v + mean[j, pl.ds(delays[i, s], SPAN), :], jnp.zeros_like(acc)
+                0, group, lambda s, v: v + mean[j, pl.ds(delays[e, i, s], SPAN), :], jnp.zeros_like(acc)
             )
         out[i] = acc - less
 
 
 def far_kernel(masks, trials, group, channels, *refs):
     known = len(masks)
-    raw, (far, out, mean, delays) = refs[:known], refs[known:]
+    raw, (far, out, mean) = refs[:known], refs[known:]
     total = raw[0][0]
     for a in range(1, known):
         total = total + raw[a][0]
@@ -192,7 +192,7 @@
     mean[1] = total
 
     def one(e):
-        windows(out.at[e], raw, masks, mean, far.at[e], delays, trials, group)
+        windows(out.at[e], raw, masks, mean, far, e, trials, group)
 
     if out.shape[0] == 1:
         one(0)
@@ -204,28 +204,26 @@
     return pl.pallas_call(
         functools.partial(far_kernel, masks, trials, group, CH_SUB * group),
         out_shape=(VMEM((far.shape[0], trials, SPAN, LANES), jnp.float32), VMEM(raw[0].shape, jnp.float32)),
-        in_specs=[IN_VMEM] * (len(raw) + 1),
+        in_specs=[IN_VMEM] * len(raw) + [IN_SMEM],
         out_specs=(IN_VMEM,) * 2,
-        scratch_shapes=[pltpu.SMEM(far.shape[1:], jnp.int32)],
-        cost_estimate=cost(0, 1 << 20),
-    )(*[in_vmem(v) for v in (*raw, far)])
+        cost_estimate=cost(0, 1 << 20),
+    )(*[in_vmem(v) for v in raw], in_smem(far))
 
 
 def near_kernel(masks, trials, group, *refs):
     known = len(masks)
-    raw, (mean, rows, out, delays) = refs[:known], refs[known:]
-    windows(out, raw, masks, mean, rows, delays, trials, group)
-
-
-def near_sums(raw, masks, mean, rows, trials, group):
+    raw, (mean, near, out) = refs[:known], refs[known:]
+    windows(out, raw, masks, mean, near, 0, trials, group)
+
+
+def near_sums(raw, masks, mean, near, trials, group):
     return pl.pallas_call(
         functools.partial(near_kernel, masks, trials, group),
         out_shape=VMEM((trials, SPAN, LANES), jnp.float32),
-        in_specs=[IN_VMEM] * (len(raw) + 2),
+        in_specs=[IN_VMEM] * (len(raw) + 1) + [IN_SMEM],
         out_specs=IN_VMEM,
-        scratch_shapes=[pltpu.SMEM(rows.shape, jnp.int32)],
-        cost_estimate=cost(0, 1 << 20),
-    )(*[in_vmem(v) for v in (*raw, mean, rows)])
+        cost_estimate=cost(0, 1 << 20),
+    )(*[in_vmem(v) for v in (*raw, mean)], in_smem(near))
 
 
 def boxcar_kernel(a, b, bands, scale, mask, out, y, sems):
@@ -281,8 +279,10 @@
         owned = jnp.concatenate([owned, swap(owned, b, group)])
     boxes = tables(widths, spans, channels)
 
-    far, mean = far_sums(raws, masks, pass_on(owned[1:]), trials, group)
-    sums = jnp.concatenate([near_sums(raws, masks, mean, rows, trials, group)[None], far])
+    near = to_scalars(rows[None], trials, group, cost(0, 1 << 20))
+    away = to_scalars(owned[1:], trials, group, cost(1 << 34, 1 << 24))
+    far, mean = far_sums(raws, masks, away, trials, group)
+    sums = jnp.concatenate([near_sums(raws, masks, mean, near, trials, group)[None], far])
     for b in reversed(far_bits):
         half = sums.shape[0] // 2
         mine, theirs = sums[:half], swap(sums[half:], b, group)

time: 18.1 us -> 18 us (level)
  waiting for transfers between devices: 2.79 us -> 2.52 us
  Pallas kernels: 4.28 us -> 4.48 us
    pallas_call x1 -> x2, Pallas kernels: 0.01 us -> 0.36 us  [to_scalars(): pl.pallas_call(functools.partial(scalars_kernel, trials, group), out_shap...]
    ppermute x9, waiting for transfers between devices: 2.79 us -> 2.52 us  [swap(): return lax.ppermute(x, 'trials', [(i, i ^ bit) for i in range(group)])]
  transfers between devices with their start and end apart: 9 -> 9, of which waited for: 6 -> 6; matrix products, arithmetic and copies ran while one was open for 0% -> 0% of each run, Pallas kernels for 6% -> 7%
where the time goes in v6:
time: 18 us; the launch traced here: 17.9 us
  starting transfers between devices  10.8 us (60%)
  Pallas kernels  4.48 us (25%)
  waiting for transfers between devices  2.52 us (14%)
    ppermute x9, starting transfers between devices, swap(): return lax.ppermute(x, 'trials', [(i, i ^ bit) for i in range(group)])  10.8 us
    ppermute x9, waiting for transfers between devices, swap(): return lax.ppermute(x, 'trials', [(i, i ^ bit) for i in range(group)])  2.52 us
    pallas_call x1, Pallas kernels, raw_series(): pl.pallas_call(functools.partial(raw_kernel, chunks), out_shape=(VMEM((SU...  1.91 us
    pallas_call x1, Pallas kernels, boxcars(): pl.pallas_call(boxcar_kernel, out_shape=jax.ShapeDtypeStruct(shape, jnp.f...  0.94 us
    pallas_call x1, Pallas kernels, tables(): pl.pallas_call(functools.partial(tables_kernel, channels), out_shape=(VME...  0.84 us
  transfers between devices with their start and end apart: 9, of which 6 were waited for; matrix products, arithmetic and copies ran while one was open for 0% of the time, Pallas kernels for 7%

profile of v6, /device:TPU:0, one launch (start us, length us, event | category | flops | bytes accessed | tf_op | source)
XLA Modules:
  0.0 17.9 jit_solution(7303724529227133435)
XLA Ops:
  0.0 1.9 %shard_map.46 = (f32[2,64,128]{2,1,0:T(8,128)S(1)}, s32[8,128]{1,0:T(8,128)S(1)}) custom-call(bf16[128,8192]{1,0:T(8,128)(2,1)} %x_hbm.1, s32[4,16]{1,0:T(4,128)} %delays_hbm.1), custom_call_target="tpu_custom_call" | custom-call | flops 33554432 | bytes 2097152 | tf_op jit(solution)/shard_map/pallas_call | solution.py:100
  1.9 4.0 %collective-permute-start.2 = (f32[2,64,128]{2,1,0:T(8,128)S(1)}, f32[2,64,128]{2,1,0:T(8,128)S(1)}, u32[]{:S(2)}, u32[]{:S(2)}) collective-permute-start(f32[2,64,128]{2,1,0:T(8,128)S(1)} %get-tuple-element.12.refs_0_), channel_id=1, source_target_pairs={{0,6},{1,7},{2,4},{3,5},{4,2},{5,3},{6,0},{7,1},{8,14},{9,15},{10,... | collective-permute-start | bytes 196616 | tf_op jit(solution)/shard_map/ppermute | solution.py:35
  6.0 0.4 %collective-permute-start.1 = (f32[2,64,128]{2,1,0:T(8,128)S(1)}, f32[2,64,128]{2,1,0:T(8,128)S(1)}, u32[]{:S(2)}, u32[]{:S(2)}) collective-permute-start(f32[2,64,128]{2,1,0:T(8,128)S(1)} %get-tuple-element.12.refs_0_), channel_id=1, source_target_pairs={{0,4},{1,5},{2,6},{3,7},{4,0},{5,1},{6,2},{7,3},{8,12},{9,13},{10,... | collective-permute-start | bytes 196616 | tf_op jit(solution)/shard_map/ppermute | solution.py:35
  6.4 0.2 %collective-permute-start = (f32[2,64,128]{2,1,0:T(8,128)S(1)}, f32[2,64,128]{2,1,0:T(8,128)S(1)}, u32[]{:S(2)}, u32[]{:S(2)}) collective-permute-start(f32[2,64,128]{2,1,0:T(8,128)S(1)} %get-tuple-element.12.refs_0_), channel_id=1, source_target_pairs={{0,2},{1,3},{2,0},{3,1},{4,6},{5,7},{6,4},{7,5},{8,10},{9,11},{10,... | collective-permute-start | bytes 196616 | tf_op jit(solution)/shard_map/ppermute | solution.py:35
  6.6 2.9 %collective-permute-start.7 = (s32[1,8,128]{2,1,0:T(8,128)S(1)}, s32[1,8,128]{2,1,0:T(8,128)S(1)}, u32[]{:S(2)}, u32[]{:S(2)}) collective-permute-start(s32[1,8,128]{2,1,0:T(8,128)S(1)} %bitcast.6), channel_id=1, source_target_pairs={{0,8},{1,9},{2,10},{3,11},{4,12},{5,13},{6,14},{7,15},{8,0},{9,1},... | collective-permute-start | bytes 12296 | tf_op jit(solution)/shard_map/ppermute | solution.py:35
  9.5 0.0 collective-permute-start.3
  9.5 0.0 collective-permute-done.2.refs_3_
  9.5 0.5 %collective-permute-start.6 = (f32[2,64,128]{2,1,0:T(8,128)S(1)}, f32[2,64,128]{2,1,0:T(8,128)S(1)}, u32[]{:S(2)}, u32[]{:S(2)}) collective-permute-start(f32[2,64,128]{2,1,0:T(8,128)S(1)} %collective-permute-done.2.refs_3_), channel_id=1, source_target_pairs={{0,1},{1,0},{2,3},{3,2},{4,5},{5,4},{6,7},{7,6},{8,9},{9,8},{10,11... | collective-permute-start | bytes 196616 | tf_op jit(solution)/shard_map/ppermute | solution.py:35
  10.0 0.2 %collective-permute-done.1.refs_2_ = f32[2,64,128]{2,1,0:T(8,128)S(1)} collective-permute-done((f32[2,64,128]{2,1,0:T(8,128)S(1)}, f32[2,64,128]{2,1,0:T(8,128)S(1)}, u32[]{:S(2)}, u32[]{:S(2)}) %collective-permute-start.1) | collective-permute-done | bytes 65568 | tf_op jit(solution)/shard_map/ppermute | solution.py:35
  10.2 0.0 collective-permute-start.5
  10.2 0.4 %collective-permute-done.refs_1_ = f32[2,64,128]{2,1,0:T(8,128)S(1)} collective-permute-done((f32[2,64,128]{2,1,0:T(8,128)S(1)}, f32[2,64,128]{2,1,0:T(8,128)S(1)}, u32[]{:S(2)}, u32[]{:S(2)}) %collective-permute-start) | collective-permute-done | bytes 65568 | tf_op jit(solution)/shard_map/ppermute | solution.py:35
  10.7 0.1 collective-permute-start.4
  10.7 0.4 %collective-permute-done.7.x = s32[1,8,128]{2,1,0:T(8,128)S(1)} collective-permute-done((s32[1,8,128]{2,1,0:T(8,128)S(1)}, s32[1,8,128]{2,1,0:T(8,128)S(1)}, u32[]{:S(2)}, u32[]{:S(2)}) %collective-permute-start.7) | collective-permute-done | bytes 4128 | tf_op jit(solution)/shard_map/ppermute | solution.py:35
  11.1 0.2 shard_map.47.refs_8_
  11.3 0.0 collective-permute-done.3.refs_4_
  11.3 0.0 collective-permute-done.6.refs_7_
  11.3 0.2 collective-permute-done.5.refs_6_
  11.5 0.4 %collective-permute-done.4.refs_5_ = f32[2,64,128]{2,1,0:T(8,128)S(1)} collective-permute-done((f32[2,64,128]{2,1,0:T(8,128)S(1)}, f32[2,64,128]{2,1,0:T(8,128)S(1)}, u32[]{:S(2)}, u32[]{:S(2)}) %collective-permute-start.4) | collective-permute-done | bytes 65568 | tf_op jit(solution)/shard_map/ppermute | solution.py:35
  11.9 0.3 %shard_map.48 = (f32[1,4,8,128]{3,2,1,0:T(8,128)S(1)}, f32[2,64,128]{2,1,0:T(8,128)S(1)}) custom-call(f32[2,64,128]{2,1,0:T(8,128)S(1)} %get-tuple-element.12.refs_0_, f32[2,64,128]{2,1,0:T(8,128)S(1)} %collective-permute-done.refs_1_, f32[2,64,128]{2,1,0:T(8,128)S(1)} %collective-permute-done.1.refs_2_, f32[2,64,128]{2,1,0:T(8,128)S(1)} %collective-permute-done.2.refs_3_, ...), custom_call_target="tpu_custom_call" | custom-call | bytes 1048576 | tf_op jit(solution)/shard_map/pallas_call | solution.py:204
  12.2 2.7 %collective-permute-start.8 = (f32[1,4,8,128]{3,2,1,0:T(8,128)S(1)}, f32[1,4,8,128]{3,2,1,0:T(8,128)S(1)}, u32[]{:S(2)}, u32[]{:S(2)}) collective-permute-start(f32[1,4,8,128]{3,2,1,0:T(8,128)S(1)} %get-tuple-element.15), channel_id=1, source_target_pairs={{0,8},{1,9},{2,10},{3,11},{4,12},{5,13},{6,14},{7,15},{8,0},{9,1},... | collective-permute-start | bytes 49160 | tf_op jit(solution)/shard_map/ppermute | solution.py:35
  14.9 0.2 shard_map.49.refs_9_
  15.1 0.8 %shard_map.51 = (bf16[256,1024]{1,0:T(8,128)(2,1)S(1)}, f32[8,128]{1,0:T(8,128)S(1)}, f32[8,128]{1,0:T(8,128)S(1)}) custom-call(s32[8]{0:T(128)} %widths.1, s32[16]{0:T(128)} %spans.1), custom_call_target="tpu_custom_call" | custom-call | bytes 1048576 | tf_op jit(solution)/shard_map/pallas_call | solution.py:149
  15.9 0.1 shard_map.50.a
  16.1 0.9 %collective-permute-done.8 = f32[1,4,8,128]{3,2,1,0:T(8,128)S(1)} collective-permute-done((f32[1,4,8,128]{3,2,1,0:T(8,128)S(1)}, f32[1,4,8,128]{3,2,1,0:T(8,128)S(1)}, u32[]{:S(2)}, u32[]{:S(2)}) %collective-permute-start.8) | collective-permute-done | bytes 16416 | tf_op jit(solution)/shard_map/ppermute | solution.py:35
  16.9 0.9 %shard_map.52 = f32[4,8,8,128]{3,2,1,0:T(8,128)} custom-call(f32[4,8,128]{2,1,0:T(8,128)S(1)} %shard_map.50.a, f32[4,8,128]{2,1,0:T(8,128)S(1)} %bitcast.5, bf16[256,1024]{1,0:T(8,128)(2,1)S(1)} %get-tuple-element.16.bands, f32[8,128]{1,0:T(8,128)S(1)} %get-tuple-element.17.scale, f32[8,128]{1,0:T(8,128)S(1)} %get-tuple-element.18.mask), custom_call_target="tpu_custom_call" | custom-call | bytes 1048576 | tf_op jit(solution)/shard_map/pallas_call | solution.py:255
Async XLA Ops:
  1.9 7.6 %collective-permute-start.2 = (f32[2,64,128]{2,1,0:T(8,128)S(1)}, f32[2,64,128]{2,1,0:T(8,128)S(1)}, u32[]{:S(2)}, u32[]{:S(2)}) collective-permute-start(f32[2,64,128]{2,1,0:T(8,128)S(1)} %get-tuple-element.12.refs_0_), channel_id=1, source_target_pairs={{0,6},{1,7},{2,4},{3,5},{4,2},{5,3},{6,0},{7,1},{8,14},{9,15},{10,... | collective-permute-start | bytes 196616 | tf_op jit(solution)/shard_map/ppermute | solution.py:35
  6.0 4.3 %collective-permute-start.1 = (f32[2,64,128]{2,1,0:T(8,128)S(1)}, f32[2,64,128]{2,1,0:T(8,128)S(1)}, u32[]{:S(2)}, u32[]{:S(2)}) collective-permute-start(f32[2,64,128]{2,1,0:T(8,128)S(1)} %get-tuple-element.12.refs_0_), channel_id=1, source_target_pairs={{0,4},{1,5},{2,6},{3,7},{4,0},{5,1},{6,2},{7,3},{8,12},{9,13},{10,... | collective-permute-start | bytes 196616 | tf_op jit(solution)/shard_map/ppermute | solution.py:35
  6.4 4.3 %collective-permute-start = (f32[2,64,128]{2,1,0:T(8,128)S(1)}, f32[2,64,128]{2,1,0:T(8,128)S(1)}, u32[]{:S(2)}, u32[]{:S(2)}) collective-permute-start(f32[2,64,128]{2,1,0:T(8,128)S(1)} %get-tuple-element.12.refs_0_), channel_id=1, source_target_pairs={{0,2},{1,3},{2,0},{3,1},{4,6},{5,7},{6,4},{7,5},{8,10},{9,11},{10,... | collective-permute-start | bytes 196616 | tf_op jit(solution)/shard_map/ppermute | solution.py:35
  6.6 4.5 %collective-permute-start.7 = (s32[1,8,128]{2,1,0:T(8,128)S(1)}, s32[1,8,128]{2,1,0:T(8,128)S(1)}, u32[]{:S(2)}, u32[]{:S(2)}) collective-permute-start(s32[1,8,128]{2,1,0:T(8,128)S(1)} %bitcast.6), channel_id=1, source_target_pairs={{0,8},{1,9},{2,10},{3,11},{4,12},{5,13},{6,14},{7,15},{8,0},{9,1},... | collective-permute-start | bytes 12296 | tf_op jit(solution)/shard_map/ppermute | solution.py:35
  9.5 1.8 %collective-permute-start.3 = (f32[2,64,128]{2,1,0:T(8,128)S(1)}, f32[2,64,128]{2,1,0:T(8,128)S(1)}, u32[]{:S(2)}, u32[]{:S(2)}) collective-permute-start(f32[2,64,128]{2,1,0:T(8,128)S(1)} %get-tuple-element.12.refs_0_), channel_id=1, source_target_pairs={{0,1},{1,0},{2,3},{3,2},{4,5},{5,4},{6,7},{7,6},{8,9},{9,8},{10,11... | collective-permute-start | bytes 196616 | tf_op jit(solution)/shard_map/ppermute | solution.py:35
  9.5 1.8 %collective-permute-start.6 = (f32[2,64,128]{2,1,0:T(8,128)S(1)}, f32[2,64,128]{2,1,0:T(8,128)S(1)}, u32[]{:S(2)}, u32[]{:S(2)}) collective-permute-start(f32[2,64,128]{2,1,0:T(8,128)S(1)} %collective-permute-done.2.refs_3_), channel_id=1, source_target_pairs={{0,1},{1,0},{2,3},{3,2},{4,5},{5,4},{6,7},{7,6},{8,9},{9,8},{10,11... | collective-permute-start | bytes 196616 | tf_op jit(solution)/shard_map/ppermute | solution.py:35
  10.2 1.3 %collective-permute-start.5 = (f32[2,64,128]{2,1,0:T(8,128)S(1)}, f32[2,64,128]{2,1,0:T(8,128)S(1)}, u32[]{:S(2)}, u32[]{:S(2)}) collective-permute-start(f32[2,64,128]{2,1,0:T(8,128)S(1)} %collective-permute-done.1.refs_2_), channel_id=1, source_target_pairs={{0,1},{1,0},{2,3},{3,2},{4,5},{5,4},{6,7},{7,6},{8,9},{9,8},{10,11... | collective-permute-start | bytes 196616 | tf_op jit(solution)/shard_map/ppermute | solution.py:35
  10.7 1.3 %collective-permute-start.4 = (f32[2,64,128]{2,1,0:T(8,128)S(1)}, f32[2,64,128]{2,1,0:T(8,128)S(1)}, u32[]{:S(2)}, u32[]{:S(2)}) collective-permute-start(f32[2,64,128]{2,1,0:T(8,128)S(1)} %collective-permute-done.refs_1_), channel_id=1, source_target_pairs={{0,1},{1,0},{2,3},{3,2},{4,5},{5,4},{6,7},{7,6},{8,9},{9,8},{10,11... | collective-permute-start | bytes 196616 | tf_op jit(solution)/shard_map/ppermute | solution.py:35
  12.2 4.7 %collective-permute-start.8 = (f32[1,4,8,128]{3,2,1,0:T(8,128)S(1)}, f32[1,4,8,128]{3,2,1,0:T(8,128)S(1)}, u32[]{:S(2)}, u32[]{:S(2)}) collective-permute-start(f32[1,4,8,128]{3,2,1,0:T(8,128)S(1)} %get-tuple-element.15), channel_id=1, source_target_pairs={{0,8},{1,9},{2,10},{3,11},{4,12},{5,13},{6,14},{7,15},{8,0},{9,1},... | collective-permute-start | bytes 49160 | tf_op jit(solution)/shard_map/ppermute | solution.py:35

commit v7 on v6

--- a/solution.py
+++ b/solution.py
@@ -35,13 +35,15 @@
     return lax.ppermute(x, "trials", [(i, i ^ bit) for i in range(group)])
 
 
-def shifted(x, k):
+def sum_ahead(x):
     lane = lax.broadcasted_iota(jnp.int32, x.shape, 1)
     row = lax.broadcasted_iota(jnp.int32, x.shape, 0)
-    here = pltpu.roll(x, LANES - k, 1)
-    after = pltpu.roll(here, x.shape[0] - 1, 0)
-    after = jnp.where(row == x.shape[0] - 1, 0.0, after)
-    return jnp.where(lane < LANES - k, here, after)
+    after = jnp.where(row == x.shape[0] - 1, 0.0, pltpu.roll(x, x.shape[0] - 1, 0))
+    for k in (1, 2, 4):
+        ahead = pltpu.roll(after, LANES - k, 1)
+        x = x + jnp.where(lane < LANES - k, pltpu.roll(x, LANES - k, 1), ahead)
+        after = after + ahead
+    return x
 
 
 def raw_kernel(chunks, x_hbm, delays_hbm, out, rows, x, delays, sems):
@@ -159,19 +161,21 @@
     )(widths, spans)
 
 
+def tree_sum(terms):
+    while len(terms) > 1:
+        terms = [terms[k] + terms[k + 1] for k in range(0, len(terms) - 1, 2)] + terms[len(terms) & ~1 :]
+    return terms[0]
+
+
 def windows(out, raw, masks, mean, delays, e, trials, group):
     me = lax.axis_index("trials")
     for i in range(trials):
         j = i % SUBT
-        acc = None
-        for a, ref in enumerate(raw):
-            cut = ref[j, pl.ds(delays[e, i, me ^ masks[a]], SPAN), :]
-            acc = cut if acc is None else acc + cut
-        less = None
+        acc = tree_sum(
+            [ref[j, pl.ds(delays[e, i, me ^ masks[a]], SPAN), :] for a, ref in enumerate(raw)]
+        )
         if group <= 16:
-            for s in range(group):
-                cut = mean[j, pl.ds(delays[e, i, s], SPAN), :]
-                less = cut if less is None else less + cut
+            less = tree_sum([mean[j, pl.ds(delays[e, i, s], SPAN), :] for s in range(group)])
         else:
             less = lax.fori_loop(
                 0, group, lambda s, v: v + mean[j, pl.ds(delays[e, i, s], SPAN), :], jnp.zeros_like(acc)
@@ -179,17 +183,34 @@
         out[i] = acc - less
 
 
-def far_kernel(masks, trials, group, channels, *refs):
+def means(total, channels):
+    return total * (CH_SUB / channels), sum_ahead(total * (PER_LAG / channels))
+
+
+def early_kernel(channels, *refs):
+    raw, out = refs[:-1], refs[-1]
+    total = raw[0][0]
+    for r in raw[1:]:
+        total = total + r[0]
+    out[0], out[1] = means(total, channels)
+
+
+def early_mean(raw, group):
+    return pl.pallas_call(
+        functools.partial(early_kernel, CH_SUB * group),
+        out_shape=VMEM(raw[0].shape, jnp.float32),
+        in_specs=[IN_VMEM] * len(raw),
+        out_specs=IN_VMEM,
+        cost_estimate=cost(0, 1 << 20),
+    )(*[in_vmem(v) for v in raw])
+
+
+def far_kernel(masks, trials, group, channels, last, *refs):
     known = len(masks)
-    raw, (far, out, mean) = refs[:known], refs[known:]
-    total = raw[0][0]
-    for a in range(1, known):
-        total = total + raw[a][0]
-    mean[0] = total * (CH_SUB / channels)
-    total = total * (PER_LAG / channels)
-    for k in (1, 2, 4):
-        total = total + shifted(total, k)
-    mean[1] = total
+    raw, (early, far, out, mean) = refs[:known], refs[known:]
+    plain, ahead = means(raw[last][0], channels)
+    mean[0] = early[0] + plain
+    mean[1] = early[1] + ahead
 
     def one(e):
         windows(out.at[e], raw, masks, mean, far, e, trials, group)
@@ -200,14 +221,14 @@
         pl.loop(0, out.shape[0])(one)
 
 
-def far_sums(raw, masks, far, trials, group):
-    return pl.pallas_call(
-        functools.partial(far_kernel, masks, trials, group, CH_SUB * group),
+def far_sums(raw, masks, early, last, far, trials, group):
+    return pl.pallas_call(
+        functools.partial(far_kernel, masks, trials, group, CH_SUB * group, last),
         out_shape=(VMEM((far.shape[0], trials, SPAN, LANES), jnp.float32), VMEM(raw[0].shape, jnp.float32)),
-        in_specs=[IN_VMEM] * len(raw) + [IN_SMEM],
+        in_specs=[IN_VMEM] * (len(raw) + 1) + [IN_SMEM],
         out_specs=(IN_VMEM,) * 2,
         cost_estimate=cost(0, 1 << 20),
-    )(*[in_vmem(v) for v in raw], in_smem(far))
+    )(*[in_vmem(v) for v in (*raw, early)], in_smem(far))
 
 
 def near_kernel(masks, trials, group, *refs):
@@ -281,7 +302,9 @@
 
     near = to_scalars(rows[None], trials, group, cost(0, 1 << 20))
     away = to_scalars(owned[1:], trials, group, cost(1 << 34, 1 << 24))
-    far, mean = far_sums(raws, masks, away, trials, group)
+    last = masks.index(3)
+    early = early_mean(raws[:last] + raws[last + 1 :], group)
+    far, mean = far_sums(raws, masks, early, last, away, trials, group)
     sums = jnp.concatenate([near_sums(raws, masks, mean, near, trials, group)[None], far])
     for b in reversed(far_bits):
         half = sums.shape[0] // 2

time: 18 us -> 18 us (level)
  waiting for transfers between devices: 2.52 us -> 2.25 us
  Pallas kernels: 4.48 us -> 4.74 us
    ppermute x9, waiting for transfers between devices: 2.52 us -> 2.25 us  [swap(): return lax.ppermute(x, 'trials', [(i, i ^ bit) for i in range(group)])]
    pallas_call x0 -> x1, Pallas kernels: none -> 0.23 us  [early_mean(): pl.pallas_call(functools.partial(early_kernel, CH_SUB * group), out_shape...]
  transfers between devices with their start and end apart: 9 -> 9, of which waited for: 6 -> 6; matrix products, arithmetic and copies ran while one was open for 0% -> 0% of each run, Pallas kernels for 7% -> 9%
where the time goes in v7:
time: 18 us; the launch traced here: 17.9 us
  starting transfers between devices  10.8 us (60%)
  Pallas kernels  4.74 us (26%)
  waiting for transfers between devices  2.25 us (12%)
    ppermute x9, starting transfers between devices, swap(): return lax.ppermute(x, 'trials', [(i, i ^ bit) for i in range(group)])  10.8 us
    ppermute x9, waiting for transfers between devices, swap(): return lax.ppermute(x, 'trials', [(i, i ^ bit) for i in range(group)])  2.25 us
    pallas_call x1, Pallas kernels, raw_series(): pl.pallas_call(functools.partial(raw_kernel, chunks), out_shape=(VMEM((SU...  1.91 us
    pallas_call x1, Pallas kernels, boxcars(): pl.pallas_call(boxcar_kernel, out_shape=jax.ShapeDtypeStruct(shape, jnp.f...  0.94 us
    pallas_call x1, Pallas kernels, tables(): pl.pallas_call(functools.partial(tables_kernel, channels), out_shape=(VME...  0.84 us
  transfers between devices with their start and end apart: 9, of which 6 were waited for; matrix products, arithmetic and copies ran while one was open for 0% of the time, Pallas kernels for 9%

profile of v7, /device:TPU:0, one launch (start us, length us, event | category | flops | bytes accessed | tf_op | source)
XLA Modules:
  0.0 17.9 jit_solution(10303956549649536684)
XLA Ops:
  0.0 1.9 %shard_map.46 = (f32[2,64,128]{2,1,0:T(8,128)S(1)}, s32[8,128]{1,0:T(8,128)S(1)}) custom-call(bf16[128,8192]{1,0:T(8,128)(2,1)} %x_hbm.1, s32[4,16]{1,0:T(4,128)} %delays_hbm.1), custom_call_target="tpu_custom_call" | custom-call | flops 33554432 | bytes 2097152 | tf_op jit(solution)/shard_map/pallas_call | solution.py:102
  1.9 4.0 %collective-permute-start.2 = (f32[2,64,128]{2,1,0:T(8,128)S(1)}, f32[2,64,128]{2,1,0:T(8,128)S(1)}, u32[]{:S(2)}, u32[]{:S(2)}) collective-permute-start(f32[2,64,128]{2,1,0:T(8,128)S(1)} %get-tuple-element.12.refs_0_), channel_id=1, source_target_pairs={{0,6},{1,7},{2,4},{3,5},{4,2},{5,3},{6,0},{7,1},{8,14},{9,15},{10,... | collective-permute-start | bytes 196616 | tf_op jit(solution)/shard_map/ppermute | solution.py:35
  6.0 0.4 %collective-permute-start.1 = (f32[2,64,128]{2,1,0:T(8,128)S(1)}, f32[2,64,128]{2,1,0:T(8,128)S(1)}, u32[]{:S(2)}, u32[]{:S(2)}) collective-permute-start(f32[2,64,128]{2,1,0:T(8,128)S(1)} %get-tuple-element.12.refs_0_), channel_id=1, source_target_pairs={{0,4},{1,5},{2,6},{3,7},{4,0},{5,1},{6,2},{7,3},{8,12},{9,13},{10,... | collective-permute-start | bytes 196616 | tf_op jit(solution)/shard_map/ppermute | solution.py:35
  6.4 0.2 %collective-permute-start = (f32[2,64,128]{2,1,0:T(8,128)S(1)}, f32[2,64,128]{2,1,0:T(8,128)S(1)}, u32[]{:S(2)}, u32[]{:S(2)}) collective-permute-start(f32[2,64,128]{2,1,0:T(8,128)S(1)} %get-tuple-element.12.refs_0_), channel_id=1, source_target_pairs={{0,2},{1,3},{2,0},{3,1},{4,6},{5,7},{6,4},{7,5},{8,10},{9,11},{10,... | collective-permute-start | bytes 196616 | tf_op jit(solution)/shard_map/ppermute | solution.py:35
  6.6 2.9 %collective-permute-start.7 = (s32[1,8,128]{2,1,0:T(8,128)S(1)}, s32[1,8,128]{2,1,0:T(8,128)S(1)}, u32[]{:S(2)}, u32[]{:S(2)}) collective-permute-start(s32[1,8,128]{2,1,0:T(8,128)S(1)} %bitcast.6), channel_id=1, source_target_pairs={{0,8},{1,9},{2,10},{3,11},{4,12},{5,13},{6,14},{7,15},{8,0},{9,1},... | collective-permute-start | bytes 12296 | tf_op jit(solution)/shard_map/ppermute | solution.py:35
  9.5 0.0 collective-permute-start.3
  9.5 0.0 collective-permute-done.2.refs_3_
  9.5 0.5 %collective-permute-start.6 = (f32[2,64,128]{2,1,0:T(8,128)S(1)}, f32[2,64,128]{2,1,0:T(8,128)S(1)}, u32[]{:S(2)}, u32[]{:S(2)}) collective-permute-start(f32[2,64,128]{2,1,0:T(8,128)S(1)} %collective-permute-done.2.refs_3_), channel_id=1, source_target_pairs={{0,1},{1,0},{2,3},{3,2},{4,5},{5,4},{6,7},{7,6},{8,9},{9,8},{10,11... | collective-permute-start | bytes 196616 | tf_op jit(solution)/shard_map/ppermute | solution.py:35
  10.0 0.2 %collective-permute-done.1.refs_2_ = f32[2,64,128]{2,1,0:T(8,128)S(1)} collective-permute-done((f32[2,64,128]{2,1,0:T(8,128)S(1)}, f32[2,64,128]{2,1,0:T(8,128)S(1)}, u32[]{:S(2)}, u32[]{:S(2)}) %collective-permute-start.1) | collective-permute-done | bytes 65568 | tf_op jit(solution)/shard_map/ppermute | solution.py:35
  10.2 0.0 collective-permute-start.5
  10.2 0.4 %collective-permute-done.refs_1_ = f32[2,64,128]{2,1,0:T(8,128)S(1)} collective-permute-done((f32[2,64,128]{2,1,0:T(8,128)S(1)}, f32[2,64,128]{2,1,0:T(8,128)S(1)}, u32[]{:S(2)}, u32[]{:S(2)}) %collective-permute-start) | collective-permute-done | bytes 65568 | tf_op jit(solution)/shard_map/ppermute | solution.py:35
  10.7 0.1 collective-permute-start.4
  10.7 0.4 %collective-permute-done.7.x = s32[1,8,128]{2,1,0:T(8,128)S(1)} collective-permute-done((s32[1,8,128]{2,1,0:T(8,128)S(1)}, s32[1,8,128]{2,1,0:T(8,128)S(1)}, u32[]{:S(2)}, u32[]{:S(2)}) %collective-permute-start.7) | collective-permute-done | bytes 4128 | tf_op jit(solution)/shard_map/ppermute | solution.py:35
  11.1 0.2 shard_map.48.refs_9_
  11.3 0.0 collective-permute-done.3.refs_4_
  11.3 0.0 collective-permute-done.6.refs_6_.refs_7_
  11.3 0.2 collective-permute-done.5.refs_5_.refs_6_
  11.5 0.2 %shard_map.47.refs_8_ = f32[2,64,128]{2,1,0:T(8,128)S(1)} custom-call(f32[2,64,128]{2,1,0:T(8,128)S(1)} %get-tuple-element.12.refs_0_, f32[2,64,128]{2,1,0:T(8,128)S(1)} %collective-permute-done.refs_1_, f32[2,64,128]{2,1,0:T(8,128)S(1)} %collective-permute-done.1.refs_2_, f32[2,64,128]{2,1,0:T(8,128)S(1)} %collective-permute-done.2.refs_3_, ...), custom_call_target="tpu_custom_call" | custom-call | bytes 1048576 | tf_op jit(solution)/shard_map/pallas_call | solution.py:199
  11.7 0.2 %collective-permute-done.4.refs_5_ = f32[2,64,128]{2,1,0:T(8,128)S(1)} collective-permute-done((f32[2,64,128]{2,1,0:T(8,128)S(1)}, f32[2,64,128]{2,1,0:T(8,128)S(1)}, u32[]{:S(2)}, u32[]{:S(2)}) %collective-permute-start.4) | collective-permute-done | bytes 65568 | tf_op jit(solution)/shard_map/ppermute | solution.py:35
  11.9 0.3 %shard_map.49 = (f32[1,4,8,128]{3,2,1,0:T(8,128)S(1)}, f32[2,64,128]{2,1,0:T(8,128)S(1)}) custom-call(f32[2,64,128]{2,1,0:T(8,128)S(1)} %get-tuple-element.12.refs_0_, f32[2,64,128]{2,1,0:T(8,128)S(1)} %collective-permute-done.refs_1_, f32[2,64,128]{2,1,0:T(8,128)S(1)} %collective-permute-done.1.refs_2_, f32[2,64,128]{2,1,0:T(8,128)S(1)} %collective-permute-done.2.refs_3_, ...), custom_call_target="tpu_custom_call" | custom-call | bytes 1048576 | tf_op jit(solution)/shard_map/pallas_call | solution.py:225
  12.2 2.7 %collective-permute-start.8 = (f32[1,4,8,128]{3,2,1,0:T(8,128)S(1)}, f32[1,4,8,128]{3,2,1,0:T(8,128)S(1)}, u32[]{:S(2)}, u32[]{:S(2)}) collective-permute-start(f32[1,4,8,128]{3,2,1,0:T(8,128)S(1)} %get-tuple-element.15), channel_id=1, source_target_pairs={{0,8},{1,9},{2,10},{3,11},{4,12},{5,13},{6,14},{7,15},{8,0},{9,1},... | collective-permute-start | bytes 49160 | tf_op jit(solution)/shard_map/ppermute | solution.py:35
  14.9 0.2 shard_map.50.refs_9_
  15.1 0.8 %shard_map.52 = (bf16[256,1024]{1,0:T(8,128)(2,1)S(1)}, f32[8,128]{1,0:T(8,128)S(1)}, f32[8,128]{1,0:T(8,128)S(1)}) custom-call(s32[8]{0:T(128)} %widths.1, s32[16]{0:T(128)} %spans.1), custom_call_target="tpu_custom_call" | custom-call | bytes 1048576 | tf_op jit(solution)/shard_map/pallas_call | solution.py:151
  15.9 0.2 shard_map.51.a
  16.1 0.8 %collective-permute-done.8 = f32[1,4,8,128]{3,2,1,0:T(8,128)S(1)} collective-permute-done((f32[1,4,8,128]{3,2,1,0:T(8,128)S(1)}, f32[1,4,8,128]{3,2,1,0:T(8,128)S(1)}, u32[]{:S(2)}, u32[]{:S(2)}) %collective-permute-start.8) | collective-permute-done | bytes 16416 | tf_op jit(solution)/shard_map/ppermute | solution.py:35
  16.9 0.9 %shard_map.53 = f32[4,8,8,128]{3,2,1,0:T(8,128)} custom-call(f32[4,8,128]{2,1,0:T(8,128)S(1)} %shard_map.51.a, f32[4,8,128]{2,1,0:T(8,128)S(1)} %bitcast.5, bf16[256,1024]{1,0:T(8,128)(2,1)S(1)} %get-tuple-element.16.bands, f32[8,128]{1,0:T(8,128)S(1)} %get-tuple-element.17.scale, f32[8,128]{1,0:T(8,128)S(1)} %get-tuple-element.18.mask), custom_call_target="tpu_custom_call" | custom-call | bytes 1048576 | tf_op jit(solution)/shard_map/pallas_call | solution.py:276
Async XLA Ops:
  1.9 7.6 %collective-permute-start.2 = (f32[2,64,128]{2,1,0:T(8,128)S(1)}, f32[2,64,128]{2,1,0:T(8,128)S(1)}, u32[]{:S(2)}, u32[]{:S(2)}) collective-permute-start(f32[2,64,128]{2,1,0:T(8,128)S(1)} %get-tuple-element.12.refs_0_), channel_id=1, source_target_pairs={{0,6},{1,7},{2,4},{3,5},{4,2},{5,3},{6,0},{7,1},{8,14},{9,15},{10,... | collective-permute-start | bytes 196616 | tf_op jit(solution)/shard_map/ppermute | solution.py:35
  6.0 4.3 %collective-permute-start.1 = (f32[2,64,128]{2,1,0:T(8,128)S(1)}, f32[2,64,128]{2,1,0:T(8,128)S(1)}, u32[]{:S(2)}, u32[]{:S(2)}) collective-permute-start(f32[2,64,128]{2,1,0:T(8,128)S(1)} %get-tuple-element.12.refs_0_), channel_id=1, source_target_pairs={{0,4},{1,5},{2,6},{3,7},{4,0},{5,1},{6,2},{7,3},{8,12},{9,13},{10,... | collective-permute-start | bytes 196616 | tf_op jit(solution)/shard_map/ppermute | solution.py:35
  6.4 4.3 %collective-permute-start = (f32[2,64,128]{2,1,0:T(8,128)S(1)}, f32[2,64,128]{2,1,0:T(8,128)S(1)}, u32[]{:S(2)}, u32[]{:S(2)}) collective-permute-start(f32[2,64,128]{2,1,0:T(8,128)S(1)} %get-tuple-element.12.refs_0_), channel_id=1, source_target_pairs={{0,2},{1,3},{2,0},{3,1},{4,6},{5,7},{6,4},{7,5},{8,10},{9,11},{10,... | collective-permute-start | bytes 196616 | tf_op jit(solution)/shard_map/ppermute | solution.py:35
  6.6 4.5 %collective-permute-start.7 = (s32[1,8,128]{2,1,0:T(8,128)S(1)}, s32[1,8,128]{2,1,0:T(8,128)S(1)}, u32[]{:S(2)}, u32[]{:S(2)}) collective-permute-start(s32[1,8,128]{2,1,0:T(8,128)S(1)} %bitcast.6), channel_id=1, source_target_pairs={{0,8},{1,9},{2,10},{3,11},{4,12},{5,13},{6,14},{7,15},{8,0},{9,1},... | collective-permute-start | bytes 12296 | tf_op jit(solution)/shard_map/ppermute | solution.py:35
  9.5 1.8 %collective-permute-start.3 = (f32[2,64,128]{2,1,0:T(8,128)S(1)}, f32[2,64,128]{2,1,0:T(8,128)S(1)}, u32[]{:S(2)}, u32[]{:S(2)}) collective-permute-start(f32[2,64,128]{2,1,0:T(8,128)S(1)} %get-tuple-element.12.refs_0_), channel_id=1, source_target_pairs={{0,1},{1,0},{2,3},{3,2},{4,5},{5,4},{6,7},{7,6},{8,9},{9,8},{10,11... | collective-permute-start | bytes 196616 | tf_op jit(solution)/shard_map/ppermute | solution.py:35
  9.5 1.8 %collective-permute-start.6 = (f32[2,64,128]{2,1,0:T(8,128)S(1)}, f32[2,64,128]{2,1,0:T(8,128)S(1)}, u32[]{:S(2)}, u32[]{:S(2)}) collective-permute-start(f32[2,64,128]{2,1,0:T(8,128)S(1)} %collective-permute-done.2.refs_3_), channel_id=1, source_target_pairs={{0,1},{1,0},{2,3},{3,2},{4,5},{5,4},{6,7},{7,6},{8,9},{9,8},{10,11... | collective-permute-start | bytes 196616 | tf_op jit(solution)/shard_map/ppermute | solution.py:35
  10.2 1.3 %collective-permute-start.5 = (f32[2,64,128]{2,1,0:T(8,128)S(1)}, f32[2,64,128]{2,1,0:T(8,128)S(1)}, u32[]{:S(2)}, u32[]{:S(2)}) collective-permute-start(f32[2,64,128]{2,1,0:T(8,128)S(1)} %collective-permute-done.1.refs_2_), channel_id=1, source_target_pairs={{0,1},{1,0},{2,3},{3,2},{4,5},{5,4},{6,7},{7,6},{8,9},{9,8},{10,11... | collective-permute-start | bytes 196616 | tf_op jit(solution)/shard_map/ppermute | solution.py:35
  10.7 1.3 %collective-permute-start.4 = (f32[2,64,128]{2,1,0:T(8,128)S(1)}, f32[2,64,128]{2,1,0:T(8,128)S(1)}, u32[]{:S(2)}, u32[]{:S(2)}) collective-permute-start(f32[2,64,128]{2,1,0:T(8,128)S(1)} %collective-permute-done.refs_1_), channel_id=1, source_target_pairs={{0,1},{1,0},{2,3},{3,2},{4,5},{5,4},{6,7},{7,6},{8,9},{9,8},{10,11... | collective-permute-start | bytes 196616 | tf_op jit(solution)/shard_map/ppermute | solution.py:35
  12.2 4.7 %collective-permute-start.8 = (f32[1,4,8,128]{3,2,1,0:T(8,128)S(1)}, f32[1,4,8,128]{3,2,1,0:T(8,128)S(1)}, u32[]{:S(2)}, u32[]{:S(2)}) collective-permute-start(f32[1,4,8,128]{3,2,1,0:T(8,128)S(1)} %get-tuple-element.15), channel_id=1, source_target_pairs={{0,8},{1,9},{2,10},{3,11},{4,12},{5,13},{6,14},{7,15},{8,0},{9,1},... | collective-permute-start | bytes 49160 | tf_op jit(solution)/shard_map/ppermute | solution.py:35

commit v8 on v6

--- a/solution.py
+++ b/solution.py
@@ -270,7 +270,7 @@
     far_bits = [b for b in (8, 16, 32, 64, 128, 256) if b < group]
 
     raw, rows = raw_series(spectra, delays)
-    masks = (0, 2, 4, 6)
+    masks = (0, 2, 4, 7)
     raws = [raw] + [swap(raw, m, group) for m in masks[1:]]
     raws = raws + [swap(r, 1, group) for r in raws]
     masks = masks + tuple(m ^ 1 for m in masks)

time: 18 us -> 17.7 us (0.983)
  waiting for transfers between devices: 2.52 us -> 2.14 us
    ppermute x9, waiting for transfers between devices: 2.52 us -> 2.14 us  [swap(): return lax.ppermute(x, 'trials', [(i, i ^ bit) for i in range(group)])]
  transfers between devices with their start and end apart: 9 -> 9, of which waited for: 6 -> 5; matrix products, arithmetic and copies ran while one was open for 0% -> 0% of each run, Pallas kernels for 7% -> 8%
where the time goes in v8:
time: 17.7 us; the launch traced here: 17.6 us
  starting transfers between devices  10.9 us (62%)
  Pallas kernels  4.48 us (25%)
  waiting for transfers between devices  2.14 us (12%)
    ppermute x9, starting transfers between devices, swap(): return lax.ppermute(x, 'trials', [(i, i ^ bit) for i in range(group)])  10.9 us
    ppermute x9, waiting for transfers between devices, swap(): return lax.ppermute(x, 'trials', [(i, i ^ bit) for i in range(group)])  2.14 us
    pallas_call x1, Pallas kernels, raw_series(): pl.pallas_call(functools.partial(raw_kernel, chunks), out_shape=(VMEM((SU...  1.91 us
    pallas_call x1, Pallas kernels, boxcars(): pl.pallas_call(boxcar_kernel, out_shape=jax.ShapeDtypeStruct(shape, jnp.f...  0.94 us
    pallas_call x1, Pallas kernels, tables(): pl.pallas_call(functools.partial(tables_kernel, channels), out_shape=(VME...  0.84 us
    pallas_call x2, Pallas kernels, to_scalars(): pl.pallas_call(functools.partial(scalars_kernel, trials, group), out_shap...  0.36 us
  transfers between devices with their start and end apart: 9, of which 5 were waited for; matrix products, arithmetic and copies ran while one was open for 0% of the time, Pallas kernels for 8%

profile of v8, /device:TPU:0, one launch (start us, length us, event | category | flops | bytes accessed | tf_op | source)
XLA Modules:
  0.0 17.6 jit_solution(3615899534691783682)
XLA Ops:
  0.0 1.9 %shard_map.46 = (f32[2,64,128]{2,1,0:T(8,128)S(1)}, s32[8,128]{1,0:T(8,128)S(1)}) custom-call(bf16[128,8192]{1,0:T(8,128)(2,1)} %x_hbm.1, s32[4,16]{1,0:T(4,128)} %delays_hbm.1), custom_call_target="tpu_custom_call" | custom-call | flops 33554432 | bytes 2097152 | tf_op jit(solution)/shard_map/pallas_call | solution.py:100
  1.9 3.5 %collective-permute-start.2 = (f32[2,64,128]{2,1,0:T(8,128)S(1)}, f32[2,64,128]{2,1,0:T(8,128)S(1)}, u32[]{:S(2)}, u32[]{:S(2)}) collective-permute-start(f32[2,64,128]{2,1,0:T(8,128)S(1)} %get-tuple-element.12.refs_0_), channel_id=1, source_target_pairs={{0,7},{1,6},{2,5},{3,4},{4,3},{5,2},{6,1},{7,0},{8,15},{9,14},{10,... | collective-permute-start | bytes 196616 | tf_op jit(solution)/shard_map/ppermute | solution.py:35
  5.4 0.4 %collective-permute-start.1 = (f32[2,64,128]{2,1,0:T(8,128)S(1)}, f32[2,64,128]{2,1,0:T(8,128)S(1)}, u32[]{:S(2)}, u32[]{:S(2)}) collective-permute-start(f32[2,64,128]{2,1,0:T(8,128)S(1)} %get-tuple-element.12.refs_0_), channel_id=1, source_target_pairs={{0,4},{1,5},{2,6},{3,7},{4,0},{5,1},{6,2},{7,3},{8,12},{9,13},{10,... | collective-permute-start | bytes 196616 | tf_op jit(solution)/shard_map/ppermute | solution.py:35
  5.8 0.8 %collective-permute-start = (f32[2,64,128]{2,1,0:T(8,128)S(1)}, f32[2,64,128]{2,1,0:T(8,128)S(1)}, u32[]{:S(2)}, u32[]{:S(2)}) collective-permute-start(f32[2,64,128]{2,1,0:T(8,128)S(1)} %get-tuple-element.12.refs_0_), channel_id=1, source_target_pairs={{0,2},{1,3},{2,0},{3,1},{4,6},{5,7},{6,4},{7,5},{8,10},{9,11},{10,... | collective-permute-start | bytes 196616 | tf_op jit(solution)/shard_map/ppermute | solution.py:35
  6.6 2.6 %collective-permute-start.7 = (s32[1,8,128]{2,1,0:T(8,128)S(1)}, s32[1,8,128]{2,1,0:T(8,128)S(1)}, u32[]{:S(2)}, u32[]{:S(2)}) collective-permute-start(s32[1,8,128]{2,1,0:T(8,128)S(1)} %bitcast.6), channel_id=1, source_target_pairs={{0,8},{1,9},{2,10},{3,11},{4,12},{5,13},{6,14},{7,15},{8,0},{9,1},... | collective-permute-start | bytes 12296 | tf_op jit(solution)/shard_map/ppermute | solution.py:35
  9.2 0.0 collective-permute-start.3
  9.2 0.0 collective-permute-done.2.refs_3_
  9.2 0.5 %collective-permute-start.6 = (f32[2,64,128]{2,1,0:T(8,128)S(1)}, f32[2,64,128]{2,1,0:T(8,128)S(1)}, u32[]{:S(2)}, u32[]{:S(2)}) collective-permute-start(f32[2,64,128]{2,1,0:T(8,128)S(1)} %collective-permute-done.2.refs_3_), channel_id=1, source_target_pairs={{0,1},{1,0},{2,3},{3,2},{4,5},{5,4},{6,7},{7,6},{8,9},{9,8},{10,11... | collective-permute-start | bytes 196616 | tf_op jit(solution)/shard_map/ppermute | solution.py:35
  9.7 0.5 %collective-permute-done.1.refs_2_ = f32[2,64,128]{2,1,0:T(8,128)S(1)} collective-permute-done((f32[2,64,128]{2,1,0:T(8,128)S(1)}, f32[2,64,128]{2,1,0:T(8,128)S(1)}, u32[]{:S(2)}, u32[]{:S(2)}) %collective-permute-start.1) | collective-permute-done | bytes 65568 | tf_op jit(solution)/shard_map/ppermute | solution.py:35
  10.2 0.0 collective-permute-start.5
  10.2 0.0 collective-permute-done.refs_1_
  10.3 0.5 %collective-permute-start.4 = (f32[2,64,128]{2,1,0:T(8,128)S(1)}, f32[2,64,128]{2,1,0:T(8,128)S(1)}, u32[]{:S(2)}, u32[]{:S(2)}) collective-permute-start(f32[2,64,128]{2,1,0:T(8,128)S(1)} %collective-permute-done.refs_1_), channel_id=1, source_target_pairs={{0,1},{1,0},{2,3},{3,2},{4,5},{5,4},{6,7},{7,6},{8,9},{9,8},{10,11... | collective-permute-start | bytes 196616 | tf_op jit(solution)/shard_map/ppermute | solution.py:35
  10.7 0.4 %collective-permute-done.7.x = s32[1,8,128]{2,1,0:T(8,128)S(1)} collective-permute-done((s32[1,8,128]{2,1,0:T(8,128)S(1)}, s32[1,8,128]{2,1,0:T(8,128)S(1)}, u32[]{:S(2)}, u32[]{:S(2)}) %collective-permute-start.7) | collective-permute-done | bytes 4128 | tf_op jit(solution)/shard_map/ppermute | solution.py:35
  11.1 0.2 %shard_map.47.refs_8_ = s32[1,8,128]{2,1,0:T(8,128)S(4)} custom-call(s32[1,8,128]{2,1,0:T(8,128)S(1)} %collective-permute-done.7.x), custom_call_target="tpu_custom_call" | custom-call | flops 17179869184 | bytes 16777216 | tf_op jit(solution)/shard_map/pallas_call | solution.py:126
  11.3 0.0 collective-permute-done.3.refs_4_
  11.3 0.0 collective-permute-done.6.refs_7_
  11.3 0.2 collective-permute-done.5.refs_6_
  11.5 0.2 collective-permute-done.4.refs_5_
  11.6 0.3 %shard_map.48 = (f32[1,4,8,128]{3,2,1,0:T(8,128)S(1)}, f32[2,64,128]{2,1,0:T(8,128)S(1)}) custom-call(f32[2,64,128]{2,1,0:T(8,128)S(1)} %get-tuple-element.12.refs_0_, f32[2,64,128]{2,1,0:T(8,128)S(1)} %collective-permute-done.refs_1_, f32[2,64,128]{2,1,0:T(8,128)S(1)} %collective-permute-done.1.refs_2_, f32[2,64,128]{2,1,0:T(8,128)S(1)} %collective-permute-done.2.refs_3_, ...), custom_call_target="tpu_custom_call" | custom-call | bytes 1048576 | tf_op jit(solution)/shard_map/pallas_call | solution.py:204
  11.9 2.7 %collective-permute-start.8 = (f32[1,4,8,128]{3,2,1,0:T(8,128)S(1)}, f32[1,4,8,128]{3,2,1,0:T(8,128)S(1)}, u32[]{:S(2)}, u32[]{:S(2)}) collective-permute-start(f32[1,4,8,128]{3,2,1,0:T(8,128)S(1)} %get-tuple-element.15), channel_id=1, source_target_pairs={{0,8},{1,9},{2,10},{3,11},{4,12},{5,13},{6,14},{7,15},{8,0},{9,1},... | collective-permute-start | bytes 49160 | tf_op jit(solution)/shard_map/ppermute | solution.py:35
  14.6 0.2 %shard_map.49.refs_9_ = s32[1,8,128]{2,1,0:T(8,128)S(4)} custom-call(s32[1,8,128]{2,1,0:T(8,128)S(1)} %bitcast.7), custom_call_target="tpu_custom_call" | custom-call | bytes 1048576 | tf_op jit(solution)/shard_map/pallas_call | solution.py:126
  14.8 0.8 %shard_map.51 = (bf16[256,1024]{1,0:T(8,128)(2,1)S(1)}, f32[8,128]{1,0:T(8,128)S(1)}, f32[8,128]{1,0:T(8,128)S(1)}) custom-call(s32[8]{0:T(128)} %widths.1, s32[16]{0:T(128)} %spans.1), custom_call_target="tpu_custom_call" | custom-call | bytes 1048576 | tf_op jit(solution)/shard_map/pallas_call | solution.py:149
  15.6 0.1 shard_map.50.a
  15.8 0.9 %collective-permute-done.8 = f32[1,4,8,128]{3,2,1,0:T(8,128)S(1)} collective-permute-done((f32[1,4,8,128]{3,2,1,0:T(8,128)S(1)}, f32[1,4,8,128]{3,2,1,0:T(8,128)S(1)}, u32[]{:S(2)}, u32[]{:S(2)}) %collective-permute-start.8) | collective-permute-done | bytes 16416 | tf_op jit(solution)/shard_map/ppermute | solution.py:35
  16.7 0.9 %shard_map.52 = f32[4,8,8,128]{3,2,1,0:T(8,128)} custom-call(f32[4,8,128]{2,1,0:T(8,128)S(1)} %shard_map.50.a, f32[4,8,128]{2,1,0:T(8,128)S(1)} %bitcast.5, bf16[256,1024]{1,0:T(8,128)(2,1)S(1)} %get-tuple-element.16.bands, f32[8,128]{1,0:T(8,128)S(1)} %get-tuple-element.17.scale, f32[8,128]{1,0:T(8,128)S(1)} %get-tuple-element.18.mask), custom_call_target="tpu_custom_call" | custom-call | bytes 1048576 | tf_op jit(solution)/shard_map/pallas_call | solution.py:255
Async XLA Ops:
  1.9 7.3 %collective-permute-start.2 = (f32[2,64,128]{2,1,0:T(8,128)S(1)}, f32[2,64,128]{2,1,0:T(8,128)S(1)}, u32[]{:S(2)}, u32[]{:S(2)}) collective-permute-start(f32[2,64,128]{2,1,0:T(8,128)S(1)} %get-tuple-element.12.refs_0_), channel_id=1, source_target_pairs={{0,7},{1,6},{2,5},{3,4},{4,3},{5,2},{6,1},{7,0},{8,15},{9,14},{10,... | collective-permute-start | bytes 196616 | tf_op jit(solution)/shard_map/ppermute | solution.py:35
  5.4 4.8 %collective-permute-start.1 = (f32[2,64,128]{2,1,0:T(8,128)S(1)}, f32[2,64,128]{2,1,0:T(8,128)S(1)}, u32[]{:S(2)}, u32[]{:S(2)}) collective-permute-start(f32[2,64,128]{2,1,0:T(8,128)S(1)} %get-tuple-element.12.refs_0_), channel_id=1, source_target_pairs={{0,4},{1,5},{2,6},{3,7},{4,0},{5,1},{6,2},{7,3},{8,12},{9,13},{10,... | collective-permute-start | bytes 196616 | tf_op jit(solution)/shard_map/ppermute | solution.py:35
  5.8 4.4 %collective-permute-start = (f32[2,64,128]{2,1,0:T(8,128)S(1)}, f32[2,64,128]{2,1,0:T(8,128)S(1)}, u32[]{:S(2)}, u32[]{:S(2)}) collective-permute-start(f32[2,64,128]{2,1,0:T(8,128)S(1)} %get-tuple-element.12.refs_0_), channel_id=1, source_target_pairs={{0,2},{1,3},{2,0},{3,1},{4,6},{5,7},{6,4},{7,5},{8,10},{9,11},{10,... | collective-permute-start | bytes 196616 | tf_op jit(solution)/shard_map/ppermute | solution.py:35
  6.6 4.5 %collective-permute-start.7 = (s32[1,8,128]{2,1,0:T(8,128)S(1)}, s32[1,8,128]{2,1,0:T(8,128)S(1)}, u32[]{:S(2)}, u32[]{:S(2)}) collective-permute-start(s32[1,8,128]{2,1,0:T(8,128)S(1)} %bitcast.6), channel_id=1, source_target_pairs={{0,8},{1,9},{2,10},{3,11},{4,12},{5,13},{6,14},{7,15},{8,0},{9,1},... | collective-permute-start | bytes 12296 | tf_op jit(solution)/shard_map/ppermute | solution.py:35
  9.2 2.1 %collective-permute-start.3 = (f32[2,64,128]{2,1,0:T(8,128)S(1)}, f32[2,64,128]{2,1,0:T(8,128)S(1)}, u32[]{:S(2)}, u32[]{:S(2)}) collective-permute-start(f32[2,64,128]{2,1,0:T(8,128)S(1)} %get-tuple-element.12.refs_0_), channel_id=1, source_target_pairs={{0,1},{1,0},{2,3},{3,2},{4,5},{5,4},{6,7},{7,6},{8,9},{9,8},{10,11... | collective-permute-start | bytes 196616 | tf_op jit(solution)/shard_map/ppermute | solution.py:35
  9.2 2.1 %collective-permute-start.6 = (f32[2,64,128]{2,1,0:T(8,128)S(1)}, f32[2,64,128]{2,1,0:T(8,128)S(1)}, u32[]{:S(2)}, u32[]{:S(2)}) collective-permute-start(f32[2,64,128]{2,1,0:T(8,128)S(1)} %collective-permute-done.2.refs_3_), channel_id=1, source_target_pairs={{0,1},{1,0},{2,3},{3,2},{4,5},{5,4},{6,7},{7,6},{8,9},{9,8},{10,11... | collective-permute-start | bytes 196616 | tf_op jit(solution)/shard_map/ppermute | solution.py:35
  10.2 1.3 %collective-permute-start.5 = (f32[2,64,128]{2,1,0:T(8,128)S(1)}, f32[2,64,128]{2,1,0:T(8,128)S(1)}, u32[]{:S(2)}, u32[]{:S(2)}) collective-permute-start(f32[2,64,128]{2,1,0:T(8,128)S(1)} %collective-permute-done.1.refs_2_), channel_id=1, source_target_pairs={{0,1},{1,0},{2,3},{3,2},{4,5},{5,4},{6,7},{7,6},{8,9},{9,8},{10,11... | collective-permute-start | bytes 196616 | tf_op jit(solution)/shard_map/ppermute | solution.py:35
  10.3 1.4 %collective-permute-start.4 = (f32[2,64,128]{2,1,0:T(8,128)S(1)}, f32[2,64,128]{2,1,0:T(8,128)S(1)}, u32[]{:S(2)}, u32[]{:S(2)}) collective-permute-start(f32[2,64,128]{2,1,0:T(8,128)S(1)} %collective-permute-done.refs_1_), channel_id=1, source_target_pairs={{0,1},{1,0},{2,3},{3,2},{4,5},{5,4},{6,7},{7,6},{8,9},{9,8},{10,11... | collective-permute-start | bytes 196616 | tf_op jit(solution)/shard_map/ppermute | solution.py:35
  11.9 4.7 %collective-permute-start.8 = (f32[1,4,8,128]{3,2,1,0:T(8,128)S(1)}, f32[1,4,8,128]{3,2,1,0:T(8,128)S(1)}, u32[]{:S(2)}, u32[]{:S(2)}) collective-permute-start(f32[1,4,8,128]{3,2,1,0:T(8,128)S(1)} %get-tuple-element.15), channel_id=1, source_target_pairs={{0,8},{1,9},{2,10},{3,11},{4,12},{5,13},{6,14},{7,15},{8,0},{9,1},... | collective-permute-start | bytes 49160 | tf_op jit(solution)/shard_map/ppermute | solution.py:35

commit v9 on v8

--- a/solution.py
+++ b/solution.py
@@ -267,7 +267,7 @@
     group = lax.axis_size("trials")
     channels = CH_SUB * group
     trials = delays.shape[0]
-    far_bits = [b for b in (8, 16, 32, 64, 128, 256) if b < group]
+    far_bits = [b for b in (9, 16, 32, 64, 128, 256) if b < group]
 
     raw, rows = raw_series(spectra, delays)
     masks = (0, 2, 4, 7)

time: 17.7 us -> 17.1 us (0.966)
  starting transfers between devices: 10.9 us -> 10.5 us
  waiting for transfers between devices: 2.14 us -> 1.96 us
    ppermute x9, starting transfers between devices: 10.9 us -> 10.5 us  [swap(): return lax.ppermute(x, 'trials', [(i, i ^ bit) for i in range(group)])]
    ppermute x9, waiting for transfers between devices: 2.14 us -> 1.96 us  [swap(): return lax.ppermute(x, 'trials', [(i, i ^ bit) for i in range(group)])]
where the time goes in v9:
time: 17.1 us; the launch traced here: 17 us
  starting transfers between devices  10.5 us (61%)
  Pallas kernels  4.48 us (26%)
  waiting for transfers between devices  1.96 us (11%)
    ppermute x9, starting transfers between devices, swap(): return lax.ppermute(x, 'trials', [(i, i ^ bit) for i in range(group)])  10.5 us
    ppermute x9, waiting for transfers between devices, swap(): return lax.ppermute(x, 'trials', [(i, i ^ bit) for i in range(group)])  1.96 us
    pallas_call x1, Pallas kernels, raw_series(): pl.pallas_call(functools.partial(raw_kernel, chunks), out_shape=(VMEM((SU...  1.91 us
    pallas_call x1, Pallas kernels, boxcars(): pl.pallas_call(boxcar_kernel, out_shape=jax.ShapeDtypeStruct(shape, jnp.f...  0.94 us
    pallas_call x1, Pallas kernels, tables(): pl.pallas_call(functools.partial(tables_kernel, channels), out_shape=(VME...  0.84 us
    pallas_call x2, Pallas kernels, to_scalars(): pl.pallas_call(functools.partial(scalars_kernel, trials, group), out_shap...  0.36 us
  transfers between devices with their start and end apart: 9, of which 5 were waited for; matrix products, arithmetic and copies ran while one was open for 0% of the time, Pallas kernels for 8%

profile of v9, /device:TPU:0, one launch (start us, length us, event | category | flops | bytes accessed | tf_op | source)
XLA Modules:
  0.0 17.0 jit_solution(1122914933686157187)
XLA Ops:
  0.0 1.9 %shard_map.46 = (f32[2,64,128]{2,1,0:T(8,128)S(1)}, s32[8,128]{1,0:T(8,128)S(1)}) custom-call(bf16[128,8192]{1,0:T(8,128)(2,1)} %x_hbm.1, s32[4,16]{1,0:T(4,128)} %delays_hbm.1), custom_call_target="tpu_custom_call" | custom-call | flops 33554432 | bytes 2097152 | tf_op jit(solution)/shard_map/pallas_call | solution.py:100
  1.9 3.5 %collective-permute-start.2 = (f32[2,64,128]{2,1,0:T(8,128)S(1)}, f32[2,64,128]{2,1,0:T(8,128)S(1)}, u32[]{:S(2)}, u32[]{:S(2)}) collective-permute-start(f32[2,64,128]{2,1,0:T(8,128)S(1)} %get-tuple-element.12.refs_0_), channel_id=1, source_target_pairs={{0,7},{1,6},{2,5},{3,4},{4,3},{5,2},{6,1},{7,0},{8,15},{9,14},{10,... | collective-permute-start | bytes 196616 | tf_op jit(solution)/shard_map/ppermute | solution.py:35
  5.4 0.4 %collective-permute-start.1 = (f32[2,64,128]{2,1,0:T(8,128)S(1)}, f32[2,64,128]{2,1,0:T(8,128)S(1)}, u32[]{:S(2)}, u32[]{:S(2)}) collective-permute-start(f32[2,64,128]{2,1,0:T(8,128)S(1)} %get-tuple-element.12.refs_0_), channel_id=1, source_target_pairs={{0,4},{1,5},{2,6},{3,7},{4,0},{5,1},{6,2},{7,3},{8,12},{9,13},{10,... | collective-permute-start | bytes 196616 | tf_op jit(solution)/shard_map/ppermute | solution.py:35
  5.8 0.8 %collective-permute-start = (f32[2,64,128]{2,1,0:T(8,128)S(1)}, f32[2,64,128]{2,1,0:T(8,128)S(1)}, u32[]{:S(2)}, u32[]{:S(2)}) collective-permute-start(f32[2,64,128]{2,1,0:T(8,128)S(1)} %get-tuple-element.12.refs_0_), channel_id=1, source_target_pairs={{0,2},{1,3},{2,0},{3,1},{4,6},{5,7},{6,4},{7,5},{8,10},{9,11},{10,... | collective-permute-start | bytes 196616 | tf_op jit(solution)/shard_map/ppermute | solution.py:35
  6.6 2.1 %collective-permute-start.7 = (s32[1,8,128]{2,1,0:T(8,128)S(1)}, s32[1,8,128]{2,1,0:T(8,128)S(1)}, u32[]{:S(2)}, u32[]{:S(2)}) collective-permute-start(s32[1,8,128]{2,1,0:T(8,128)S(1)} %bitcast.6), channel_id=1, source_target_pairs={{0,9},{1,8},{2,11},{3,10},{4,13},{5,12},{6,15},{7,14},{8,1},{9,0},... | collective-permute-start | bytes 12296 | tf_op jit(solution)/shard_map/ppermute | solution.py:35
  8.7 0.6 %collective-permute-start.3 = (f32[2,64,128]{2,1,0:T(8,128)S(1)}, f32[2,64,128]{2,1,0:T(8,128)S(1)}, u32[]{:S(2)}, u32[]{:S(2)}) collective-permute-start(f32[2,64,128]{2,1,0:T(8,128)S(1)} %get-tuple-element.12.refs_0_), channel_id=1, source_target_pairs={{0,1},{1,0},{2,3},{3,2},{4,5},{5,4},{6,7},{7,6},{8,9},{9,8},{10,11... | collective-permute-start | bytes 196616 | tf_op jit(solution)/shard_map/ppermute | solution.py:35
  9.3 0.0 collective-permute-done.2.refs_3_
  9.3 0.0 collective-permute-start.6
  9.3 0.9 %collective-permute-done.1.refs_2_ = f32[2,64,128]{2,1,0:T(8,128)S(1)} collective-permute-done((f32[2,64,128]{2,1,0:T(8,128)S(1)}, f32[2,64,128]{2,1,0:T(8,128)S(1)}, u32[]{:S(2)}, u32[]{:S(2)}) %collective-permute-start.1) | collective-permute-done | bytes 65568 | tf_op jit(solution)/shard_map/ppermute | solution.py:35
  10.2 0.0 collective-permute-start.5
  10.2 0.1 collective-permute-done.refs_1_
  10.3 0.4 %collective-permute-start.4 = (f32[2,64,128]{2,1,0:T(8,128)S(1)}, f32[2,64,128]{2,1,0:T(8,128)S(1)}, u32[]{:S(2)}, u32[]{:S(2)}) collective-permute-start(f32[2,64,128]{2,1,0:T(8,128)S(1)} %collective-permute-done.refs_1_), channel_id=1, source_target_pairs={{0,1},{1,0},{2,3},{3,2},{4,5},{5,4},{6,7},{7,6},{8,9},{9,8},{10,11... | collective-permute-start | bytes 196616 | tf_op jit(solution)/shard_map/ppermute | solution.py:35
  10.7 0.0 collective-permute-done.7.x
  10.7 0.2 %shard_map.47.refs_8_ = s32[1,8,128]{2,1,0:T(8,128)S(4)} custom-call(s32[1,8,128]{2,1,0:T(8,128)S(1)} %collective-permute-done.7.x), custom_call_target="tpu_custom_call" | custom-call | flops 17179869184 | bytes 16777216 | tf_op jit(solution)/shard_map/pallas_call | solution.py:126
  10.9 0.0 collective-permute-done.3.refs_4_
  10.9 0.0 collective-permute-done.6.refs_7_
  10.9 0.5 %collective-permute-done.5.refs_6_ = f32[2,64,128]{2,1,0:T(8,128)S(1)} collective-permute-done((f32[2,64,128]{2,1,0:T(8,128)S(1)}, f32[2,64,128]{2,1,0:T(8,128)S(1)}, u32[]{:S(2)}, u32[]{:S(2)}) %collective-permute-start.5) | collective-permute-done | bytes 65568 | tf_op jit(solution)/shard_map/ppermute | solution.py:35
  11.4 0.2 collective-permute-done.4.refs_5_
  11.6 0.3 %shard_map.48 = (f32[1,4,8,128]{3,2,1,0:T(8,128)S(1)}, f32[2,64,128]{2,1,0:T(8,128)S(1)}) custom-call(f32[2,64,128]{2,1,0:T(8,128)S(1)} %get-tuple-element.12.refs_0_, f32[2,64,128]{2,1,0:T(8,128)S(1)} %collective-permute-done.refs_1_, f32[2,64,128]{2,1,0:T(8,128)S(1)} %collective-permute-done.1.refs_2_, f32[2,64,128]{2,1,0:T(8,128)S(1)} %collective-permute-done.2.refs_3_, ...), custom_call_target="tpu_custom_call" | custom-call | bytes 1048576 | tf_op jit(solution)/shard_map/pallas_call | solution.py:204
  11.9 2.7 %collective-permute-start.8 = (f32[1,4,8,128]{3,2,1,0:T(8,128)S(1)}, f32[1,4,8,128]{3,2,1,0:T(8,128)S(1)}, u32[]{:S(2)}, u32[]{:S(2)}) collective-permute-start(f32[1,4,8,128]{3,2,1,0:T(8,128)S(1)} %get-tuple-element.15), channel_id=1, source_target_pairs={{0,9},{1,8},{2,11},{3,10},{4,13},{5,12},{6,15},{7,14},{8,1},{9,0},... | collective-permute-start | bytes 49160 | tf_op jit(solution)/shard_map/ppermute | solution.py:35
  14.6 0.2 %shard_map.49.refs_9_ = s32[1,8,128]{2,1,0:T(8,128)S(4)} custom-call(s32[1,8,128]{2,1,0:T(8,128)S(1)} %bitcast.7), custom_call_target="tpu_custom_call" | custom-call | bytes 1048576 | tf_op jit(solution)/shard_map/pallas_call | solution.py:126
  14.7 0.8 %shard_map.51 = (bf16[256,1024]{1,0:T(8,128)(2,1)S(1)}, f32[8,128]{1,0:T(8,128)S(1)}, f32[8,128]{1,0:T(8,128)S(1)}) custom-call(s32[8]{0:T(128)} %widths.1, s32[16]{0:T(128)} %spans.1), custom_call_target="tpu_custom_call" | custom-call | bytes 1048576 | tf_op jit(solution)/shard_map/pallas_call | solution.py:149
  15.6 0.1 shard_map.50.a
  15.7 0.3 %collective-permute-done.8 = f32[1,4,8,128]{3,2,1,0:T(8,128)S(1)} collective-permute-done((f32[1,4,8,128]{3,2,1,0:T(8,128)S(1)}, f32[1,4,8,128]{3,2,1,0:T(8,128)S(1)}, u32[]{:S(2)}, u32[]{:S(2)}) %collective-permute-start.8) | collective-permute-done | bytes 16416 | tf_op jit(solution)/shard_map/ppermute | solution.py:35
  16.0 0.9 %shard_map.52 = f32[4,8,8,128]{3,2,1,0:T(8,128)} custom-call(f32[4,8,128]{2,1,0:T(8,128)S(1)} %shard_map.50.a, f32[4,8,128]{2,1,0:T(8,128)S(1)} %bitcast.5, bf16[256,1024]{1,0:T(8,128)(2,1)S(1)} %get-tuple-element.16.bands, f32[8,128]{1,0:T(8,128)S(1)} %get-tuple-element.17.scale, f32[8,128]{1,0:T(8,128)S(1)} %get-tuple-element.18.mask), custom_call_target="tpu_custom_call" | custom-call | bytes 1048576 | tf_op jit(solution)/shard_map/pallas_call | solution.py:255
Async XLA Ops:
  1.9 7.4 %collective-permute-start.2 = (f32[2,64,128]{2,1,0:T(8,128)S(1)}, f32[2,64,128]{2,1,0:T(8,128)S(1)}, u32[]{:S(2)}, u32[]{:S(2)}) collective-permute-start(f32[2,64,128]{2,1,0:T(8,128)S(1)} %get-tuple-element.12.refs_0_), channel_id=1, source_target_pairs={{0,7},{1,6},{2,5},{3,4},{4,3},{5,2},{6,1},{7,0},{8,15},{9,14},{10,... | collective-permute-start | bytes 196616 | tf_op jit(solution)/shard_map/ppermute | solution.py:35
  5.4 4.8 %collective-permute-start.1 = (f32[2,64,128]{2,1,0:T(8,128)S(1)}, f32[2,64,128]{2,1,0:T(8,128)S(1)}, u32[]{:S(2)}, u32[]{:S(2)}) collective-permute-start(f32[2,64,128]{2,1,0:T(8,128)S(1)} %get-tuple-element.12.refs_0_), channel_id=1, source_target_pairs={{0,4},{1,5},{2,6},{3,7},{4,0},{5,1},{6,2},{7,3},{8,12},{9,13},{10,... | collective-permute-start | bytes 196616 | tf_op jit(solution)/shard_map/ppermute | solution.py:35
  5.8 4.4 %collective-permute-start = (f32[2,64,128]{2,1,0:T(8,128)S(1)}, f32[2,64,128]{2,1,0:T(8,128)S(1)}, u32[]{:S(2)}, u32[]{:S(2)}) collective-permute-start(f32[2,64,128]{2,1,0:T(8,128)S(1)} %get-tuple-element.12.refs_0_), channel_id=1, source_target_pairs={{0,2},{1,3},{2,0},{3,1},{4,6},{5,7},{6,4},{7,5},{8,10},{9,11},{10,... | collective-permute-start | bytes 196616 | tf_op jit(solution)/shard_map/ppermute | solution.py:35
  6.6 4.1 %collective-permute-start.7 = (s32[1,8,128]{2,1,0:T(8,128)S(1)}, s32[1,8,128]{2,1,0:T(8,128)S(1)}, u32[]{:S(2)}, u32[]{:S(2)}) collective-permute-start(s32[1,8,128]{2,1,0:T(8,128)S(1)} %bitcast.6), channel_id=1, source_target_pairs={{0,9},{1,8},{2,11},{3,10},{4,13},{5,12},{6,15},{7,14},{8,1},{9,0},... | collective-permute-start | bytes 12296 | tf_op jit(solution)/shard_map/ppermute | solution.py:35
  8.7 2.2 %collective-permute-start.3 = (f32[2,64,128]{2,1,0:T(8,128)S(1)}, f32[2,64,128]{2,1,0:T(8,128)S(1)}, u32[]{:S(2)}, u32[]{:S(2)}) collective-permute-start(f32[2,64,128]{2,1,0:T(8,128)S(1)} %get-tuple-element.12.refs_0_), channel_id=1, source_target_pairs={{0,1},{1,0},{2,3},{3,2},{4,5},{5,4},{6,7},{7,6},{8,9},{9,8},{10,11... | collective-permute-start | bytes 196616 | tf_op jit(solution)/shard_map/ppermute | solution.py:35
  9.3 1.6 %collective-permute-start.6 = (f32[2,64,128]{2,1,0:T(8,128)S(1)}, f32[2,64,128]{2,1,0:T(8,128)S(1)}, u32[]{:S(2)}, u32[]{:S(2)}) collective-permute-start(f32[2,64,128]{2,1,0:T(8,128)S(1)} %collective-permute-done.2.refs_3_), channel_id=1, source_target_pairs={{0,1},{1,0},{2,3},{3,2},{4,5},{5,4},{6,7},{7,6},{8,9},{9,8},{10,11... | collective-permute-start | bytes 196616 | tf_op jit(solution)/shard_map/ppermute | solution.py:35
  10.2 1.3 %collective-permute-start.5 = (f32[2,64,128]{2,1,0:T(8,128)S(1)}, f32[2,64,128]{2,1,0:T(8,128)S(1)}, u32[]{:S(2)}, u32[]{:S(2)}) collective-permute-start(f32[2,64,128]{2,1,0:T(8,128)S(1)} %collective-permute-done.1.refs_2_), channel_id=1, source_target_pairs={{0,1},{1,0},{2,3},{3,2},{4,5},{5,4},{6,7},{7,6},{8,9},{9,8},{10,11... | collective-permute-start | bytes 196616 | tf_op jit(solution)/shard_map/ppermute | solution.py:35
  10.3 1.3 %collective-permute-start.4 = (f32[2,64,128]{2,1,0:T(8,128)S(1)}, f32[2,64,128]{2,1,0:T(8,128)S(1)}, u32[]{:S(2)}, u32[]{:S(2)}) collective-permute-start(f32[2,64,128]{2,1,0:T(8,128)S(1)} %collective-permute-done.refs_1_), channel_id=1, source_target_pairs={{0,1},{1,0},{2,3},{3,2},{4,5},{5,4},{6,7},{7,6},{8,9},{9,8},{10,11... | collective-permute-start | bytes 196616 | tf_op jit(solution)/shard_map/ppermute | solution.py:35
  11.9 4.1 %collective-permute-start.8 = (f32[1,4,8,128]{3,2,1,0:T(8,128)S(1)}, f32[1,4,8,128]{3,2,1,0:T(8,128)S(1)}, u32[]{:S(2)}, u32[]{:S(2)}) collective-permute-start(f32[1,4,8,128]{3,2,1,0:T(8,128)S(1)} %get-tuple-element.15), channel_id=1, source_target_pairs={{0,9},{1,8},{2,11},{3,10},{4,13},{5,12},{6,15},{7,14},{8,1},{9,0},... | collective-permute-start | bytes 49160 | tf_op jit(solution)/shard_map/ppermute | solution.py:35
